TPU v7x, 32 devices: a whole 2x2x4 slice. The times are simulated.
32 devices in a mesh: seq: 8 (over y, x, core), tp: 4 (over z).
Axes of the slice: x: 2, y: 2, z: 4, core: 2. Of those that a mesh axis runs over, the one named last changes fastest.
Arguments:
- stream: bfloat16 [16384, 1024], P(('seq', 'tp')), may hold values from -6 to 6
- segments: int32 [16384], replicated, may hold values from 0 to 63, never falling along the last dimension, each value on 1 to 1024 neighbouring positions
- skip_values: bfloat16 [16384, 512], P('seq', 'tp'), may hold values from -6 to 6
- first_gain: float32 [1024], replicated, may hold values from 0.5 to 1.5
- first_shift: float32 [1024], replicated, may hold values from -1.75 to 1.75
- query_weight: bfloat16 [1024, 1024], P(None, 'tp'), may hold values from -0.1875 to 0.1875
- query_bias: float32 [1024], P('tp'), may hold values from -3 to 3
- key_weight: bfloat16 [1024, 1024], P(None, 'tp'), may hold values from -0.1875 to 0.1875
- value_weight: bfloat16 [1024, 512], P(None, 'tp'), may hold values from -0.1875 to 0.1875
- value_bias: float32 [512], P('tp'), may hold values from -3 to 3
- mixing_weight: bfloat16 [1024, 1024], P('tp'), may hold values from -1.5 to 1.5
- mixing_bias: float32 [1024], replicated, may hold values from -1.75 to 1.75
- second_gain: float32 [1024], replicated, may hold values from 0.5 to 1.5
- second_shift: float32 [1024], replicated, may hold values from -1.75 to 1.75
- up_weight: bfloat16 [1024, 4096], P(None, 'tp'), may hold values from -0.1875 to 0.1875
- up_bias: float32 [4096], P('tp'), may hold values from -3 to 3
- down_weight: bfloat16 [4096, 1024], P('tp'), may hold values from -0.09375 to 0.09375
- down_bias: float32 [1024], replicated, may hold values from -1.75 to 1.75
- cotangent: bfloat16 [16384, 1024], P(('seq', 'tp')), may hold values from -6 to 6
Outputs:
- output: bfloat16 [16384, 1024], P(('seq', 'tp'))
- stream_gradient: float32 [16384, 1024], P(('seq', 'tp'))
- skip_gradient: float32 [16384, 512], P('seq', 'tp')
- query_gradient: float32 [1024, 1024], P('seq', 'tp')
- query_bias_gradient: float32 [1024], replicated
- key_gradient: float32 [1024, 1024], P('seq', 'tp')
- value_gradient: float32 [1024, 512], P('seq', 'tp')
- value_bias_gradient: float32 [512], replicated
- mixing_gradient: float32 [1024, 1024], P('tp', 'seq')
- mixing_bias_gradient: float32 [1024], replicated
- first_gain_gradient: float32 [1024], replicated
- first_shift_gradient: float32 [1024], replicated
- second_gain_gradient: float32 [1024], replicated
- second_shift_gradient: float32 [1024], replicated
- up_gradient: float32 [1024, 4096], P('seq', 'tp')
- up_bias_gradient: float32 [4096], replicated
- down_gradient: float32 [4096, 1024], P('tp', 'seq')
- down_bias_gradient: float32 [1024], replicated
Inputs may be any that keep to these rules, and one draw needn't show every extreme that they name: `segments`: segment numbers never fall along the stream; each document spans 1 to 1024 tokens, and some document spans exactly 1024.
All inputs are finite; a program needn't handle non-finite values.
Results may differ from a plain program's by a relative error of at most 0.012.
Values may be sent and summed in bfloat16 or wider, within the bound.
No kernel may reach another device: no remote copies, remote signals or barrier semaphores. Data moves between devices by JAX's collectives and lax.ppermute only.
A program may use at most 128 MiB of HBM per device.

v0:
```python
import jax
import jax.numpy as jnp
from jax import lax
from jax.sharding import PartitionSpec as P

HEAD = 64
QUERY_BLOCK = 512
DOC_MAX = 1024


epsilon = 1e-05


def shifted(value, axis, steps):
    count = lax.axis_size(axis)
    leading, last = (max(0, -steps), min(count, count - steps))
    return lax.ppermute(value, axis, [(source, source + steps) for source in range(leading, last)])


def layer_norm(matrix, scale_gain, scale_shift):
    average = jnp.mean(matrix, axis=-1, keepdims=True)
    centered = matrix - average
    inverse = lax.rsqrt(jnp.mean(centered * centered, axis=-1, keepdims=True) + epsilon)
    return centered * inverse * scale_gain + scale_shift


def gelu_tanh(hidden):
    return jax.nn.gelu(hidden, approximate=True)


def merge_values(fresh, reused):
    row_count = fresh.shape[0]
    groups = fresh.shape[1] // (2 * HEAD)
    paired = jnp.stack(
        (fresh.reshape(row_count, groups, 2 * HEAD), reused.reshape(row_count, groups, 2 * HEAD)),
        axis=2,
    )
    return paired.reshape(row_count, 4 * groups * HEAD)


def split_values(merged):
    row_count = merged.shape[0]
    groups = merged.shape[1] // (4 * HEAD)
    paired = merged.reshape(row_count, groups, 2, 2 * HEAD)
    return (
        paired[:, :, 0].reshape(row_count, groups * 2 * HEAD),
        paired[:, :, 1].reshape(row_count, groups * 2 * HEAD),
    )


def rows_product(first_operand, second_operand):
    return lax.dot_general(
        first_operand, second_operand, (((0,), (0,)), ((), ())), preferred_element_type=jnp.float32
    )


def transposed_product(first_operand, second_operand):
    return lax.dot_general(
        first_operand, second_operand, (((1,), (1,)), ((), ())), preferred_element_type=jnp.float32
    )


def masked_scores(query_block, key_window, segment_query, segment_key):
    row_count = query_block.shape[0]
    window = key_window.shape[0]
    heads = query_block.shape[1] // HEAD
    scores = jnp.einsum(
        "qhd,khd->hqk",
        query_block.reshape(row_count, heads, HEAD),
        key_window.reshape(window, heads, HEAD),
        preferred_element_type=jnp.float32,
    ) * HEAD ** (-0.5)
    allowed = (segment_query[:, None] == segment_key[None, :]) & (
        jnp.arange(window)[None, :] <= jnp.arange(row_count)[:, None] + DOC_MAX
    )
    return jnp.where(allowed[None], scores, -1e30)


def widen(partial_sum, full_length, place):
    return lax.dynamic_update_slice_in_dim(
        jnp.zeros((full_length,), jnp.float32), partial_sum, place * partial_sum.shape[0], 0
    )


def local(
    stream,
    segments,
    skip_values,
    first_gain,
    first_shift,
    query_weight,
    query_bias,
    key_weight,
    value_weight,
    value_bias,
    mixing_weight,
    mixing_bias,
    second_gain,
    second_shift,
    up_weight,
    up_bias,
    down_weight,
    down_bias,
    cotangent,
):
    width = query_weight.shape[1]
    tok_count = skip_values.shape[0]
    block_count = tok_count // QUERY_BLOCK
    window = DOC_MAX + QUERY_BLOCK
    heads = width // HEAD
    tp_count = lax.axis_size("tp")
    seq_place = lax.axis_index("seq")
    tp_place = lax.axis_index("tp")
    stream_wide = stream.astype(jnp.float32)
    first_normed, first_pullback = jax.vjp(layer_norm, stream_wide, first_gain, first_shift)
    gathered_first = lax.all_gather(first_normed.astype(jnp.bfloat16), "tp", axis=0, tiled=True)
    query = (
        jnp.dot(gathered_first, query_weight, preferred_element_type=jnp.float32) + query_bias
    ).astype(jnp.bfloat16)
    keys = jnp.dot(gathered_first, key_weight, preferred_element_type=jnp.float32).astype(
        jnp.bfloat16
    )
    fresh = (
        jnp.dot(gathered_first, value_weight, preferred_element_type=jnp.float32) + value_bias
    ).astype(jnp.bfloat16)
    values = merge_values(fresh, skip_values)
    earlier = shifted(
        jnp.stack((keys[tok_count - DOC_MAX :], values[tok_count - DOC_MAX :])), "seq", 1
    )
    keys_ext = jnp.concatenate((earlier[0], keys), axis=0)
    values_ext = jnp.concatenate((earlier[1], values), axis=0)
    segment_padded = jnp.concatenate((jnp.full((DOC_MAX,), -1, jnp.int32), segments))
    segment_ext = lax.dynamic_slice_in_dim(
        segment_padded, seq_place * tok_count, DOC_MAX + tok_count, 0
    )

    def forward_block(block_index):
        row_start = block_index * QUERY_BLOCK
        query_block = lax.dynamic_slice_in_dim(query, row_start, QUERY_BLOCK, 0)
        key_window = lax.dynamic_slice_in_dim(keys_ext, row_start, window, 0)
        value_window = lax.dynamic_slice_in_dim(values_ext, row_start, window, 0)
        scores = masked_scores(
            query_block,
            key_window,
            lax.dynamic_slice_in_dim(segment_ext, row_start + DOC_MAX, QUERY_BLOCK, 0),
            lax.dynamic_slice_in_dim(segment_ext, row_start, window, 0),
        )
        maximum = jnp.max(scores, axis=-1, keepdims=True)
        exponent = jnp.exp(scores - maximum)
        denominator = jnp.sum(exponent, axis=-1, keepdims=True)
        probability = (exponent / denominator).astype(jnp.bfloat16)
        mixed = jnp.einsum(
            "hqk,khd->qhd",
            probability,
            value_window.reshape(window, heads, HEAD),
            preferred_element_type=jnp.float32,
        )
        return (
            mixed.reshape(QUERY_BLOCK, width).astype(jnp.bfloat16),
            maximum[..., 0] + jnp.log(denominator[..., 0]),
        )

    attended_blocks, log_totals = lax.map(forward_block, jnp.arange(block_count, dtype=jnp.int32))
    attended = attended_blocks.reshape(tok_count, width)
    middle = (
        stream_wide
        + lax.psum_scatter(
            jnp.dot(attended, mixing_weight, preferred_element_type=jnp.float32),
            "tp",
            scatter_dimension=0,
            tiled=True,
        )
        + mixing_bias
    )
    second_normed, second_pullback = jax.vjp(layer_norm, middle, second_gain, second_shift)
    gathered_second = lax.all_gather(second_normed.astype(jnp.bfloat16), "tp", axis=0, tiled=True)
    hidden = jnp.dot(gathered_second, up_weight, preferred_element_type=jnp.float32) + up_bias
    activated_wide, gelu_pullback = jax.vjp(gelu_tanh, hidden)
    activated = activated_wide.astype(jnp.bfloat16)
    output = (
        middle
        + lax.psum_scatter(
            jnp.dot(activated, down_weight, preferred_element_type=jnp.float32).astype(
                jnp.bfloat16
            ),
            "tp",
            scatter_dimension=0,
            tiled=True,
        ).astype(jnp.float32)
        + down_bias
    ).astype(jnp.bfloat16)
    upstream = cotangent.astype(jnp.float32)
    cotangent_all = lax.all_gather(cotangent, "tp", axis=0, tiled=True)
    activated_back = transposed_product(cotangent_all, down_weight)
    down_local = rows_product(activated, cotangent_all)
    hidden_back = gelu_pullback(activated_back)[0].astype(jnp.bfloat16)
    unit_column = jnp.ones((tok_count,), jnp.bfloat16)
    up_bias_part = jnp.dot(unit_column, hidden_back, preferred_element_type=jnp.float32)
    up_local = rows_product(gathered_second, hidden_back)
    second_normed_back = lax.psum_scatter(
        transposed_product(hidden_back, up_weight), "tp", scatter_dimension=0, tiled=True
    )
    middle_from_norm, second_gain_part, second_shift_part = second_pullback(second_normed_back)
    middle_back = upstream + middle_from_norm
    middle_all = lax.all_gather(middle_back.astype(jnp.bfloat16), "tp", axis=0, tiled=True)
    attended_back = transposed_product(middle_all, mixing_weight).astype(jnp.bfloat16)
    mixing_local = rows_product(attended, middle_all)

    def backward_block(carried, block_index):
        key_sum, value_sum = carried
        row_start = block_index * QUERY_BLOCK
        query_block = lax.dynamic_slice_in_dim(query, row_start, QUERY_BLOCK, 0)
        key_window = lax.dynamic_slice_in_dim(keys_ext, row_start, window, 0)
        value_window = lax.dynamic_slice_in_dim(values_ext, row_start, window, 0)
        scores = masked_scores(
            query_block,
            key_window,
            lax.dynamic_slice_in_dim(segment_ext, row_start + DOC_MAX, QUERY_BLOCK, 0),
            lax.dynamic_slice_in_dim(segment_ext, row_start, window, 0),
        )
        probability = jnp.exp(scores - log_totals[block_index][..., None])
        out_back = lax.dynamic_slice_in_dim(attended_back, row_start, QUERY_BLOCK, 0).reshape(
            QUERY_BLOCK, heads, HEAD
        )
        prob_back = jnp.einsum(
            "qhd,khd->hqk",
            out_back,
            value_window.reshape(window, heads, HEAD),
            preferred_element_type=jnp.float32,
        )
        correction = jnp.sum(probability * prob_back, axis=-1, keepdims=True)
        score_back = (probability * (prob_back - correction)).astype(jnp.bfloat16)
        query_part = jnp.einsum(
            "hqk,khd->qhd",
            score_back,
            key_window.reshape(window, heads, HEAD),
            preferred_element_type=jnp.float32,
        ) * HEAD ** (-0.5)
        key_part = jnp.einsum(
            "hqk,qhd->khd",
            score_back,
            query_block.reshape(QUERY_BLOCK, heads, HEAD),
            preferred_element_type=jnp.float32,
        ) * HEAD ** (-0.5)
        value_part = jnp.einsum(
            "hqk,qhd->khd",
            probability.astype(jnp.bfloat16),
            out_back,
            preferred_element_type=jnp.float32,
        )
        key_sum = lax.dynamic_update_slice_in_dim(
            key_sum,
            lax.dynamic_slice_in_dim(key_sum, row_start, window, 0)
            + key_part.reshape(window, width),
            row_start,
            0,
        )
        value_sum = lax.dynamic_update_slice_in_dim(
            value_sum,
            lax.dynamic_slice_in_dim(value_sum, row_start, window, 0)
            + value_part.reshape(window, width),
            row_start,
            0,
        )
        return ((key_sum, value_sum), query_part.reshape(QUERY_BLOCK, width))

    empty_sum = jnp.zeros((DOC_MAX + tok_count, width), jnp.float32)
    (key_ext_back, value_ext_back), query_blocks = lax.scan(
        backward_block, (empty_sum, empty_sum), jnp.arange(block_count, dtype=jnp.int32)
    )
    returned = shifted(
        jnp.stack((key_ext_back[:DOC_MAX], value_ext_back[:DOC_MAX])).astype(jnp.bfloat16),
        "seq",
        -1,
    ).astype(jnp.float32)
    key_back = jnp.concatenate(
        (key_ext_back[DOC_MAX:tok_count], key_ext_back[tok_count:] + returned[0]), axis=0
    ).astype(jnp.bfloat16)
    value_back = jnp.concatenate(
        (value_ext_back[DOC_MAX:tok_count], value_ext_back[tok_count:] + returned[1]), axis=0
    )
    fresh_wide, skip_gradient = split_values(value_back)
    fresh_back = fresh_wide.astype(jnp.bfloat16)
    query_back = query_blocks.reshape(tok_count, width).astype(jnp.bfloat16)
    query_bias_part = jnp.dot(unit_column, query_back, preferred_element_type=jnp.float32)
    value_bias_part = jnp.dot(unit_column, fresh_back, preferred_element_type=jnp.float32)
    query_local = rows_product(gathered_first, query_back)
    key_local = rows_product(gathered_first, key_back)
    value_local = rows_product(gathered_first, fresh_back)
    total = transposed_product(query_back, query_weight)
    total = total + transposed_product(key_back, key_weight)
    first_normed_back = lax.psum_scatter(
        total + transposed_product(fresh_back, value_weight), "tp", scatter_dimension=0, tiled=True
    )
    stream_from_norm, first_gain_part, first_shift_part = first_pullback(first_normed_back)
    stream_gradient = middle_back + stream_from_norm
    (
        first_gain_gradient,
        first_shift_gradient,
        second_gain_gradient,
        second_shift_gradient,
        mixing_bias_gradient,
        down_bias_gradient,
        query_bias_gradient,
        value_bias_gradient,
        up_bias_gradient,
    ) = lax.psum(
        (
            first_gain_part,
            first_shift_part,
            second_gain_part,
            second_shift_part,
            jnp.sum(middle_back, axis=0),
            jnp.sum(upstream, axis=0),
            widen(query_bias_part, width * tp_count, tp_place),
            widen(value_bias_part, value_bias_part.shape[0] * tp_count, tp_place),
            widen(up_bias_part, up_bias_part.shape[0] * tp_count, tp_place),
        ),
        ("seq", "tp"),
    )
    query_gradient, key_gradient, value_gradient, mixing_gradient, up_gradient, down_gradient = (
        lax.psum_scatter(query_local, "seq", scatter_dimension=0, tiled=True),
        lax.psum_scatter(key_local, "seq", scatter_dimension=0, tiled=True),
        lax.psum_scatter(value_local, "seq", scatter_dimension=0, tiled=True),
        lax.psum_scatter(mixing_local, "seq", scatter_dimension=1, tiled=True),
        lax.psum_scatter(up_local, "seq", scatter_dimension=0, tiled=True),
        lax.psum_scatter(down_local, "seq", scatter_dimension=1, tiled=True),
    )
    return (
        output,
        stream_gradient,
        skip_gradient,
        query_gradient,
        query_bias_gradient,
        key_gradient,
        value_gradient,
        value_bias_gradient,
        mixing_gradient,
        mixing_bias_gradient,
        first_gain_gradient,
        first_shift_gradient,
        second_gain_gradient,
        second_shift_gradient,
        up_gradient,
        up_bias_gradient,
        down_gradient,
        down_bias_gradient,
    )


def solution(mesh):
    in_specs = (
        P(("seq", "tp"), None),
        P(),
        P("seq", "tp"),
        P(),
        P(),
        P(None, "tp"),
        P("tp"),
        P(None, "tp"),
        P(None, "tp"),
        P("tp"),
        P("tp", None),
        P(),
        P(),
        P(),
        P(None, "tp"),
        P("tp"),
        P("tp", None),
        P(),
        P(("seq", "tp"), None),
    )
    out_specs = (
        P(("seq", "tp"), None),
        P(("seq", "tp"), None),
        P("seq", "tp"),
        P("seq", "tp"),
        P(),
        P("seq", "tp"),
        P("seq", "tp"),
        P(),
        P("tp", "seq"),
        P(),
        P(),
        P(),
        P(),
        P(),
        P("seq", "tp"),
        P(),
        P("tp", "seq"),
        P(),
    )
    return jax.shard_map(local, mesh=mesh, in_specs=in_specs, out_specs=out_specs, check_vma=False)
```

profile of v0, /device:TPU:0, one launch (start us, length us, event | category | flops | bytes accessed | tf_op | source)
XLA Modules:
  0.0 1425.8 jit_solution(13958946887283911155)
XLA Ops:
  10.6 2.7 fusion.27
  13.6 83.3 %all-gather.5.cloned.1.call-done = bf16[2048,1024]{1,0:T(8,128)(2,1)} async-done(((bf16[512,1024]{1,0:T(8,128)(2,1)}), bf16[2048,1024]{1,0:T(8,128)(2,1)}) %all-gather.5.cloned.1.call-update) | async-done | bytes 4194320 | tf_op jit(solution)/shard_map/all_gather | solution.py:116
  96.9 3.7 fusion.25
  103.5 3.6 convolution_convert_fusion.2
  109.2 2.8 collective-permute-start
  112.0 4.5 fusion.21
  123.3 2.6 copy.49
  130.2 64.8 %while.30 = (s32[]{:T(128)}, bf16[4,512,256]{2,1,0:T(8,128)(2,1)}, f32[4,4,512]{2,1,0:T(4,128)S(1)}, s32[4]{0:T(128)S(1)}, bf16[3072,256]{0,1:T(8,128)(2,1)}, /*...) while((s32[]{:T(128)}, bf16[4,512,256]{2,1,0:T(8,128)(2,1)}, ...), condition=%wide.region_5.6_spmd, body=%wide.region_2.5_spmd.sunk | while | flops 845543936 | bytes 47804716 | solution.py:163
  137.4 3.5 fusion.143
  141.0 4.5 fusion.144
  153.6 3.5 fusion.143
  157.2 4.5 fusion.144
  169.8 3.5 fusion.143
  173.4 4.5 fusion.144
  186.0 3.5 fusion.143
  189.6 4.5 fusion.144
  195.0 5.7 fusion.67
  200.8 148.9 %reduce-scatter.11.cloned.1.call-done = f32[512,1024]{1,0:T(8,128)} async-done(((f32[2048,1024]{1,0:T(8,128)}), f32[512,1024]{1,0:T(8,128)}) %reduce-scatter.11.cloned.1.call-update) | async-done | bytes 2097168 | tf_op jit(solution)/shard_map/reduce_scatter | solution.py:167
  355.3 80.6 %all-gather.7.cloned.1.call-done = bf16[2048,1024]{1,0:T(8,128)(2,1)} async-done(((bf16[512,1024]{1,0:T(8,128)(2,1)}), bf16[2048,1024]{1,0:T(8,128)(2,1)}) %all-gather.7.cloned.1.call-update) | async-done | bytes 4194320 | tf_op jit(solution)/shard_map/all_gather | solution.py:176
  435.9 8.9 fusion.68
  444.8 71.8 %all-gather.9.cloned.1.call-done = bf16[2048,1024]{1,0:T(8,128)(2,1)} async-done(((bf16[512,1024]{1,0:T(8,128)(2,1)}), bf16[2048,1024]{1,0:T(8,128)(2,1)}) %all-gather.9.cloned.1.call-update) | async-done | bytes 4194320 | tf_op jit(solution)/shard_map/all_gather | solution.py:193
  516.6 12.7 fusion.16
  531.3 7.0 fusion.69
  539.8 11.4 convolution_convert_fusion
  551.4 130.2 %reduce-scatter.15.cloned.1.call-done = f32[512,1024]{1,0:T(8,128)} async-done(((f32[2048,1024]{1,0:T(8,128)}), f32[512,1024]{1,0:T(8,128)}) %reduce-scatter.15.cloned.1.call-update) | async-done | bytes 2097168 | tf_op jit(solution)/shard_map/reduce_scatter | solution.py:200
  681.5 2.9 multiply_reduce_fusion.1
  684.5 76.6 %reduce-scatter.13.cloned.1.call-done = bf16[512,1024]{1,0:T(8,128)(2,1)} async-done(((bf16[2048,1024]{1,0:T(8,128)(2,1)}), bf16[512,1024]{1,0:T(8,128)(2,1)}) %reduce-scatter.13.cloned.1.call-update) | async-done | bytes 1048592 | tf_op jit(solution)/shard_map/reduce_scatter | solution.py:182
  761.1 3.7 fusion.61
  767.5 81.4 %all-gather.11.cloned.1.call-done = bf16[2048,1024]{1,0:T(8,128)(2,1)} async-done(((bf16[512,1024]{1,0:T(8,128)(2,1)}), bf16[2048,1024]{1,0:T(8,128)(2,1)}) %all-gather.11.cloned.1.call-update) | async-done | bytes 4194320 | tf_op jit(solution)/shard_map/all_gather | solution.py:205
  848.8 4.5 convolution_convert_fusion.1
  857.4 122.1 %while.31 = (s32[]{:T(128)}, f32[3072,256]{0,1:T(8,128)}, f32[3072,256]{0,1:T(8,128)}, bf16[4,512,256]{2,1,0:T(8,128)(2,1)}, s32[4]{0:T(128)S(1)}, /*index=5*/bf...) while((s32[]{:T(128)}, f32[3072,256]{0,1:T(8,128)}, ...), condition=%wide.region_15.16_spmd, body=%wide.region_13.15_spmd.sunk | while | flops 2045377024 | bytes 155783632 | solution.py:268
  867.1 4.3 multiply_reduce_fusion.5
  871.4 3.6 multiply_convert_fusion.5
  878.3 2.7 convolution_multiply_fusion.5
  884.1 4.0 constant_dynamic-update-slice_fusion.8
  897.6 4.3 multiply_reduce_fusion.5
  901.9 3.6 multiply_convert_fusion.5
  908.8 2.7 convolution_multiply_fusion.5
  914.6 4.0 constant_dynamic-update-slice_fusion.8
  928.1 4.3 multiply_reduce_fusion.5
  932.4 3.6 multiply_convert_fusion.5
  939.3 2.7 convolution_multiply_fusion.5
  945.0 4.0 constant_dynamic-update-slice_fusion.8
  958.6 4.3 multiply_reduce_fusion.5
  962.9 3.6 multiply_convert_fusion.5
  969.8 2.7 convolution_multiply_fusion.5
  975.6 4.0 constant_dynamic-update-slice_fusion.8
  992.3 4.6 add_add_fusion
  997.0 10.0 fusion.73
  1007.7 12.6 fusion.59
  1020.4 4.9 fusion.72
  1025.3 4.4 fusion.71
  1029.9 2.8 fusion.39
  1033.3 4.4 fusion.52
  1038.1 4.5 fusion.35
  1043.9 2.5 copy.55
  1046.7 104.6 %reduce-scatter.17.cloned.1.call-done = f32[512,1024]{1,0:T(8,128)} async-done(((f32[2048,1024]{1,0:T(8,128)}), f32[512,1024]{1,0:T(8,128)}) %reduce-scatter.17.cloned.1.call-update) | async-done | bytes 2097168 | tf_op jit(solution)/shard_map/reduce_scatter | solution.py:292
  1157.0 42.2 %all-reduce.1 = (f32[1024]{0:T(1024)}, f32[512]{0:T(512)}, f32[1024]{0:T(1024)}, f32[1024]{0:T(1024)}, f32[1024]{0:T(1024)}, /*index=5*/f32[1024]{0:T(1024)}, f32[1024]{0:T(1024)}, f32[4096]{0:T(1024)}, f32[1024]{0:T(1024)}) all-reduce(f32[1024]{0:T(1024)S(1)} %dynamic_update_slice.42, ...), channel_id=1, replica_groups=mesh['seq'=8,'tp'=4] {'seq','tp'}, use_global_device_ids=true, to_apply=%region_20.21 | all-reduce | flops 11776 | bytes 94208 | tf_op jit(solution)/shard_map/psum | solution.py:307
  1199.2 8.0 reduce-scatter.27.cloned.1.call-done
  1207.2 54.9 %reduce-scatter.29.cloned.1.call-done = f32[1024,128]{1,0:T(8,128)} async-done(((f32[1024,1024]{1,0:T(8,128)}), f32[1024,128]{1,0:T(8,128)}) %reduce-scatter.29.cloned.1.call-update) | async-done | bytes 524304 | tf_op jit(solution)/shard_map/reduce_scatter | solution.py:327
  1262.0 39.7 %reduce-scatter.25.cloned.1.call-done = f32[256,128]{1,0:T(8,128)} async-done(((f32[256,1024]{1,0:T(8,128)}), f32[256,128]{1,0:T(8,128)}) %reduce-scatter.25.cloned.1.call-update) | async-done | bytes 131088 | tf_op jit(solution)/shard_map/reduce_scatter | solution.py:325
  1301.8 39.6 %reduce-scatter.19.cloned.1.call-done = f32[128,256]{1,0:T(8,128)} async-done(((f32[1024,256]{1,0:T(8,128)}), f32[128,256]{1,0:T(8,128)}) %reduce-scatter.19.cloned.1.call-update) | async-done | bytes 131088 | tf_op jit(solution)/shard_map/reduce_scatter | solution.py:322
  1341.4 37.8 %reduce-scatter.23.cloned.1.call-done = f32[128,128]{1,0:T(8,128)} async-done(((f32[1024,128]{1,0:T(8,128)}), f32[128,128]{1,0:T(8,128)}) %reduce-scatter.23.cloned.1.call-update) | async-done | bytes 65552 | tf_op jit(solution)/shard_map/reduce_scatter | solution.py:324
  1379.2 39.6 %reduce-scatter.21.cloned.1.call-done = f32[128,256]{1,0:T(8,128)} async-done(((f32[1024,256]{1,0:T(8,128)}), f32[128,256]{1,0:T(8,128)}) %reduce-scatter.21.cloned.1.call-update) | async-done | bytes 131088 | tf_op jit(solution)/shard_map/reduce_scatter | solution.py:323
  (317 shorter events, 139.8 us)
Async XLA Ops:
  7.2 428.7 %copy-start = (bf16[1024,1024]{1,0:T(8,128)(2,1)S(1)}, bf16[1024,1024]{1,0:T(8,128)(2,1)}, u32[]{:S(2)}) copy-start(bf16[1024,1024]{1,0:T(8,128)(2,1)} %param.37) | copy-start | bytes 6291460
  7.2 6.1 copy-start.31
  7.2 89.7 %copy-start.25 = (bf16[1024,128]{1,0:T(8,128)(2,1)S(1)}, bf16[1024,128]{1,0:T(8,128)(2,1)}, u32[]{:S(2)}) copy-start(bf16[1024,128]{1,0:T(8,128)(2,1)} %param.31) | copy-start | bytes 786436
  7.2 89.6 %copy-start.48 = (f32[128]{0:T(128)S(1)}, f32[128]{0:T(128)}, u32[]{:S(2)}) copy-start(f32[128]{0:T(128)} %param.32) | copy-start | bytes 1540
  7.2 89.6 %all-gather.5.cloned.1.call-start = ((), (), s32[]{:S(2)}) async-start(), calls=%async_computation.10 | async-start | bytes 5242880 | tf_op jit(solution)/shard_map/all_gather | solution.py:116
  8.9 4.4 copy-start.32
  10.5 2.7 copy-start.41
  10.5 2.7 copy-start.37
  13.3 336.4 %reduce-scatter.11.cloned.1.call-start = ((), (), s32[]{:S(2)}) async-start(), calls=%async_computation.11 | async-start | bytes 10485760 | tf_op jit(solution)/shard_map/reduce_scatter | solution.py:167
  103.5 4.7 copy-start.22
  108.1 3.9 copy-start.35
  108.1 4.0 copy-start.52
  109.2 10.7 collective-permute-start
  118.9 3.1 copy-start.19
  122.0 5.9 copy-start.16
  130.2 64.8 %copy-start.27 = (bf16[256,1024]{1,0:T(8,128)(2,1)S(1)}, bf16[256,1024]{1,0:T(8,128)(2,1)}, u32[]{:S(2)}) copy-start(bf16[256,1024]{1,0:T(8,128)(2,1)} %param.33) | copy-start | bytes 1572868
  200.7 149.0 %copy-start.8 = (bf16[512,1024]{1,0:T(8,128)(2,1)S(1)}, bf16[512,1024]{1,0:T(8,128)(2,1)}, u32[]{:S(2)}) copy-start(bf16[512,1024]{1,0:T(8,128)(2,1)} %param.23) | copy-start | bytes 3145732
  200.7 149.0 %copy-start.47 = (f32[1024]{0:T(1024)S(1)}, f32[1024]{0:T(1024)}, u32[]{:S(2)}) copy-start(f32[1024]{0:T(1024)} %param.34) | copy-start | bytes 12292
  200.8 152.2 %copy-start.36 = (f32[1024]{0:T(1024)S(1)}, f32[1024]{0:T(1024)}, u32[]{:S(2)}) copy-start(f32[1024]{0:T(1024)} %param.35) | copy-start | bytes 12292
  200.8 152.2 %copy-start.45 = (f32[1024]{0:T(1024)S(1)}, f32[1024]{0:T(1024)}, u32[]{:S(2)}) copy-start(f32[1024]{0:T(1024)} %param.36) | copy-start | bytes 12292
  200.8 235.1 %all-gather.7.cloned.1.call-start = ((), (), s32[]{:S(2)}) async-start(), calls=%async_computation.12 | async-start | bytes 5242880 | tf_op jit(solution)/shard_map/all_gather | solution.py:176
  354.4 162.2 %all-gather.9.cloned.1.call-start = ((), (), s32[]{:S(2)}) async-start(), calls=%async_computation.14 | async-start | bytes 5242880 | tf_op jit(solution)/shard_map/all_gather | solution.py:193
  355.0 161.6 %copy-start.50 = (f32[1024]{0:T(1024)S(1)}, f32[1024]{0:T(1024)}, u32[]{:S(2)}) copy-start(f32[1024]{0:T(1024)} %param.38) | copy-start | bytes 12292
  355.0 326.6 %reduce-scatter.15.cloned.1.call-start = ((), (), s32[]{:S(2)}) async-start(), calls=%async_computation.15 | async-start | bytes 10485760 | tf_op jit(solution)/shard_map/reduce_scatter | solution.py:200
  538.3 222.8 %reduce-scatter.13.cloned.1.call-start = ((), (), s32[]{:S(2)}) async-start(), calls=%async_computation.13 | async-start | bytes 5242880 | tf_op jit(solution)/shard_map/reduce_scatter | solution.py:182
  551.3 130.2 %copy-start.7 = (f32[512,1024]{1,0:T(8,128)S(1)}, f32[512,1024]{1,0:T(8,128)}, u32[]{:S(2)}) copy-start(f32[512,1024]{1,0:T(8,128)} %copy-done.6) | copy-start | bytes 6291460
  551.3 209.8 %copy-start.46 = (f32[1024]{0:T(1024)S(1)}, f32[1024]{0:T(1024)}, u32[]{:S(2)}) copy-start(f32[1024]{0:T(1024)} %param.40) | copy-start | bytes 12292
  551.3 297.5 %all-gather.11.cloned.1.call-start = ((), (), s32[]{:S(2)}) async-start(), calls=%async_computation.16 | async-start | bytes 5242880 | tf_op jit(solution)/shard_map/all_gather | solution.py:205
  684.5 81.6 %copy-start.13 = (bf16[512,1024]{1,0:T(8,128)(2,1)S(1)}, bf16[512,1024]{1,0:T(8,128)(2,1)}, u32[]{:S(2)}) copy-start(bf16[512,1024]{1,0:T(8,128)(2,1)} %param.41) | copy-start | bytes 3145732
  764.8 84.0 %copy-start.28 = (bf16[256,1024]{1,0:T(8,128)(2,1)S(1)}, bf16[256,1024]{1,0:T(8,128)(2,1)}, u32[]{:S(2)}) copy-start(bf16[256,1024]{1,0:T(8,128)(2,1)} %param.33) | copy-start | bytes 1572868
  764.8 88.6 %copy-start.39 = (f32[512]{0:T(512)}, f32[512]{0:T(512)S(1)}, u32[]{:S(2)}) copy-start(f32[512]{0:T(512)S(1)} %negate_multiply_fusion.1) | copy-start | bytes 6148
  767.4 383.9 %reduce-scatter.17.cloned.1.call-start = ((), (), s32[]{:S(2)}) async-start(), calls=%async_computation.17 | async-start | bytes 10485760 | tf_op jit(solution)/shard_map/reduce_scatter | solution.py:292
  862.0 3.2 copy-start.5
  875.0 3.4 copy-start.2
  881.0 3.0 copy-start.3
  892.5 3.2 copy-start.5
  905.5 3.4 copy-start.2
  911.5 3.0 copy-start.3
  923.0 3.2 copy-start.5
  935.9 3.4 copy-start.2
  942.0 3.0 copy-start.3
  953.5 3.2 copy-start.5
  966.4 3.4 copy-start.2
  972.5 3.0 copy-start.3
  983.0 9.2 copy-start.20
  983.2 4.7 collective-permute-start.1
  989.8 2.4 copy-start.23
  996.9 210.2 %reduce-scatter.27.cloned.1.call-start = ((), (), s32[]{:S(2)}) async-start(), calls=%async_computation.22 | async-start | bytes 4718592 | tf_op jit(solution)/shard_map/reduce_scatter | solution.py:326
  1007.0 255.0 %reduce-scatter.29.cloned.1.call-start = ((), (), s32[]{:S(2)}) async-start(), calls=%async_computation.23 | async-start | bytes 4718592 | tf_op jit(solution)/shard_map/reduce_scatter | solution.py:327
  1020.3 281.5 %reduce-scatter.25.cloned.1.call-start = ((), (), s32[]{:S(2)}) async-start(), calls=%async_computation.21 | async-start | bytes 1179648 | tf_op jit(solution)/shard_map/reduce_scatter | solution.py:325
  1025.3 316.1 %reduce-scatter.19.cloned.1.call-start = ((), (), s32[]{:S(2)}) async-start(), calls=%async_computation.18 | async-start | bytes 1179648 | tf_op jit(solution)/shard_map/reduce_scatter | solution.py:322
  1029.8 349.4 %reduce-scatter.23.cloned.1.call-start = ((), (), s32[]{:S(2)}) async-start(), calls=%async_computation.20 | async-start | bytes 589824 | tf_op jit(solution)/shard_map/reduce_scatter | solution.py:324
  1033.3 4.8 copy-start.21
  1033.3 4.8 copy-start.24
  1037.8 381.0 %reduce-scatter.21.cloned.1.call-start = ((), (), s32[]{:S(2)}) async-start(), calls=%async_computation.19 | async-start | bytes 1179648 | tf_op jit(solution)/shard_map/reduce_scatter | solution.py:323
  1042.6 108.7 %copy-start.9 = (bf16[512,1024]{1,0:T(8,128)(2,1)S(1)}, bf16[512,1024]{1,0:T(8,128)(2,1)}, u32[]{:S(2)}) copy-start(bf16[512,1024]{1,0:T(8,128)(2,1)} %param.23) | copy-start | bytes 3145732
  1042.6 108.7 %copy-start.33 = (f32[512]{0:T(512)S(1)}, f32[512]{0:T(512)}, u32[]{:S(2)}) copy-start(f32[512]{0:T(512)} %copy-done.32) | copy-start | bytes 6148
  1042.6 108.7 %copy-start.34 = (f32[1024]{0:T(1024)S(1)}, f32[1024]{0:T(1024)}, u32[]{:S(2)}) copy-start(f32[1024]{0:T(1024)} %param.26) | copy-start | bytes 12292
  1043.7 109.9 %copy-start.42 = (f32[512]{0:T(512)S(1)}, f32[512]{0:T(512)}, u32[]{:S(2)}) copy-start(f32[512]{0:T(512)} %copy-done.41) | copy-start | bytes 6148
  1043.7 109.9 %copy-start.38 = (f32[512]{0:T(512)S(1)}, f32[512]{0:T(512)}, u32[]{:S(2)}) copy-start(f32[512]{0:T(512)} %copy-done.37) | copy-start | bytes 6148
  1046.7 108.0 %copy-start.40 = (f32[512]{0:T(512)S(1)}, f32[512]{0:T(512)}, u32[]{:S(2)}) copy-start(f32[512]{0:T(512)} %copy-done.39) | copy-start | bytes 6148
  1151.3 3.4 copy-start.12
  1151.3 3.4 copy-start.14
  1154.6 264.1 %copy-start.1 = (bf16[1024,1024]{1,0:T(8,128)(2,1)S(1)}, bf16[1024,1024]{1,0:T(8,128)(2,1)}, u32[]{:S(2)}) copy-start(bf16[1024,1024]{1,0:T(8,128)(2,1)} %param.37) | copy-start | bytes 6291460
  (14 other events, 23.0 us)
Sparse Core Ops, SparseCore 0:
  13.4 83.4 all-gather.4
  200.9 148.7 reduce-scatter.10
  354.5 81.3 all-gather.6
  437.3 79.2 all-gather.8
  538.4 143.0 reduce-scatter.14
  683.7 77.3 reduce-scatter.12
  767.5 81.2 all-gather.10
  997.0 154.1 reduce-scatter.16
  1155.2 51.9 reduce-scatter.26
  1210.9 51.0 reduce-scatter.28
  1265.8 35.9 reduce-scatter.24
  1305.4 35.9 reduce-scatter.18
  1345.0 34.0 reduce-scatter.22
  1382.8 35.9 reduce-scatter.20
where the time goes:
time: 1430 us
  waiting for transfers between devices  999 us (70%)
  matrix products  191 us (13%)
  other arithmetic  85.1 us (6%)
  local copies, waits for them, and re-layouts  72.8 us (5%)
  blocking collectives  42.2 us (3%)
  between operations  15.1 us (1%)
    reduce_scatter x1, waiting for transfers between devices, local(): lax.psum_scatter(jnp.dot(attended, mixing_weight, preferred_element_type=...  149 us
    reduce_scatter x1, waiting for transfers between devices, local(): lax.psum_scatter(transposed_product(hidden_back, up_weight), 'tp', scatte...  130 us
    reduce_scatter x1, waiting for transfers between devices, local(): lax.psum_scatter(total + transposed_product(fresh_back, value_weight), 't...  105 us
    all_gather x1, waiting for transfers between devices, local(): lax.all_gather(first_normed.astype(jnp.bfloat16), 'tp', axis=0, tiled=True)  83.3 us
    all_gather x1, waiting for transfers between devices, local(): lax.all_gather(middle_back.astype(jnp.bfloat16), 'tp', axis=0, tiled=True)  81.4 us
    all_gather x1, waiting for transfers between devices, local(): lax.all_gather(second_normed.astype(jnp.bfloat16), 'tp', axis=0, tiled=True)  80.6 us
    reduce_scatter x1, waiting for transfers between devices, local(): lax.psum_scatter(jnp.dot(activated, down_weight, preferred_element_type=j...  76.6 us
    all_gather x1, waiting for transfers between devices, local(): cotangent_all = lax.all_gather(cotangent, 'tp', axis=0, tiled=True)  71.8 us
  transfers between devices with their start and end apart: 16, of which 15 were waited for; matrix products, arithmetic and copies ran while one was open for 6% of the time, Pallas kernels for 0%

commit v1 on v0

v1 whole, which is shorter than its diff:
```python
import functools

import jax
import jax.numpy as jnp
from jax import lax
from jax.experimental import pallas as pl
from jax.experimental.pallas import tpu as pltpu
from jax.sharding import PartitionSpec as P

HEAD = 64
DOC_MAX = 1024
PAIR = 2 * HEAD
TILE = 256
UNIT = 512
EPSILON = 1e-05
F32 = jnp.float32
BF16 = jnp.bfloat16
SCALE = HEAD ** -0.5
GELU_A = 0.7978845608028654
GELU_B = 0.044715


def dot(a, b, dims, out=F32):
    return lax.dot_general(a, b, (dims, ((), ())), preferred_element_type=out)


def nn(a, b):
    return dot(a, b, ((1,), (0,)))


def nt(a, b):
    return dot(a, b, ((1,), (1,)))


def tn(a, b):
    return dot(a, b, ((0,), (0,)))


def wide(tile):
    lane = lax.broadcasted_iota(jnp.int32, tile.shape, 1)
    zero = jnp.zeros_like(tile)
    return jnp.concatenate(
        (jnp.where(lane < HEAD, tile, zero), jnp.where(lane < HEAD, zero, tile)), axis=0
    )


def both(row):
    return jnp.concatenate((row, row), axis=1)


def heads_of(acc):
    return jnp.concatenate((acc[:HEAD, :TILE], acc[HEAD:, TILE:]), axis=0)


def mask_rows(start_ref, step, shift):
    start = both(start_ref[...] - shift)
    place = both((step + 4) * TILE + lax.broadcasted_iota(jnp.int32, (1, TILE), 1))
    return start, place


def allowed(tile_index, start, place):
    key = tile_index * TILE + lax.broadcasted_iota(jnp.int32, (TILE, 2 * TILE), 0)
    return (key >= start) & (key <= place)


def attend_kernel(base, shift, low_ref, start_ref, q_ref, k_ref, v_ref, *rest):
    o_ref, turned_ref, log_ref, acc_ref = rest[-4:]
    step = pl.program_id(0)
    query = wide(q_ref[...] * jnp.asarray(SCALE, BF16))
    start, place = mask_rows(start_ref, step, shift)
    acc_ref[...] = jnp.zeros_like(acc_ref)

    def body(j, carried):
        top, total = carried
        rows = pl.ds(pl.multiple_of(j * TILE, TILE), TILE)
        scores = nt(k_ref[rows, :], query)
        scores = jnp.where(allowed(j, start, place), scores, -1e30)
        new_top = jnp.maximum(top, jnp.max(scores, axis=0, keepdims=True))
        part = jnp.exp(scores - new_top)
        factor = jnp.exp(top - new_top)
        total = total * factor + jnp.sum(part, axis=0, keepdims=True)
        acc_ref[...] = acc_ref[...] * factor + tn(v_ref[rows, :], part.astype(BF16))
        return new_top, total

    top, total = lax.fori_loop(
        low_ref[base + step] - shift // TILE,
        step + 5,
        body,
        (jnp.full((1, 2 * TILE), -1e30, F32), jnp.zeros((1, 2 * TILE), F32)),
    )
    turned = heads_of(acc_ref[...] / total)
    turned_ref[...] = turned
    o_ref[...] = turned.T.astype(BF16)
    logs = top + jnp.log(total)
    log_ref[0:1, :] = logs[:, :TILE]
    log_ref[1:2, :] = logs[:, TILE:]


def attend(base, shift, low, start, q, qcol, k, kcol, v, vcol, earlier, tokens):
    n = k.shape[0]
    steps = (n - DOC_MAX) // TILE
    alias = earlier is not None
    specs = [
        pl.BlockSpec((1, TILE), lambda i, *_: (0, base + i)),
        pl.BlockSpec((TILE, PAIR), lambda i, *_: (base + i, qcol)),
        pl.BlockSpec((n, PAIR), lambda i, *_: (0, kcol)),
        pl.BlockSpec((n, PAIR), lambda i, *_: (0, vcol)),
    ] + [pl.BlockSpec(memory_space=pl.ANY)] * (3 if alias else 0)
    return pl.pallas_call(
        functools.partial(attend_kernel, base, shift),
        grid_spec=pltpu.PrefetchScalarGridSpec(
            num_scalar_prefetch=1,
            grid=(steps,),
            in_specs=specs,
            out_specs=[
                pl.BlockSpec((TILE, PAIR), lambda i, *_: (base + i, 0)),
                pl.BlockSpec((PAIR, TILE), lambda i, *_: (0, base + i)),
                pl.BlockSpec((8, TILE), lambda i, *_: (0, base + i)),
            ],
            scratch_shapes=[pltpu.VMEM((PAIR, 2 * TILE), F32)],
        ),
        out_shape=[
            jax.ShapeDtypeStruct((tokens, PAIR), BF16),
            jax.ShapeDtypeStruct((PAIR, tokens), F32),
            jax.ShapeDtypeStruct((8, tokens), F32),
        ],
        input_output_aliases={5: 0, 6: 1, 7: 2} if alias else {},
        cost_estimate=pl.CostEstimate(
            flops=4 * steps * 3 * TILE * TILE * 2 * PAIR,
            bytes_accessed=4 * n * PAIR + 8 * steps * TILE * PAIR,
            transcendentals=steps * 3 * TILE * 2 * TILE,
        ),
        name="attend",
    )(low, start, q, k, v, *(earlier if alias else ()))


def attend_back_kernel(base, shift, first, low_ref, start_ref, q_ref, k_ref, v_ref, do_ref, turned_ref, log_ref, *rest):
    if first:
        dq_ref, dk_ref, dv_ref, acc_ref = rest
    else:
        dk_in, dv_in, _, dq_ref, dk_ref, dv_ref, acc_ref = rest
    step = pl.program_id(0)

    @pl.when(step == 0)
    def _():
        dk_ref[...] = jnp.zeros_like(dk_ref)
        dv_ref[...] = jnp.zeros_like(dv_ref)
        if not first:
            held = dk_in.shape[0]
            dk_ref[:held, :] = dk_in[...]
            dv_ref[:held, :] = dv_in[...]

    query = wide(q_ref[...] * jnp.asarray(SCALE, BF16))
    out_back = wide(do_ref[...])
    start, place = mask_rows(start_ref, step, shift)
    product = do_ref[...].astype(F32).T * turned_ref[...]
    delta = jnp.concatenate(
        (
            jnp.sum(product[:HEAD], axis=0, keepdims=True),
            jnp.sum(product[HEAD:], axis=0, keepdims=True),
        ),
        axis=1,
    )
    logs = jnp.concatenate((log_ref[0:1, :], log_ref[1:2, :]), axis=1)
    acc_ref[...] = jnp.zeros_like(acc_ref)

    def body(j, carried):
        rows = pl.ds(pl.multiple_of(j * TILE, TILE), TILE)
        key_tile = k_ref[rows, :]
        scores = jnp.where(allowed(j, start, place), nt(key_tile, query), -1e30)
        prob = jnp.exp(scores - logs)
        prob_back = nt(v_ref[rows, :], out_back)
        score_back = (prob * (prob_back - delta)).astype(BF16)
        dv_ref[rows, :] += nn(prob.astype(BF16), out_back)
        dk_ref[rows, :] += nn(score_back, query)
        acc_ref[...] += tn(key_tile, score_back)
        return carried

    lax.fori_loop(low_ref[base + step] - shift // TILE, step + 5, body, 0)
    dq_ref[...] = (heads_of(acc_ref[...]) * SCALE).T.astype(BF16)


def attend_back(base, shift, low, start, q, qcol, k, kcol, v, vcol, do, turned, logs, earlier, tokens):
    n = k.shape[0]
    steps = (n - DOC_MAX) // TILE
    first = earlier is None
    held = n - DOC_MAX
    specs = [
        pl.BlockSpec((1, TILE), lambda i, *_: (0, base + i)),
        pl.BlockSpec((TILE, PAIR), lambda i, *_: (base + i, qcol)),
        pl.BlockSpec((n, PAIR), lambda i, *_: (0, kcol)),
        pl.BlockSpec((n, PAIR), lambda i, *_: (0, vcol)),
        pl.BlockSpec((TILE, PAIR), lambda i, *_: (base + i, 0)),
        pl.BlockSpec((PAIR, TILE), lambda i, *_: (0, base + i)),
        pl.BlockSpec((8, TILE), lambda i, *_: (0, base + i)),
    ]
    if not first:
        specs += [
            pl.BlockSpec((held, PAIR), lambda i, *_: (DOC_MAX // held, 0)),
            pl.BlockSpec((held, PAIR), lambda i, *_: (DOC_MAX // held, 0)),
            pl.BlockSpec(memory_space=pl.ANY),
        ]
    return pl.pallas_call(
        functools.partial(attend_back_kernel, base, shift, first),
        grid_spec=pltpu.PrefetchScalarGridSpec(
            num_scalar_prefetch=1,
            grid=(steps,),
            in_specs=specs,
            out_specs=[
                pl.BlockSpec((TILE, PAIR), lambda i, *_: (base + i, 0)),
                pl.BlockSpec((n, PAIR), lambda i, *_: (0, 0)),
                pl.BlockSpec((n, PAIR), lambda i, *_: (0, 0)),
            ],
            scratch_shapes=[pltpu.VMEM((PAIR, 2 * TILE), F32)],
        ),
        out_shape=[
            jax.ShapeDtypeStruct((tokens, PAIR), BF16),
            jax.ShapeDtypeStruct((n, PAIR), F32),
            jax.ShapeDtypeStruct((n, PAIR), F32),
        ],
        input_output_aliases={} if first else {10: 0},
        cost_estimate=pl.CostEstimate(
            flops=10 * steps * 3 * TILE * TILE * 2 * PAIR,
            bytes_accessed=12 * n * PAIR + 10 * steps * TILE * PAIR,
            transcendentals=steps * 3 * TILE * 2 * TILE,
        ),
        name="attend_back",
    )(low, start, q, k, v, do, turned, logs, *(() if first else earlier))


def up_kernel(sn_ref, cot_ref, up_ref, bias_ref, down_ref, out_ref, slope_ref, grad_ref):
    step = pl.program_id(0)
    hidden = nn(sn_ref[...], up_ref[0]) + bias_ref[0]
    square = hidden * hidden
    curve = jnp.tanh(GELU_A * (hidden + GELU_B * (hidden * square)))
    half = 0.5 * (1.0 + curve)
    activated = (hidden * half).astype(BF16)
    slope_ref[...] = half + 0.5 * hidden * (1.0 - curve * curve) * (
        GELU_A * (1.0 + 3.0 * GELU_B * square)
    )
    part = nn(activated, down_ref[...])

    @pl.when(step == 0)
    def _():
        out_ref[...] = part

    @pl.when(step > 0)
    def _():
        out_ref[...] += part

    grad_ref[0] = nn(cot_ref[...], activated).astype(BF16)


def feed_up(sn, cot_turned, up, bias, down):
    rows, width = sn.shape
    parts, _, hid = up.shape
    per = hid // UNIT
    steps = parts * per
    return pl.pallas_call(
        up_kernel,
        grid=(steps,),
        in_specs=[
            pl.BlockSpec((rows, width), lambda i: (0, 0)),
            pl.BlockSpec((width, rows), lambda i: (0, 0)),
            pl.BlockSpec((1, width, UNIT), lambda i: (i // per, 0, i % per)),
            pl.BlockSpec((1, 1, UNIT), lambda i: (i // per, 0, i % per)),
            pl.BlockSpec((UNIT, width), lambda i: (i, 0)),
        ],
        out_specs=[
            pl.BlockSpec((rows, width), lambda i: (0, 0)),
            pl.BlockSpec((rows, UNIT), lambda i: (0, i)),
            pl.BlockSpec((1, width, UNIT), lambda i: (i // per, 0, i % per)),
        ],
        out_shape=[
            jax.ShapeDtypeStruct((rows, width), F32),
            jax.ShapeDtypeStruct((rows, parts * hid), F32),
            jax.ShapeDtypeStruct((parts, width, hid), BF16),
        ],
        cost_estimate=pl.CostEstimate(
            flops=6 * rows * width * parts * hid,
            bytes_accessed=10 * rows * width + 6 * width * parts * hid + 4 * rows * parts * hid,
            transcendentals=rows * parts * hid,
        ),
        name="feed_up",
    )(sn, cot_turned, up, bias, down)


def down_kernel(cot_ref, sn_ref, slope_ref, up_ref, down_ref, back_ref, grad_ref, bias_ref):
    step = pl.program_id(0)
    hidden_back = nt(cot_ref[...], down_ref[...]) * slope_ref[...]
    rounded = hidden_back.astype(BF16)
    bias_ref[0] = jnp.sum(rounded.astype(F32), axis=0, keepdims=True)
    part = nt(rounded, up_ref[0])

    @pl.when(step == 0)
    def _():
        back_ref[...] = part

    @pl.when(step > 0)
    def _():
        back_ref[...] += part

    grad_ref[0] = nn(sn_ref[...], rounded).astype(BF16)


def feed_down(cot, sn_turned, slope, up, down):
    rows, width = cot.shape
    parts, _, hid = up.shape
    per = hid // UNIT
    return pl.pallas_call(
        down_kernel,
        grid=(parts * per,),
        in_specs=[
            pl.BlockSpec((rows, width), lambda i: (0, 0)),
            pl.BlockSpec((width, rows), lambda i: (0, 0)),
            pl.BlockSpec((rows, UNIT), lambda i: (0, i)),
            pl.BlockSpec((1, width, UNIT), lambda i: (i // per, 0, i % per)),
            pl.BlockSpec((UNIT, width), lambda i: (i, 0)),
        ],
        out_specs=[
            pl.BlockSpec((rows, width), lambda i: (0, 0)),
            pl.BlockSpec((1, width, UNIT), lambda i: (i // per, 0, i % per)),
            pl.BlockSpec((1, 1, UNIT), lambda i: (i // per, 0, i % per)),
        ],
        out_shape=[
            jax.ShapeDtypeStruct((rows, width), F32),
            jax.ShapeDtypeStruct((parts, width, hid), BF16),
            jax.ShapeDtypeStruct((parts, 1, hid), F32),
        ],
        cost_estimate=pl.CostEstimate(
            flops=6 * rows * width * parts * hid,
            bytes_accessed=10 * rows * width + 6 * width * parts * hid + 4 * rows * parts * hid,
            transcendentals=0,
        ),
        name="feed_down",
    )(cot, sn_turned, slope, up, down)


def around(value, steps):
    count = lax.axis_size("tp")
    return lax.ppermute(value, "tp", [(i, (i + steps) % count) for i in range(count)])


def flipped(value, axis, bit):
    count = lax.axis_size(axis)
    return lax.ppermute(value, axis, [(i, i ^ bit) for i in range(count)])


def along(value, steps):
    count = lax.axis_size("seq")
    first, last = max(0, -steps), min(count, count - steps)
    return lax.ppermute(value, "seq", [(i, i + steps) for i in range(first, last)])


def summed(value):
    for axis in ("seq", "tp"):
        bit = 1
        while bit < lax.axis_size(axis):
            value = value + flipped(value, axis, bit)
            bit *= 2
    return value


def pick(value, index, dim):
    return lax.dynamic_index_in_dim(value, index, dim, keepdims=False)


def halved(value, place, bit, dim):
    mine = (place // bit) % 2
    sent = pick(value, 1 - mine, dim)
    kept = pick(value, mine, dim)
    return (kept.astype(F32) + flipped(sent, "seq", bit).astype(F32)).astype(BF16)


def seq_bits():
    bits, bit = [], 1
    while bit < lax.axis_size("seq"):
        bits.append(bit)
        bit *= 2
    return bits


def scatter_seq(value, place, bits):
    lead, count, rows, cols = value.shape
    order = sorted(bits, reverse=True)
    left = value.reshape((lead,) + (2,) * len(order) + (rows, cols))
    remaining = list(order)
    for bit in bits:
        dim = 1 + remaining.index(bit)
        left = halved(left, place, bit, dim)
        remaining.remove(bit)
    return left


def scatter_all(value, place, tp_place):
    bits = seq_bits()
    lead = value.shape[0]
    head, tail = bits[0], bits[1:]
    other = tail[1:] + tail[:1]
    first = scatter_seq(value[: lead // 2], place, [head] + tail)
    second = scatter_seq(value[lead // 2 :], place, [head] + other)
    blocks = [first[i] for i in range(lead // 2)] + [second[i] for i in range(lead // 2)]
    total = blocks[0].astype(F32)
    for k in range(1, lead):
        total = total + around(blocks[k], k).astype(F32)
    return total


def rotated(value, tp_place, sign):
    count = value.shape[0]
    return jnp.stack([pick(value, (tp_place + sign * k) % count, 0) for k in range(count)])


def center(rows):
    average = jnp.mean(rows, axis=-1, keepdims=True)
    centered = rows - average
    inverse = lax.rsqrt(jnp.mean(centered * centered, axis=-1, keepdims=True) + EPSILON)
    return centered * inverse, inverse


def norm_back(grad, gain, xhat, inverse):
    e = grad * gain
    return inverse * (
        e
        - jnp.mean(e, axis=-1, keepdims=True)
        - xhat * jnp.mean(e * xhat, axis=-1, keepdims=True)
    )


def local(
    stream, segments, skip_values, first_gain, first_shift, query_weight, query_bias, key_weight,
    value_weight, value_bias, mixing_weight, mixing_bias, second_gain, second_shift, up_weight,
    up_bias, down_weight, down_bias, cotangent,
):
    rows, width = stream.shape
    tokens = skip_values.shape[0]
    own = query_weight.shape[1]
    tp_count = lax.axis_size("tp")
    seq_count = lax.axis_size("seq")
    seq_place = lax.axis_index("seq")
    tp_place = lax.axis_index("tp")
    half = tokens - DOC_MAX

    def share(shard):
        part = shard.shape[0] // seq_count
        mine = lax.dynamic_slice_in_dim(shard, seq_place * part, part, 0)
        return lax.all_gather(mine, ("tp", "seq"), axis=0, tiled=True)

    mixing_full = share(mixing_weight).reshape(tp_count, own, width)
    up_full = share(up_weight).reshape(tp_count, width, up_weight.shape[1])
    down_full = share(down_weight)
    wqkv = jnp.concatenate((query_weight, key_weight, value_weight), axis=1)
    turned_low = jnp.concatenate(
        (query_weight[:, :PAIR], key_weight[:, :PAIR], value_weight), axis=1
    ).T
    turned_high = jnp.concatenate((query_weight[:, PAIR:], key_weight[:, PAIR:]), axis=1).T

    stream_wide = stream.astype(F32)
    first_hat, first_inverse = center(stream_wide)
    piece = (first_hat * first_gain + first_shift).astype(BF16)
    bias = jnp.concatenate((query_bias, jnp.zeros((own,), F32), value_bias))
    qkv = jnp.zeros((tp_count, rows, wqkv.shape[1]), BF16)
    normed = jnp.zeros((tp_count, rows, width), BF16)
    for k in range(tp_count):
        ahead = around(piece, 1) if k < tp_count - 1 else None
        block = (tp_place - k) % tp_count
        projected = (nn(piece, wqkv) + bias).astype(BF16)
        qkv = lax.dynamic_update_index_in_dim(qkv, projected, block, 0)
        normed = lax.dynamic_update_index_in_dim(normed, piece, block, 0)
        piece = ahead
    qkv = qkv.reshape(tokens, wqkv.shape[1])
    normed = normed.reshape(tokens, width)

    padded = jnp.concatenate((jnp.full((DOC_MAX,), -1, jnp.int32), segments))
    window = lax.dynamic_slice_in_dim(padded, seq_place * tokens, DOC_MAX + tokens, 0)
    start = jnp.sum(
        (window[:, None] < window[None, DOC_MAX:]).astype(jnp.int32), axis=0, keepdims=True
    )
    low = start[0, ::TILE] // TILE

    halo_skip = along(skip_values[half:], 1)
    halo = along(qkv[half:, own:], 1)
    skip_early = jnp.concatenate((halo_skip, skip_values[:half]), axis=0)
    early = jnp.concatenate((halo, qkv[:half, own:]), axis=0)
    kcol = own // PAIR

    def values_of(pair):
        if pair == 0:
            return (qkv, 2 * kcol), (early, kcol)
        return (skip_values, 0), (skip_early, 0)

    steps = half // TILE
    attended = []
    for pair in range(2):
        (v, vcol), (ve, vecol) = values_of(pair)
        late = attend(steps, DOC_MAX, low, start, qkv, pair, qkv, kcol + pair, v, vcol, None, tokens)
        attended.append(
            attend(0, 0, low, start, qkv, pair, early, pair, ve, vecol, late, tokens)
        )

    def exchanged(blocks, sign):
        return [pick(blocks, tp_place, 0)] + [
            around(pick(blocks, (tp_place + sign * k) % tp_count, 0), sign * k)
            for k in range(1, tp_count)
        ]

    arrived = [
        exchanged(attended[pair][0].reshape(tp_count, rows, PAIR), 1) for pair in range(2)
    ]
    mixed_in = jnp.concatenate(
        [arrived[pair][k] for k in range(tp_count) for pair in range(2)], axis=1
    )
    mixing_rot = rotated(mixing_full, tp_place, -1).reshape(tp_count * own, width)
    middle = stream_wide + nn(mixed_in, mixing_rot) + mixing_bias
    second_hat, second_inverse = center(middle)
    second = (second_hat * second_gain + second_shift).astype(BF16)

    bias_pieces = [up_bias] + [around(up_bias, k) for k in range(1, tp_count)]
    bias_full = jnp.zeros((tp_count, 1, up_bias.shape[0]), F32)
    for k in range(tp_count):
        bias_full = lax.dynamic_update_index_in_dim(
            bias_full, bias_pieces[k][None], (tp_place - k) % tp_count, 0
        )
    lost, slope, down_grad = feed_up(second, cotangent.T, up_full, bias_full, down_full)
    output = (middle + lost + down_bias).astype(BF16)
    second_back, up_grad, up_bias_grad = feed_down(cotangent, second.T, slope, up_full, down_full)

    def reduced(grad):
        blocks = rotated(grad, tp_place, 1)
        return scatter_all(
            blocks.reshape(tp_count, seq_count, blocks.shape[1] // seq_count, blocks.shape[2]),
            seq_place,
            tp_place,
        )

    down_gradient = reduced(down_grad).T
    up_gradient = reduced(up_grad)

    upstream = cotangent.astype(F32)
    middle_back = upstream + norm_back(second_back, second_gain, second_hat, second_inverse)
    mixing_back = middle_back.astype(BF16)
    attended_back = nt(mixing_back, mixing_rot).astype(BF16).reshape(rows, tp_count, 2, PAIR)
    returned = []
    for pair in range(2):
        pieces = [attended_back[:, k, pair] for k in range(tp_count)]
        full = jnp.zeros((tp_count, rows, PAIR), BF16)
        for k in range(tp_count):
            got = pieces[k] if k == 0 else around(pieces[k], -k)
            full = lax.dynamic_update_index_in_dim(full, got, (tp_place + k) % tp_count, 0)
        returned.append(full.reshape(tokens, PAIR))
    mixing_grad = tn(mixing_back, mixed_in).astype(BF16)
    mixing_grad = mixing_grad.reshape(seq_count, width // seq_count, tp_count, own)
    mixing_grad = mixing_grad.transpose(2, 0, 1, 3)
    mixing_grad = jnp.stack([mixing_grad[-k % tp_count] for k in range(tp_count)])
    mixing_gradient = scatter_all(mixing_grad, seq_place, tp_place).T

    low_full = share(turned_low)
    high_full = share(turned_high)
    shares = [low_full.reshape(tp_count, -1, width), high_full.reshape(tp_count, -1, width)]
    first_back = None
    weight_parts = []
    dq_sum, dv_sum, skip_gradient = [], None, None
    for pair in range(2):
        (v, vcol), (ve, vecol) = values_of(pair)
        _, turned, logs = attended[pair]
        dq_b, dk_b, dv_b = attend_back(
            0, 0, low, start, qkv, pair, early, pair, ve, vecol,
            returned[pair], turned, logs, None, tokens,
        )
        dq, dk_a, dv_a = attend_back(
            steps, DOC_MAX, low, start, qkv, pair, qkv, kcol + pair, v, vcol,
            returned[pair], turned, logs, (dk_b, dv_b, dq_b), tokens,
        )
        gone = jnp.concatenate((dk_b[:DOC_MAX], dv_b[:DOC_MAX]), axis=1).astype(BF16)
        back = along(gone, -1).astype(F32)
        dk = jnp.concatenate((dk_a[:half], dk_a[half:] + back[:, :PAIR]), axis=0).astype(BF16)
        dv = jnp.concatenate((dv_a[:half], dv_a[half:] + back[:, PAIR:]), axis=0)
        grads = [dq, dk]
        dq_sum.append(jnp.sum(dq.astype(F32), axis=0))
        if pair == 0:
            fresh_back = dv.astype(BF16)
            grads.append(fresh_back)
            dv_sum = jnp.sum(fresh_back.astype(F32), axis=0)
        else:
            skip_gradient = dv
        packed = jnp.concatenate(grads, axis=1)
        weight_parts.append(tn(normed, packed).astype(BF16))
        pieces = exchanged(packed.reshape(tp_count, rows, packed.shape[1]), 1)
        weights = rotated(shares[pair], tp_place, -1).reshape(-1, width)
        part = nn(jnp.concatenate(pieces, axis=1), weights)
        first_back = part if first_back is None else first_back + part

    stream_gradient = middle_back + norm_back(first_back, first_gain, first_hat, first_inverse)
    weight_grad = jnp.concatenate(weight_parts, axis=1)
    weight_grad = weight_grad.reshape(1, seq_count, width // seq_count, weight_grad.shape[1])
    weight_grad = scatter_seq(weight_grad, seq_place, seq_bits())[0].astype(F32)
    query_gradient = jnp.concatenate(
        (weight_grad[:, :PAIR], weight_grad[:, 3 * PAIR : 4 * PAIR]), axis=1
    )
    key_gradient = jnp.concatenate(
        (weight_grad[:, PAIR : 2 * PAIR], weight_grad[:, 4 * PAIR :]), axis=1
    )
    value_gradient = weight_grad[:, 2 * PAIR : 3 * PAIR]

    def widen(part):
        size = part.shape[0]
        return lax.dynamic_update_slice_in_dim(
            jnp.zeros((size * tp_count,), F32), part, tp_place * size, 0
        )

    parts = [
        jnp.sum(first_back * first_hat, axis=0),
        jnp.sum(first_back, axis=0),
        jnp.sum(second_back * second_hat, axis=0),
        jnp.sum(second_back, axis=0),
        jnp.sum(middle_back, axis=0),
        jnp.sum(upstream, axis=0),
        widen(jnp.concatenate(dq_sum)),
        widen(dv_sum),
        up_bias_grad.reshape(-1),
    ]
    sums = summed(jnp.concatenate(parts).reshape(-1, PAIR)).reshape(-1)
    cuts, offset = [], 0
    for part in parts:
        cuts.append(sums[offset : offset + part.shape[0]])
        offset += part.shape[0]
    return (
        output,
        stream_gradient,
        skip_gradient,
        query_gradient,
        cuts[6],
        key_gradient,
        value_gradient,
        cuts[7],
        mixing_gradient,
        cuts[4],
        cuts[0],
        cuts[1],
        cuts[2],
        cuts[3],
        up_gradient,
        cuts[8],
        down_gradient,
        cuts[5],
    )


def solution(mesh):
    split = P(("seq", "tp"), None)
    column = P(None, "tp")
    in_specs = (
        split, P(), P("seq", "tp"), P(), P(), column, P("tp"), column, column, P("tp"),
        P("tp", None), P(), P(), P(), column, P("tp"), P("tp", None), P(), split,
    )
    tile = P("seq", "tp")
    out_specs = (
        split, split, tile, tile, P(), tile, tile, P(), P("tp", "seq"), P(), P(), P(), P(), P(),
        tile, P(), P("tp", "seq"), P(),
    )
    return jax.shard_map(local, mesh=mesh, in_specs=in_specs, out_specs=out_specs, check_vma=False)
```

time: 1430 us -> 859 us (0.60)
  waiting for transfers between devices: 999 us -> 384 us
  matrix products: 191 us -> 30.5 us
  Pallas kernels: 0 us -> 116 us
  starting transfers between devices: 6.25 us -> 85.4 us
  local copies, waits for them, and re-layouts: 72.8 us -> 147 us
  blocking collectives: 42.2 us -> 0 us
  other arithmetic: 85.1 us -> 65.8 us
    reduce_scatter x10 -> x0, waiting for transfers between devices: 680 us -> none  [the longest x1 149 us: local(): lax.psum_scatter(jnp.dot(attended, mixing_weight, preferred_element_type=...]
    ppermute x2 -> x63, waiting for transfers between devices: 1.72 us -> 211 us  [the longest x33 126 us: around(): lax.ppermute(value, 'tp', [(i, (i + steps) % count) for i in range(count)])]
    dot_general x49 -> x11, matrix products: 191 us -> 30.5 us  [dot(): return lax.dot_general(a, b, (dims, ((), ())), preferred_element_type=out)]
    all_gather x4 -> x5, waiting for transfers between devices: 317 us -> 173 us  [share(): return lax.all_gather(mine, ('tp', 'seq'), axis=0, tiled=True)]
    pallas_call x0 -> x10, Pallas kernels: none -> 116 us  [the longest x4 38.1 us: attend_back(): pl.pallas_call(functools.partial(attend_back_kernel, base, shift, first),...]
    ppermute x2 -> x63, starting transfers between devices: 4.41 us -> 85.2 us  [the longest x33 63 us: around(): lax.ppermute(value, 'tp', [(i, (i + steps) % count) for i in range(count)])]
    psum x1 -> x0, blocking collectives: 42.2 us -> none  [local(): lax.psum((first_gain_part, first_shift_part, second_gain_part, second_shi...]
    unnamed x102 -> x190, local copies, waits for them, and re-layouts: 10.6 us -> 38.5 us
  transfers between devices with their start and end apart: 16 -> 68, of which waited for: 15 -> 28; matrix products, arithmetic and copies ran while one was open for 6% -> 20% of each run, Pallas kernels for 0% -> 8%
where the time goes in v1:
time: 859 us; the launch traced here: 845 us
  waiting for transfers between devices  384 us (45%)
  local copies, waits for them, and re-layouts  147 us (17%)
  Pallas kernels  116 us (14%)
  starting transfers between devices  85.4 us (10%)
  other arithmetic  65.8 us (8%)
  matrix products  30.5 us (4%)
  between operations  15.8 us (2%)
    all_gather x5, waiting for transfers between devices, share(): return lax.all_gather(mine, ('tp', 'seq'), axis=0, tiled=True)  173 us
    ppermute x33, waiting for transfers between devices, around(): lax.ppermute(value, 'tp', [(i, (i + steps) % count) for i in range(count)])  126 us
    ppermute x26, waiting for transfers between devices, flipped(): return lax.ppermute(value, axis, [(i, i ^ bit) for i in range(count)])  85.1 us
    ppermute x33, starting transfers between devices, around(): lax.ppermute(value, 'tp', [(i, (i + steps) % count) for i in range(count)])  63 us
    dynamic_slice x16, local copies, waits for them, and re-layouts, pick(): return lax.dynamic_index_in_dim(value, index, dim, keepdims=False)  44.4 us
    unnamed x190, local copies, waits for them, and re-layouts  38.5 us
    pallas_call x4, Pallas kernels, attend_back(): pl.pallas_call(functools.partial(attend_back_kernel, base, shift, first),...  38.1 us
    pallas_call x4, Pallas kernels, attend(): pl.pallas_call(functools.partial(attend_kernel, base, shift), grid_spec=p...  31.9 us
  transfers between devices with their start and end apart: 68, of which 28 were waited for; matrix products, arithmetic and copies ran while one was open for 20% of the time, Pallas kernels for 8%

profile of v1, /device:TPU:0, one launch (start us, length us, event | category | flops | bytes accessed | tf_op | source)
XLA Modules:
  0.0 845.0 jit_solution(12045022977020626692)
XLA Ops:
  19.3 3.1 collective-permute-start.11
  35.4 22.7 %collective-permute-done = bf16[512,1024]{0,1:T(8,128)(2,1)} collective-permute-done((bf16[512,1024]{0,1:T(8,128)(2,1)}, bf16[512,1024]{0,1:T(8,128)(2,1)}, u32[]{:S(2)}, u32[]{:S(2)}) %collective-permute-start) | collective-permute-done | bytes 1048608 | tf_op jit(solution)/shard_map/ppermute | solution.py:341
  60.5 3.0 fusion.46
  63.5 26.0 %collective-permute-done.1 = bf16[512,1024]{0,1:T(8,128)(2,1)} collective-permute-done((bf16[512,1024]{0,1:T(8,128)(2,1)}, bf16[512,1024]{0,1:T(8,128)(2,1)}, u32[]{:S(2)}, u32[]{:S(2)}) %collective-permute-start.1) | collective-permute-done | bytes 1048608 | tf_op jit(solution)/shard_map/ppermute | solution.py:341
  91.9 2.8 fusion.44
  97.1 18.6 %collective-permute-done.2 = bf16[512,1024]{0,1:T(8,128)(2,1)} collective-permute-done((bf16[512,1024]{0,1:T(8,128)(2,1)}, bf16[512,1024]{0,1:T(8,128)(2,1)}, u32[]{:S(2)}, u32[]{:S(2)}) %collective-permute-start.2) | collective-permute-done | bytes 1048608 | tf_op jit(solution)/shard_map/ppermute | solution.py:341
  119.0 2.6 collective-permute-start.3
  130.0 9.2 %attend.6 = (bf16[2048,128]{1,0:T(8,128)(2,1)}, f32[128,2048]{1,0:T(8,128)}, f32[8,2048]{1,0:T(8,128)}) custom-call(s32[8]{0:T(128)} %and_select_fusion.low_ref, s32[1,2048]{1,0:T(1,128)} %bitcast.374, bf16[2048,640]{1,0:T(8,128)(2,1)} %bitcast.330, bf16[2048,640]{1,0:T(8,128)(2,1)} %bitcast.331, bf16[2048,128]{1,0:T(8,128)(2,1)} %v_ref.3), custom_call_target="tpu_custom_call" | custom-call | flops 805306368 | bytes 2097152 | tf_op jit(solution)/shard_map/attend/pallas_call | solution.py:109
  139.3 9.2 %attend.4 = (bf16[2048,128]{1,0:T(8,128)(2,1)}, f32[128,2048]{1,0:T(8,128)}, f32[8,2048]{1,0:T(8,128)}) custom-call(s32[8]{0:T(128)} %and_select_fusion.low_ref, s32[1,2048]{1,0:T(1,128)} %bitcast.375, bf16[2048,640]{1,0:T(8,128)(2,1)} %bitcast.332, bf16[2048,640]{1,0:T(8,128)(2,1)} %bitcast.333, bf16[2048,640]{1,0:T(8,128)(2,1)} %bitcast.334), custom_call_target="tpu_custom_call" | custom-call | flops 805306368 | bytes 2097152 | tf_op jit(solution)/shard_map/attend/pallas_call | solution.py:109
  151.9 6.7 attend.5
  160.4 6.7 attend.7
  168.9 4.4 collective-permute-start.7
  192.0 2.6 fusion.100
  200.5 20.1 %all-gather.12.cloned.1.call-done = bf16[1536,1024]{1,0:T(8,128)(2,1)} async-done(((bf16[48,1024]{1,0:T(8,128)(2,1)}), bf16[1536,1024]{1,0:T(8,128)(2,1)}) %all-gather.12.cloned.1.call-update) | async-done | bytes 3145744 | tf_op jit(solution)/shard_map/all_gather | solution.py:447
  224.5 74.5 %all-gather.10.cloned.1.call-done.down_ref = bf16[4096,1024]{1,0:T(8,128)(2,1)} async-done(((bf16[128,1024]{1,0:T(8,128)(2,1)}), bf16[4096,1024]{1,0:T(8,128)(2,1)}) %all-gather.10.cloned.1.call-update) | async-done | bytes 8388624 | tf_op jit(solution)/shard_map/all_gather | solution.py:447
  299.1 78.4 %all-gather.8.cloned.1.call-done = bf16[4096,1024]{1,0:T(8,128)(2,1)} async-done(((bf16[128,1024]{1,0:T(8,128)(2,1)}), bf16[4096,1024]{1,0:T(8,128)(2,1)}) %all-gather.8.cloned.1.call-update) | async-done | bytes 8388624 | tf_op jit(solution)/shard_map/all_gather | solution.py:447
  377.5 24.7 %feed_up.1 = (f32[512,1024]{1,0:T(8,128)}, f32[512,4096]{1,0:T(8,128)}, bf16[4,1024,1024]{2,1,0:T(8,128)(2,1)}) custom-call(bf16[512,1024]{1,0:T(8,128)(2,1)} %copy.159.sn_ref, bf16[1024,512]{1,0:T(8,128)(2,1)} %bitcast.350, bf16[4,1024,1024]{2,1,0:T(8,128)(2,1)} %bitcast.390, f32[4,1,1024]{2,1,0:T(1,128)} %copy-done.66, ...), custom_call_target="tpu_custom_call" | custom-call | flops 12884901888 | bytes 38797312 | tf_op jit(solution)/shard_map/feed_up/pallas_call | solution.py:259
  402.2 21.7 %feed_down.1 = (f32[512,1024]{1,0:T(8,128)}, bf16[4,1024,1024]{2,1,0:T(8,128)(2,1)}, f32[4,1,1024]{2,1,0:T(1,128)}) custom-call(bf16[512,1024]{1,0:T(8,128)(2,1)} %cot_ref.1, bf16[1024,512]{1,0:T(8,128)(2,1)} %fusion.119.sn_ref, f32[512,4096]{1,0:T(8,128)} %get-tuple-element.57.slope_ref, bf16[4,1024,1024]{2,1,0:T(8,128)(2,1)} %bitcast.391, ...), custom_call_target="tpu_custom_call" | custom-call | flops 12884901888 | bytes 38797312 | tf_op jit(solution)/shard_map/feed_down/pallas_call | solution.py:310
  423.9 2.9 copy.162
  426.8 2.9 multiply_reduce_fusion
  429.7 2.9 copy.160
  432.6 4.5 fusion.91
  437.2 4.7 convolution_convert_fusion
  444.9 10.9 %constant_dynamic-slice_fusion.7 = (bf16[1,1024,1024]{2,1,0:T(8,128)(2,1)S(1)}, bf16[1,1024,1024]{2,1,0:T(8,128)(2,1)}, bf16[1,1024,1024]{2,1,0:T(8,128)(2,1)}, ...) fusion(bf16[4,1024,1024]{2,1,0:T(8,128)(2,1)} %get-tuple-elemen, ...), kind=kLoop, calls=%fused_computation.244 | loop fusion | bytes 33554448 | tf_op jit(solution)/shard_map/jit(dynamic_index_in_dim)/dynamic_slice | solution.py:365
  458.0 4.2 copy.193
  469.1 3.9 copy.195
  486.7 3.3 reshape.290
  507.9 2.9 collective-permute-start.21
  511.7 2.9 collective-permute-done.15
  515.5 4.2 collective-permute-start.23
  521.5 8.0 attend_back.4
  529.5 10.8 %attend_back.5 = (bf16[2048,128]{1,0:T(8,128)(2,1)}, f32[2048,128]{1,0:T(8,128)}, f32[2048,128]{1,0:T(8,128)}) custom-call(s32[8]{0:T(128)} %and_select_fusion.low_ref, s32[1,2048]{1,0:T(1,128)} %bitcast.379, bf16[2048,640]{1,0:T(8,128)(2,1)} %bitcast.338, bf16[2048,640]{1,0:T(8,128)(2,1)} %bitcast.339, ...), custom_call_target="tpu_custom_call", output_to_operand_aliasing={{0}: (10, {})} | custom-call | flops 2013265920 | bytes 4456448 | tf_op jit(solution)/shard_map/attend_back/pallas_call | solution.py:203
  551.0 8.0 attend_back.6
  563.7 11.3 %attend_back.7 = (bf16[2048,128]{1,0:T(8,128)(2,1)}, f32[2048,128]{1,0:T(8,128)}, f32[2048,128]{1,0:T(8,128)}) custom-call(s32[8]{0:T(128)} %and_select_fusion.low_ref, s32[1,2048]{1,0:T(1,128)} %bitcast.381, bf16[2048,640]{1,0:T(8,128)(2,1)} %bitcast.342, bf16[2048,640]{1,0:T(8,128)(2,1)} %bitcast.343, ...), custom_call_target="tpu_custom_call", output_to_operand_aliasing={{0}: (10, {})} | custom-call | flops 2013265920 | bytes 4456448 | tf_op jit(solution)/shard_map/attend_back/pallas_call | solution.py:203
  583.8 3.0 collective-permute-start.41
  598.5 3.6 reshape_reshape.3
  602.0 4.2 constant_dynamic-slice_fusion.19
  606.3 3.8 copy.183
  610.0 3.6 copy.214
  614.7 2.6 collective-permute-start.18
  625.1 4.4 collective-permute-done.38
  630.7 3.8 collective-permute-done.42
  634.5 2.7 collective-permute-start.27
  637.3 5.5 collective-permute-done.25
  642.8 19.7 %collective-permute-done.26 = bf16[512,256]{1,0:T(8,128)(2,1)S(1)} collective-permute-done((bf16[512,256]{1,0:T(8,128)(2,1)S(1)}, bf16[512,256]{1,0:T(8,128)(2,1)S(1)}, u32[]{:S(2)}, u32[]{:S(2)}) %collective-permute-start.26) | collective-permute-done | bytes 262176 | tf_op jit(solution)/shard_map/ppermute | solution.py:341
  665.4 12.4 %collective-permute-start.39 = (bf16[128,256]{1,0:T(8,128)(2,1)S(1)}, bf16[128,256]{1,0:T(8,128)(2,1)S(1)}, u32[]{:S(2)}, u32[]{:S(2)}) collective-permute-start(bf16[128,256]{1,0:T(8,128)(2,1)S(1)} %slice_bitcast_fusion.10), channel_id=1, source_target_pairs={{0,1},{1,2},{2,3},{3,0},{4,5},{5,6},{6,7},{7,4},{8,9},{9,10},{10,1... | collective-permute-start | bytes 196616 | tf_op jit(solution)/shard_map/ppermute | solution.py:341
  679.3 4.9 fusion.16
  684.6 3.8 collective-permute-start.43
  689.2 3.5 collective-permute-done.43
  694.2 3.3 collective-permute-done.32
  697.6 4.0 collective-permute-done.33
  702.8 3.0 collective-permute-done.34
  707.2 2.9 fusion.15
  714.5 8.9 %collective-permute-done.29 = bf16[1,2,128,640]{3,2,1,0:T(8,128)(2,1)S(1)} collective-permute-done((bf16[1,2,128,640]{3,2,1,0:T(8,128)(2,1)S(1)}, bf16[1,2,128,640]{3,2,1,0:T(8,128)(2,1)S(1)}, u32[]{:S(2)}, u32[]{:S(2)}) %collective-permute-start.29) | collective-permute-done | bytes 327712 | tf_op jit(solution)/shard_map/ppermute | solution.py:346
  724.2 5.2 collective-permute-done.30
  744.8 14.9 %collective-permute-done.55 = bf16[2,2,128,1024]{2,3,0,1:T(8,128)(2,1)S(1)} collective-permute-done((bf16[2,2,128,1024]{2,3,0,1:T(8,128)(2,1)S(1)}, bf16[2,2,128,1024]{2,3,0,1:T(8,128)(2,1)S(1)}, u32[]{:S(2)}, u32[]{:S(2)}) %collective-permute-start.55) | collective-permute-done | bytes 1048608 | tf_op jit(solution)/shard_map/ppermute | solution.py:346
  760.4 3.0 collective-permute-done.59
  764.4 17.7 %collective-permute-done.46 = bf16[2,2,128,1024]{3,2,0,1:T(8,128)(2,1)S(1)} collective-permute-done((bf16[2,2,128,1024]{3,2,0,1:T(8,128)(2,1)S(1)}, bf16[2,2,128,1024]{3,2,0,1:T(8,128)(2,1)S(1)}, u32[]{:S(2)}, u32[]{:S(2)}) %collective-permute-start.46) | collective-permute-done | bytes 1048608 | tf_op jit(solution)/shard_map/ppermute | solution.py:346
  783.0 2.9 collective-permute-done.50
  787.0 10.1 %collective-permute-done.56 = bf16[2,128,1024]{1,2,0:T(8,128)(2,1)S(1)} collective-permute-done((bf16[2,128,1024]{1,2,0:T(8,128)(2,1)S(1)}, bf16[2,128,1024]{1,2,0:T(8,128)(2,1)S(1)}, u32[]{:S(2)}, u32[]{:S(2)}) %collective-permute-start.56) | collective-permute-done | bytes 524320 | tf_op jit(solution)/shard_map/ppermute | solution.py:346
  802.5 3.7 collective-permute-done.47
  811.7 9.8 %collective-permute-done.61 = bf16[128,1024]{0,1:T(8,128)(2,1)S(1)} collective-permute-done((bf16[128,1024]{0,1:T(8,128)(2,1)S(1)}, bf16[128,1024]{0,1:T(8,128)(2,1)S(1)}, u32[]{:S(2)}, u32[]{:S(2)}) %collective-permute-start.61) | collective-permute-done | bytes 262176 | tf_op jit(solution)/shard_map/ppermute | solution.py:341
  822.4 2.8 collective-permute-done.48
  825.2 12.2 %collective-permute-done.52 = bf16[128,1024]{1,0:T(8,128)(2,1)S(1)} collective-permute-done((bf16[128,1024]{1,0:T(8,128)(2,1)S(1)}, bf16[128,1024]{1,0:T(8,128)(2,1)S(1)}, u32[]{:S(2)}, u32[]{:S(2)}) %collective-permute-start.52) | collective-permute-done | bytes 262176 | tf_op jit(solution)/shard_map/ppermute | solution.py:341
  (470 shorter events, 217.9 us)
Async XLA Ops:
  7.2 171.6 %all-gather.6.cloned.1.call-start = ((), (), s32[]{:S(2)}) async-start(), calls=%async_computation | async-start | bytes 2162688 | tf_op jit(solution)/shard_map/all_gather | solution.py:447
  8.9 171.6 %all-gather.14.cloned.1.call-start = ((), (), s32[]{:S(2)}) async-start(), calls=%async_computation.4 | async-start | bytes 2162688 | tf_op jit(solution)/shard_map/all_gather | solution.py:447
  13.5 207.0 %all-gather.12.cloned.1.call-start = ((), (), s32[]{:S(2)}) async-start(), calls=%async_computation.3 | async-start | bytes 3244032 | tf_op jit(solution)/shard_map/all_gather | solution.py:447
  16.7 282.4 %all-gather.10.cloned.1.call-start = ((), (), s32[]{:S(2)}) async-start(), calls=%async_computation.2 | async-start | bytes 8650752 | tf_op jit(solution)/shard_map/all_gather | solution.py:447
  17.5 360.0 %all-gather.8.cloned.1.call-start = ((), (), s32[]{:S(2)}) async-start(), calls=%async_computation.1 | async-start | bytes 8650752 | tf_op jit(solution)/shard_map/all_gather | solution.py:447
  19.3 72.6 %collective-permute-start.11 = (f32[1024]{0:T(1024)S(1)}, f32[1024]{0:T(1024)S(1)}, u32[]{:S(2)}, u32[]{:S(2)}) collective-permute-start(f32[1024]{0:T(1024)S(1)} %copy-done.73), channel_id=1, source_target_pairs={{0,1},{1,2},{2,3},{3,0},{4,5},{5,6},{6,7},{7,4},{8,9},{9,10},{10,1... | collective-permute-start | bytes 12296 | tf_op jit(solution)/shard_map/ppermute | solution.py:341
  22.4 69.5 %collective-permute-start.12 = (f32[1024]{0:T(1024)S(1)}, f32[1024]{0:T(1024)S(1)}, u32[]{:S(2)}, u32[]{:S(2)}) collective-permute-start(f32[1024]{0:T(1024)S(1)} %copy-done.73), channel_id=1, source_target_pairs={{0,2},{1,3},{2,0},{3,1},{4,6},{5,7},{6,4},{7,5},{8,10},{9,11},{10,... | collective-permute-start | bytes 12296 | tf_op jit(solution)/shard_map/ppermute | solution.py:341
  25.0 66.9 %collective-permute-start.13 = (f32[1024]{0:T(1024)S(1)}, f32[1024]{0:T(1024)S(1)}, u32[]{:S(2)}, u32[]{:S(2)}) collective-permute-start(f32[1024]{0:T(1024)S(1)} %copy-done.73), channel_id=1, source_target_pairs={{0,3},{1,0},{2,1},{3,2},{4,7},{5,4},{6,5},{7,6},{8,11},{9,8},{10,9... | collective-permute-start | bytes 12296 | tf_op jit(solution)/shard_map/ppermute | solution.py:341
  28.9 29.2 %collective-permute-start = (bf16[512,1024]{0,1:T(8,128)(2,1)}, bf16[512,1024]{0,1:T(8,128)(2,1)}, u32[]{:S(2)}, u32[]{:S(2)}) collective-permute-start(bf16[512,1024]{0,1:T(8,128)(2,1)} %fusion.11), channel_id=1, source_target_pairs={{0,1},{1,2},{2,3},{3,0},{4,5},{5,6},{6,7},{7,4},{8,9},{9,10},{10,1... | collective-permute-start | bytes 3145736 | tf_op jit(solution)/shard_map/ppermute | solution.py:341
  30.4 91.2 %collective-permute-start.4 = (bf16[1024,128]{1,0:T(8,128)(2,1)}, bf16[1024,128]{1,0:T(8,128)(2,1)}, u32[]{:S(2)}, u32[]{:S(2)}) collective-permute-start(bf16[1024,128]{1,0:T(8,128)(2,1)} %get-tuple-element.234), channel_id=1, source_target_pairs={{0,4},{4,8},{8,12},{12,16},{16,20},{20,24},{24,28},{1,5},{5,9},{9,... | collective-permute-start | bytes 786440 | tf_op jit(solution)/shard_map/ppermute | solution.py:352
  58.1 31.4 %collective-permute-start.1 = (bf16[512,1024]{0,1:T(8,128)(2,1)}, bf16[512,1024]{0,1:T(8,128)(2,1)}, u32[]{:S(2)}, u32[]{:S(2)}) collective-permute-start(bf16[512,1024]{0,1:T(8,128)(2,1)} %collective-permute-done), channel_id=1, source_target_pairs={{0,1},{1,2},{2,3},{3,0},{4,5},{5,6},{6,7},{7,4},{8,9},{9,10},{10,1... | collective-permute-start | bytes 3145736 | tf_op jit(solution)/shard_map/ppermute | solution.py:341
  89.5 26.1 %collective-permute-start.2 = (bf16[512,1024]{0,1:T(8,128)(2,1)}, bf16[512,1024]{0,1:T(8,128)(2,1)}, u32[]{:S(2)}, u32[]{:S(2)}) collective-permute-start(bf16[512,1024]{0,1:T(8,128)(2,1)} %collective-permute-done.1), channel_id=1, source_target_pairs={{0,1},{1,2},{2,3},{3,0},{4,5},{5,6},{6,7},{7,4},{8,9},{9,10},{10,1... | collective-permute-start | bytes 3145736 | tf_op jit(solution)/shard_map/ppermute | solution.py:341
  119.0 30.5 %collective-permute-start.3 = (bf16[1024,384]{1,0:T(8,128)(2,1)}, bf16[1024,384]{1,0:T(8,128)(2,1)}, u32[]{:S(2)}, u32[]{:S(2)}) collective-permute-start(bf16[1024,384]{1,0:T(8,128)(2,1)} %get-tuple-element.179), channel_id=1, source_target_pairs={{0,4},{4,8},{8,12},{12,16},{16,20},{20,24},{24,28},{1,5},{5,9},{9,... | collective-permute-start | bytes 2359304 | tf_op jit(solution)/shard_map/ppermute | solution.py:352
  160.4 23.7 %collective-permute-start.5 = (bf16[512,128]{1,0:T(8,128)(2,1)}, bf16[512,128]{1,0:T(8,128)(2,1)S(1)}, u32[]{:S(2)}, u32[]{:S(2)}) collective-permute-start(bf16[512,128]{1,0:T(8,128)(2,1)} %get-tuple-element.233), channel_id=1, source_target_pairs={{0,1},{1,2},{2,3},{3,0},{4,5},{5,6},{6,7},{7,4},{8,9},{9,10},{10,1... | collective-permute-start | bytes 393224 | tf_op jit(solution)/shard_map/ppermute | solution.py:341
  168.9 17.9 %collective-permute-start.6 = (bf16[512,128]{1,0:T(8,128)(2,1)}, bf16[512,128]{1,0:T(8,128)(2,1)}, u32[]{:S(2)}, u32[]{:S(2)}) collective-permute-start(bf16[512,128]{1,0:T(8,128)(2,1)} %get-tuple-element.230), channel_id=1, source_target_pairs={{0,1},{1,2},{2,3},{3,0},{4,5},{5,6},{6,7},{7,4},{8,9},{9,10},{10,1... | collective-permute-start | bytes 393224 | tf_op jit(solution)/shard_map/ppermute | solution.py:341
  168.9 19.5 %collective-permute-start.7 = (bf16[512,128]{1,0:T(8,128)(2,1)}, bf16[512,128]{1,0:T(8,128)(2,1)}, u32[]{:S(2)}, u32[]{:S(2)}) collective-permute-start(bf16[512,128]{1,0:T(8,128)(2,1)} %get-tuple-element.232), channel_id=1, source_target_pairs={{0,2},{1,3},{2,0},{3,1},{4,6},{5,7},{6,4},{7,5},{8,10},{9,11},{10,... | collective-permute-start | bytes 393224 | tf_op jit(solution)/shard_map/ppermute | solution.py:341
  173.3 16.6 %collective-permute-start.8 = (bf16[512,128]{1,0:T(8,128)(2,1)}, bf16[512,128]{1,0:T(8,128)(2,1)S(1)}, u32[]{:S(2)}, u32[]{:S(2)}) collective-permute-start(bf16[512,128]{1,0:T(8,128)(2,1)} %get-tuple-element.229), channel_id=1, source_target_pairs={{0,2},{1,3},{2,0},{3,1},{4,6},{5,7},{6,4},{7,5},{8,10},{9,11},{10,... | collective-permute-start | bytes 393224 | tf_op jit(solution)/shard_map/ppermute | solution.py:341
  173.4 17.3 %collective-permute-start.9 = (bf16[512,128]{1,0:T(8,128)(2,1)}, bf16[512,128]{1,0:T(8,128)(2,1)S(1)}, u32[]{:S(2)}, u32[]{:S(2)}) collective-permute-start(bf16[512,128]{1,0:T(8,128)(2,1)} %get-tuple-element.231), channel_id=1, source_target_pairs={{0,3},{1,0},{2,1},{3,2},{4,7},{5,4},{6,5},{7,6},{8,11},{9,8},{10,9... | collective-permute-start | bytes 393224 | tf_op jit(solution)/shard_map/ppermute | solution.py:341
  184.1 7.2 collective-permute-start.10
  491.6 86.0 %collective-permute-start.36 = (bf16[2,2,2,128,256]{4,3,2,1,0:T(8,128)(2,1)}, bf16[2,2,2,128,256]{4,3,2,1,0:T(8,128)(2,1)}, u32[]{:S(2)}, u32[]{:S(2)}) collective-permute-start(bf16[2,2,2,128,256]{4,3,2,1,0:T(8,128)(2,1)} %dynamic-slice_bitcast_fusion.8), channel_id=1, source_target_pairs={{0,4},{4,0},{8,12},{12,8},{16,20},{20,16},{24,28},{28,24},{1,5},{5... | collective-permute-start | bytes 1572872 | tf_op jit(solution)/shard_map/ppermute | solution.py:346
  493.7 88.2 %collective-permute-start.40 = (bf16[2,2,2,128,256]{4,3,0,2,1:T(8,128)(2,1)}, bf16[2,2,2,128,256]{4,3,0,2,1:T(8,128)(2,1)}, u32[]{:S(2)}, u32[]{:S(2)}) collective-permute-start(bf16[2,2,2,128,256]{4,3,0,2,1:T(8,128)(2,1)} %bitcast.322), channel_id=1, source_target_pairs={{0,4},{4,0},{8,12},{12,8},{16,20},{20,16},{24,28},{28,24},{1,5},{5... | collective-permute-start | bytes 1572872 | tf_op jit(solution)/shard_map/ppermute | solution.py:346
  498.7 9.1 %collective-permute-start.14 = (bf16[512,128]{1,0:T(8,128)(2,1)}, bf16[512,128]{1,0:T(8,128)(2,1)}, u32[]{:S(2)}, u32[]{:S(2)}) collective-permute-start(bf16[512,128]{1,0:T(8,128)(2,1)} %bitcast.328), channel_id=1, source_target_pairs={{0,3},{1,0},{2,1},{3,2},{4,7},{5,4},{6,5},{7,6},{8,11},{9,8},{10,9... | collective-permute-start | bytes 393224 | tf_op jit(solution)/shard_map/ppermute | solution.py:341
  501.3 13.3 %collective-permute-start.15 = (bf16[512,128]{1,0:T(8,128)(2,1)}, bf16[512,128]{1,0:T(8,128)(2,1)}, u32[]{:S(2)}, u32[]{:S(2)}) collective-permute-start(bf16[512,128]{1,0:T(8,128)(2,1)} %bitcast.327), channel_id=1, source_target_pairs={{0,2},{1,3},{2,0},{3,1},{4,6},{5,7},{6,4},{7,5},{8,10},{9,11},{10,... | collective-permute-start | bytes 393224 | tf_op jit(solution)/shard_map/ppermute | solution.py:341
  503.0 12.5 %collective-permute-start.16 = (bf16[512,128]{1,0:T(8,128)(2,1)}, bf16[512,128]{1,0:T(8,128)(2,1)}, u32[]{:S(2)}, u32[]{:S(2)}) collective-permute-start(bf16[512,128]{1,0:T(8,128)(2,1)} %bitcast.326), channel_id=1, source_target_pairs={{0,1},{1,2},{2,3},{3,0},{4,5},{5,6},{6,7},{7,4},{8,9},{9,10},{10,1... | collective-permute-start | bytes 393224 | tf_op jit(solution)/shard_map/ppermute | solution.py:341
  507.9 38.3 %collective-permute-start.21 = (bf16[512,128]{1,0:T(8,128)(2,1)}, bf16[512,128]{1,0:T(8,128)(2,1)}, u32[]{:S(2)}, u32[]{:S(2)}) collective-permute-start(bf16[512,128]{1,0:T(8,128)(2,1)} %bitcast.384), channel_id=1, source_target_pairs={{0,3},{1,0},{2,1},{3,2},{4,7},{5,4},{6,5},{7,6},{8,11},{9,8},{10,9... | collective-permute-start | bytes 393224 | tf_op jit(solution)/shard_map/ppermute | solution.py:341
  514.6 33.8 %collective-permute-start.22 = (bf16[512,128]{1,0:T(8,128)(2,1)}, bf16[512,128]{1,0:T(8,128)(2,1)}, u32[]{:S(2)}, u32[]{:S(2)}) collective-permute-start(bf16[512,128]{1,0:T(8,128)(2,1)} %bitcast.324), channel_id=1, source_target_pairs={{0,2},{1,3},{2,0},{3,1},{4,6},{5,7},{6,4},{7,5},{8,10},{9,11},{10,... | collective-permute-start | bytes 393224 | tf_op jit(solution)/shard_map/ppermute | solution.py:341
  515.5 33.8 %collective-permute-start.23 = (bf16[512,128]{1,0:T(8,128)(2,1)S(1)}, bf16[512,128]{1,0:T(8,128)(2,1)}, u32[]{:S(2)}, u32[]{:S(2)}) collective-permute-start(bf16[512,128]{1,0:T(8,128)(2,1)S(1)} %bitcast.383), channel_id=1, source_target_pairs={{0,1},{1,2},{2,3},{3,0},{4,5},{5,6},{6,7},{7,4},{8,9},{9,10},{10,1... | collective-permute-start | bytes 393224 | tf_op jit(solution)/shard_map/ppermute | solution.py:341
  546.1 40.7 %collective-permute-start.17 = (bf16[1024,256]{1,0:T(8,128)(2,1)}, bf16[1024,256]{1,0:T(8,128)(2,1)}, u32[]{:S(2)}, u32[]{:S(2)}) collective-permute-start(bf16[1024,256]{1,0:T(8,128)(2,1)} %pad_maximum_fusion.13), channel_id=1, source_target_pairs={{4,0},{8,4},{12,8},{16,12},{20,16},{24,20},{28,24},{5,1},{9,5},{13... | collective-permute-start | bytes 1572872 | tf_op jit(solution)/shard_map/ppermute | solution.py:352
  562.1 30.5 %collective-permute-start.24 = (bf16[1024,256]{1,0:T(8,128)(2,1)}, bf16[1024,256]{1,0:T(8,128)(2,1)}, u32[]{:S(2)}, u32[]{:S(2)}) collective-permute-start(bf16[1024,256]{1,0:T(8,128)(2,1)} %pad_maximum_fusion.14), channel_id=1, source_target_pairs={{4,0},{8,4},{12,8},{16,12},{20,16},{24,20},{28,24},{5,1},{9,5},{13... | collective-permute-start | bytes 1572872 | tf_op jit(solution)/shard_map/ppermute | solution.py:352
  579.5 41.9 %collective-permute-start.37 = (bf16[2,2,128,256]{3,2,1,0:T(8,128)(2,1)}, bf16[2,2,128,256]{3,2,1,0:T(8,128)(2,1)}, u32[]{:S(2)}, u32[]{:S(2)}) collective-permute-start(bf16[2,2,128,256]{3,2,1,0:T(8,128)(2,1)} %dynamic-slice_bitcast_fusion.15), channel_id=1, source_target_pairs={{0,8},{4,12},{8,0},{12,4},{16,24},{20,28},{24,16},{28,20},{1,9},{5... | collective-permute-start | bytes 786440 | tf_op jit(solution)/shard_map/ppermute | solution.py:346
  583.8 40.0 %collective-permute-start.41 = (bf16[2,2,128,256]{3,2,0,1:T(8,128)(2,1)}, bf16[2,2,128,256]{3,2,0,1:T(8,128)(2,1)}, u32[]{:S(2)}, u32[]{:S(2)}) collective-permute-start(bf16[2,2,128,256]{3,2,0,1:T(8,128)(2,1)} %dynamic-slice_bitcast_fusion.14), channel_id=1, source_target_pairs={{0,16},{4,20},{8,24},{12,28},{16,0},{20,4},{24,8},{28,12},{1,17},{... | collective-permute-start | bytes 786440 | tf_op jit(solution)/shard_map/ppermute | solution.py:346
  614.7 50.7 %collective-permute-start.18 = (bf16[512,384]{1,0:T(8,128)(2,1)}, bf16[512,384]{1,0:T(8,128)(2,1)}, u32[]{:S(2)}, u32[]{:S(2)}) collective-permute-start(bf16[512,384]{1,0:T(8,128)(2,1)} %get-tuple-element.197), channel_id=1, source_target_pairs={{0,1},{1,2},{2,3},{3,0},{4,5},{5,6},{6,7},{7,4},{8,9},{9,10},{10,1... | collective-permute-start | bytes 1179656 | tf_op jit(solution)/shard_map/ppermute | solution.py:341
  617.3 60.5 %collective-permute-start.19 = (bf16[512,384]{1,0:T(8,128)(2,1)}, bf16[512,384]{1,0:T(8,128)(2,1)}, u32[]{:S(2)}, u32[]{:S(2)}) collective-permute-start(bf16[512,384]{1,0:T(8,128)(2,1)} %get-tuple-element.196), channel_id=1, source_target_pairs={{0,2},{1,3},{2,0},{3,1},{4,6},{5,7},{6,4},{7,5},{8,10},{9,11},{10,... | collective-permute-start | bytes 1179656 | tf_op jit(solution)/shard_map/ppermute | solution.py:341
  618.3 24.4 %collective-permute-start.25 = (bf16[512,256]{1,0:T(8,128)(2,1)}, bf16[512,256]{1,0:T(8,128)(2,1)}, u32[]{:S(2)}, u32[]{:S(2)}) collective-permute-start(bf16[512,256]{1,0:T(8,128)(2,1)} %get-tuple-element.219), channel_id=1, source_target_pairs={{0,1},{1,2},{2,3},{3,0},{4,5},{5,6},{6,7},{7,4},{8,9},{9,10},{10,1... | collective-permute-start | bytes 786440 | tf_op jit(solution)/shard_map/ppermute | solution.py:341
  621.4 41.1 %collective-permute-start.26 = (bf16[512,256]{1,0:T(8,128)(2,1)S(1)}, bf16[512,256]{1,0:T(8,128)(2,1)S(1)}, u32[]{:S(2)}, u32[]{:S(2)}) collective-permute-start(bf16[512,256]{1,0:T(8,128)(2,1)S(1)} %copy-done.49), channel_id=1, source_target_pairs={{0,2},{1,3},{2,0},{3,1},{4,6},{5,7},{6,4},{7,5},{8,10},{9,11},{10,... | collective-permute-start | bytes 786440 | tf_op jit(solution)/shard_map/ppermute | solution.py:341
  623.9 5.6 collective-permute-start.38
  629.5 5.0 collective-permute-start.42
  634.5 28.1 %collective-permute-start.27 = (bf16[512,256]{1,0:T(8,128)(2,1)S(1)}, bf16[512,256]{1,0:T(8,128)(2,1)S(1)}, u32[]{:S(2)}, u32[]{:S(2)}) collective-permute-start(bf16[512,256]{1,0:T(8,128)(2,1)S(1)} %copy-done.48), channel_id=1, source_target_pairs={{0,3},{1,0},{2,1},{3,2},{4,7},{5,4},{6,5},{7,6},{8,11},{9,8},{10,9... | collective-permute-start | bytes 786440 | tf_op jit(solution)/shard_map/ppermute | solution.py:341
  642.8 36.5 %collective-permute-start.20 = (bf16[512,384]{1,0:T(8,128)(2,1)S(1)}, bf16[512,384]{1,0:T(8,128)(2,1)S(1)}, u32[]{:S(2)}, u32[]{:S(2)}) collective-permute-start(bf16[512,384]{1,0:T(8,128)(2,1)S(1)} %copy-done.45), channel_id=1, source_target_pairs={{0,3},{1,0},{2,1},{3,2},{4,7},{5,4},{6,5},{7,6},{8,11},{9,8},{10,9... | collective-permute-start | bytes 1179656 | tf_op jit(solution)/shard_map/ppermute | solution.py:341
  662.5 68.9 %collective-permute-start.54 = (bf16[2,2,2,128,1024]{3,4,0,1,2:T(8,128)(2,1)}, bf16[2,2,2,128,1024]{3,4,0,1,2:T(8,128)(2,1)}, u32[]{:S(2)}, u32[]{:S(2)}) collective-permute-start(bf16[2,2,2,128,1024]{3,4,0,1,2:T(8,128)(2,1)} %bitcast.121), channel_id=1, source_target_pairs={{0,4},{4,0},{8,12},{12,8},{16,20},{20,16},{24,28},{28,24},{1,5},{5... | collective-permute-start | bytes 6291464 | tf_op jit(solution)/shard_map/ppermute | solution.py:346
  662.6 71.7 %collective-permute-start.58 = (bf16[2,2,2,128,1024]{3,4,0,2,1:T(8,128)(2,1)}, bf16[2,2,2,128,1024]{3,4,0,2,1:T(8,128)(2,1)}, u32[]{:S(2)}, u32[]{:S(2)}) collective-permute-start(bf16[2,2,2,128,1024]{3,4,0,2,1:T(8,128)(2,1)} %bitcast.130), channel_id=1, source_target_pairs={{0,4},{4,0},{8,12},{12,8},{16,20},{20,16},{24,28},{28,24},{1,5},{5... | collective-permute-start | bytes 6291464 | tf_op jit(solution)/shard_map/ppermute | solution.py:346
  665.4 23.7 %collective-permute-start.39 = (bf16[128,256]{1,0:T(8,128)(2,1)S(1)}, bf16[128,256]{1,0:T(8,128)(2,1)S(1)}, u32[]{:S(2)}, u32[]{:S(2)}) collective-permute-start(bf16[128,256]{1,0:T(8,128)(2,1)S(1)} %slice_bitcast_fusion.10), channel_id=1, source_target_pairs={{0,1},{1,2},{2,3},{3,0},{4,5},{5,6},{6,7},{7,4},{8,9},{9,10},{10,1... | collective-permute-start | bytes 196616 | tf_op jit(solution)/shard_map/ppermute | solution.py:341
  684.6 8.1 collective-permute-start.43
  688.4 5.0 collective-permute-start.44
  689.2 48.5 %collective-permute-start.45 = (bf16[2,2,2,128,1024]{4,3,0,1,2:T(8,128)(2,1)}, bf16[2,2,2,128,1024]{4,3,0,1,2:T(8,128)(2,1)}, u32[]{:S(2)}, u32[]{:S(2)}) collective-permute-start(bf16[2,2,2,128,1024]{4,3,0,1,2:T(8,128)(2,1)} %bitcast.320), channel_id=1, source_target_pairs={{0,4},{4,0},{8,12},{12,8},{16,20},{20,16},{24,28},{28,24},{1,5},{5... | collective-permute-start | bytes 6291464 | tf_op jit(solution)/shard_map/ppermute | solution.py:346
  692.7 19.2 %collective-permute-start.28 = (bf16[1,2,2,128,640]{4,3,1,2,0:T(8,128)(2,1)}, bf16[1,2,2,128,640]{4,3,1,2,0:T(8,128)(2,1)}, u32[]{:S(2)}, u32[]{:S(2)}) collective-permute-start(bf16[1,2,2,128,640]{4,3,1,2,0:T(8,128)(2,1)} %bitcast.64), channel_id=1, source_target_pairs={{0,4},{4,0},{8,12},{12,8},{16,20},{20,16},{24,28},{28,24},{1,5},{5... | collective-permute-start | bytes 1966088 | tf_op jit(solution)/shard_map/ppermute | solution.py:346
  705.8 6.0 collective-permute-start.35
  711.9 30.3 %collective-permute-start.49 = (bf16[2,2,2,128,1024]{4,3,0,2,1:T(8,128)(2,1)}, bf16[2,2,2,128,1024]{4,3,0,2,1:T(8,128)(2,1)S(1)}, u32[]{:S(2)}, u32[]{:S(2)}) collective-permute-start(bf16[2,2,2,128,1024]{4,3,0,2,1:T(8,128)(2,1)} %bitcast.365), channel_id=1, source_target_pairs={{0,4},{4,0},{8,12},{12,8},{16,20},{20,16},{24,28},{28,24},{1,5},{5... | collective-permute-start | bytes 6291464 | tf_op jit(solution)/shard_map/ppermute | solution.py:346
  713.2 10.2 %collective-permute-start.29 = (bf16[1,2,128,640]{3,2,1,0:T(8,128)(2,1)S(1)}, bf16[1,2,128,640]{3,2,1,0:T(8,128)(2,1)S(1)}, u32[]{:S(2)}, u32[]{:S(2)}) collective-permute-start(bf16[1,2,128,640]{3,2,1,0:T(8,128)(2,1)S(1)} %dynamic-slice_bitcast_fusion.13), channel_id=1, source_target_pairs={{0,8},{4,12},{8,0},{12,4},{16,24},{20,28},{24,16},{28,20},{1,9},{5... | collective-permute-start | bytes 983048 | tf_op jit(solution)/shard_map/ppermute | solution.py:346
  723.5 5.8 collective-permute-start.30
  733.6 26.1 %collective-permute-start.55 = (bf16[2,2,128,1024]{2,3,0,1:T(8,128)(2,1)S(1)}, bf16[2,2,128,1024]{2,3,0,1:T(8,128)(2,1)S(1)}, u32[]{:S(2)}, u32[]{:S(2)}) collective-permute-start(bf16[2,2,128,1024]{2,3,0,1:T(8,128)(2,1)S(1)} %dynamic-slice_bitcast_fusion.1), channel_id=1, source_target_pairs={{0,8},{4,12},{8,0},{12,4},{16,24},{20,28},{24,16},{28,20},{1,9},{5... | collective-permute-start | bytes 3145736 | tf_op jit(solution)/shard_map/ppermute | solution.py:346
  737.3 26.1 %collective-permute-start.59 = (bf16[2,2,128,1024]{2,3,0,1:T(8,128)(2,1)S(1)}, bf16[2,2,128,1024]{2,3,0,1:T(8,128)(2,1)S(1)}, u32[]{:S(2)}, u32[]{:S(2)}) collective-permute-start(bf16[2,2,128,1024]{2,3,0,1:T(8,128)(2,1)S(1)} %dynamic-slice_bitcast_fusion), channel_id=1, source_target_pairs={{0,16},{4,20},{8,24},{12,28},{16,0},{20,4},{24,8},{28,12},{1,17},{... | collective-permute-start | bytes 3145736 | tf_op jit(solution)/shard_map/ppermute | solution.py:346
  741.5 40.7 %collective-permute-start.46 = (bf16[2,2,128,1024]{3,2,0,1:T(8,128)(2,1)S(1)}, bf16[2,2,128,1024]{3,2,0,1:T(8,128)(2,1)S(1)}, u32[]{:S(2)}, u32[]{:S(2)}) collective-permute-start(bf16[2,2,128,1024]{3,2,0,1:T(8,128)(2,1)S(1)} %dynamic-slice_bitcast_fusion.3), channel_id=1, source_target_pairs={{0,8},{4,12},{8,0},{12,4},{16,24},{20,28},{24,16},{28,20},{1,9},{5... | collective-permute-start | bytes 3145736 | tf_op jit(solution)/shard_map/ppermute | solution.py:346
  744.1 41.8 %collective-permute-start.50 = (bf16[2,2,128,1024]{3,2,0,1:T(8,128)(2,1)S(1)}, bf16[2,2,128,1024]{3,2,0,1:T(8,128)(2,1)S(1)}, u32[]{:S(2)}, u32[]{:S(2)}) collective-permute-start(bf16[2,2,128,1024]{3,2,0,1:T(8,128)(2,1)S(1)} %dynamic-slice_bitcast_fusion.2), channel_id=1, source_target_pairs={{0,16},{4,20},{8,24},{12,28},{16,0},{20,4},{24,8},{28,12},{1,17},{... | collective-permute-start | bytes 3145736 | tf_op jit(solution)/shard_map/ppermute | solution.py:346
  760.0 37.1 %collective-permute-start.56 = (bf16[2,128,1024]{1,2,0:T(8,128)(2,1)S(1)}, bf16[2,128,1024]{1,2,0:T(8,128)(2,1)S(1)}, u32[]{:S(2)}, u32[]{:S(2)}) collective-permute-start(bf16[2,128,1024]{1,2,0:T(8,128)(2,1)S(1)} %dynamic-slice_bitcast_fusion.5), channel_id=1, source_target_pairs={{0,16},{4,20},{8,24},{12,28},{16,0},{20,4},{24,8},{28,12},{1,17},{... | collective-permute-start | bytes 1572872 | tf_op jit(solution)/shard_map/ppermute | solution.py:346
  763.8 36.1 %collective-permute-start.60 = (bf16[2,128,1024]{1,2,0:T(8,128)(2,1)S(1)}, bf16[2,128,1024]{1,2,0:T(8,128)(2,1)S(1)}, u32[]{:S(2)}, u32[]{:S(2)}) collective-permute-start(bf16[2,128,1024]{1,2,0:T(8,128)(2,1)S(1)} %dynamic-slice_bitcast_fusion.4), channel_id=1, source_target_pairs={{0,8},{4,12},{8,0},{12,4},{16,24},{20,28},{24,16},{28,20},{1,9},{5... | collective-permute-start | bytes 1572872 | tf_op jit(solution)/shard_map/ppermute | solution.py:346
  782.6 23.6 %collective-permute-start.47 = (bf16[2,128,1024]{2,1,0:T(8,128)(2,1)S(1)}, bf16[2,128,1024]{2,1,0:T(8,128)(2,1)S(1)}, u32[]{:S(2)}, u32[]{:S(2)}) collective-permute-start(bf16[2,128,1024]{2,1,0:T(8,128)(2,1)S(1)} %dynamic-slice_bitcast_fusion.7), channel_id=1, source_target_pairs={{0,16},{4,20},{8,24},{12,28},{16,0},{20,4},{24,8},{28,12},{1,17},{... | collective-permute-start | bytes 1572872 | tf_op jit(solution)/shard_map/ppermute | solution.py:346
  786.4 22.6 %collective-permute-start.51 = (bf16[2,128,1024]{2,1,0:T(8,128)(2,1)S(1)}, bf16[2,128,1024]{2,1,0:T(8,128)(2,1)S(1)}, u32[]{:S(2)}, u32[]{:S(2)}) collective-permute-start(bf16[2,128,1024]{2,1,0:T(8,128)(2,1)S(1)} %dynamic-slice_bitcast_fusion.6), channel_id=1, source_target_pairs={{0,8},{4,12},{8,0},{12,4},{16,24},{20,28},{24,16},{28,20},{1,9},{5... | collective-permute-start | bytes 1572872 | tf_op jit(solution)/shard_map/ppermute | solution.py:346
  797.3 12.4 %collective-permute-start.57 = (bf16[128,1024]{0,1:T(8,128)(2,1)S(1)}, bf16[128,1024]{0,1:T(8,128)(2,1)S(1)}, u32[]{:S(2)}, u32[]{:S(2)}) collective-permute-start(bf16[128,1024]{0,1:T(8,128)(2,1)S(1)} %slice_bitcast_fusion.2), channel_id=1, source_target_pairs={{0,1},{1,2},{2,3},{3,0},{4,5},{5,6},{6,7},{7,4},{8,9},{9,10},{10,1... | collective-permute-start | bytes 786440 | tf_op jit(solution)/shard_map/ppermute | solution.py:341
  800.0 21.5 %collective-permute-start.61 = (bf16[128,1024]{0,1:T(8,128)(2,1)S(1)}, bf16[128,1024]{0,1:T(8,128)(2,1)S(1)}, u32[]{:S(2)}, u32[]{:S(2)}) collective-permute-start(bf16[128,1024]{0,1:T(8,128)(2,1)S(1)} %get-tuple-element.220), channel_id=1, source_target_pairs={{0,2},{1,3},{2,0},{3,1},{4,6},{5,7},{6,4},{7,5},{8,10},{9,11},{10,... | collective-permute-start | bytes 786440 | tf_op jit(solution)/shard_map/ppermute | solution.py:341
  800.5 21.0 %collective-permute-start.62 = (bf16[128,1024]{0,1:T(8,128)(2,1)S(1)}, bf16[128,1024]{0,1:T(8,128)(2,1)S(1)}, u32[]{:S(2)}, u32[]{:S(2)}) collective-permute-start(bf16[128,1024]{0,1:T(8,128)(2,1)S(1)} %get-tuple-element.221), channel_id=1, source_target_pairs={{0,3},{1,0},{2,1},{3,2},{4,7},{5,4},{6,5},{7,6},{8,11},{9,8},{10,9... | collective-permute-start | bytes 786440 | tf_op jit(solution)/shard_map/ppermute | solution.py:341
  806.4 18.8 %collective-permute-start.48 = (bf16[128,1024]{1,0:T(8,128)(2,1)S(1)}, bf16[128,1024]{1,0:T(8,128)(2,1)S(1)}, u32[]{:S(2)}, u32[]{:S(2)}) collective-permute-start(bf16[128,1024]{1,0:T(8,128)(2,1)S(1)} %slice_bitcast_fusion.6), channel_id=1, source_target_pairs={{0,1},{1,2},{2,3},{3,0},{4,5},{5,6},{6,7},{7,4},{8,9},{9,10},{10,1... | collective-permute-start | bytes 786440 | tf_op jit(solution)/shard_map/ppermute | solution.py:341
  809.2 28.2 %collective-permute-start.52 = (bf16[128,1024]{1,0:T(8,128)(2,1)S(1)}, bf16[128,1024]{1,0:T(8,128)(2,1)S(1)}, u32[]{:S(2)}, u32[]{:S(2)}) collective-permute-start(bf16[128,1024]{1,0:T(8,128)(2,1)S(1)} %get-tuple-element.222), channel_id=1, source_target_pairs={{0,2},{1,3},{2,0},{3,1},{4,6},{5,7},{6,4},{7,5},{8,10},{9,11},{10,... | collective-permute-start | bytes 786440 | tf_op jit(solution)/shard_map/ppermute | solution.py:341
  809.7 27.7 %collective-permute-start.53 = (bf16[128,1024]{1,0:T(8,128)(2,1)S(1)}, bf16[128,1024]{1,0:T(8,128)(2,1)S(1)}, u32[]{:S(2)}, u32[]{:S(2)}) collective-permute-start(bf16[128,1024]{1,0:T(8,128)(2,1)S(1)} %get-tuple-element.223), channel_id=1, source_target_pairs={{0,3},{1,0},{2,1},{3,2},{4,7},{5,4},{6,5},{7,6},{8,11},{9,8},{10,9... | collective-permute-start | bytes 786440 | tf_op jit(solution)/shard_map/ppermute | solution.py:341
  (81 other events, 666.3 us)
Sparse Core Ops, SparseCore 0:
  10.9 80.2 all-gather.5
  94.0 57.6 all-gather.13
  154.6 65.9 all-gather.11
  223.3 75.7 all-gather.9
  301.8 75.6 all-gather.7

commit v2 on v1

v2 whole, which is shorter than its diff:
```python
import functools

import jax
import jax.numpy as jnp
from jax import lax
from jax.experimental import pallas as pl
from jax.experimental.pallas import tpu as pltpu
from jax.sharding import PartitionSpec as P

HEAD = 64
DOC_MAX = 1024
PAIR = 2 * HEAD
TILE = 256
UNIT = 512
EPSILON = 1e-05
F32 = jnp.float32
BF16 = jnp.bfloat16
SCALE = HEAD ** -0.5
GELU_A = 0.7978845608028654
GELU_B = 0.044715


def dot(a, b, dims, out=F32):
    return lax.dot_general(a, b, (dims, ((), ())), preferred_element_type=out)


def nn(a, b):
    return dot(a, b, ((1,), (0,)))


def nt(a, b):
    return dot(a, b, ((1,), (1,)))


def tn(a, b):
    return dot(a, b, ((0,), (0,)))


def light(bytes_accessed):
    return pl.CostEstimate(flops=1, bytes_accessed=bytes_accessed, transcendentals=0)


ANY = pl.BlockSpec(memory_space=pl.ANY)


def project_kernel(slot, place_ref, piece_ref, weight_ref, bias_ref, *rest):
    qkv_ref, normed_ref = rest[-2:]
    piece = piece_ref[...]
    qkv_ref[...] = (nn(piece, weight_ref[...]) + bias_ref[...]).astype(BF16)
    normed_ref[...] = piece


def project(k, count, place, piece, weight, bias, earlier):
    rows, width = piece.shape
    cols = weight.shape[1]
    slot = (count - k) % count
    tile = rows // 2
    alias = earlier is not None
    return pl.pallas_call(
        functools.partial(project_kernel, slot),
        grid_spec=pltpu.PrefetchScalarGridSpec(
            num_scalar_prefetch=1,
            grid=(2,),
            in_specs=[
                pl.BlockSpec((tile, width), lambda i, p: (i, 0)),
                pl.BlockSpec((width, cols), lambda i, p: (0, 0)),
                pl.BlockSpec((1, cols), lambda i, p: (0, 0)),
            ]
            + ([ANY, ANY] if alias else []),
            out_specs=[
                pl.BlockSpec((tile, cols), lambda i, p: (2 * lax.rem(p[0] + slot, count) + i, 0)),
                pl.BlockSpec((tile, width), lambda i, p: (2 * slot + i, 0)),
            ],
        ),
        out_shape=[
            jax.ShapeDtypeStruct((count * rows, cols), BF16),
            jax.ShapeDtypeStruct((count * rows, width), BF16),
        ],
        input_output_aliases={4: 0, 5: 1} if alias else {},
        cost_estimate=light(4 * rows * width),
        name="project",
    )(place, piece, weight, bias, *(earlier if alias else ()))


def wide(tile):
    lane = lax.broadcasted_iota(jnp.int32, tile.shape, 1)
    zero = jnp.zeros_like(tile)
    return jnp.concatenate(
        (jnp.where(lane < HEAD, tile, zero), jnp.where(lane < HEAD, zero, tile)), axis=0
    )


def both(row):
    return jnp.concatenate((row, row), axis=1)


def heads_of(acc):
    return jnp.concatenate((acc[:HEAD, :TILE], acc[HEAD:, TILE:]), axis=0)


def mask_rows(start_ref, step, shift):
    start = both(start_ref[...] - shift)
    place = both((step + 4) * TILE + lax.broadcasted_iota(jnp.int32, (1, TILE), 1))
    return start, place


def allowed(tile_index, start, place):
    key = tile_index * TILE + lax.broadcasted_iota(jnp.int32, (TILE, 2 * TILE), 0)
    return (key >= start) & (key <= place)


def turn(tile, meta_ref, tiles, per, count):
    block = tile // per
    return per * lax.rem(block - meta_ref[tiles] + count, count) + lax.rem(tile, per)


def attend_kernel(base, shift, meta_ref, start_ref, q_ref, k_ref, v_ref, *rest):
    o_ref, turned_ref, log_ref, acc_ref = rest[-4:]
    step = pl.program_id(0)
    query = wide(q_ref[...] * jnp.asarray(SCALE, BF16))
    start, place = mask_rows(start_ref, step, shift)
    acc_ref[...] = jnp.zeros_like(acc_ref)

    def body(j, carried):
        top, total = carried
        rows = pl.ds(pl.multiple_of(j * TILE, TILE), TILE)
        scores = nt(k_ref[rows, :], query)
        scores = jnp.where(allowed(j, start, place), scores, -1e30)
        new_top = jnp.maximum(top, jnp.max(scores, axis=0, keepdims=True))
        part = jnp.exp(scores - new_top)
        factor = jnp.exp(top - new_top)
        total = total * factor + jnp.sum(part, axis=0, keepdims=True)
        acc_ref[...] = acc_ref[...] * factor + tn(v_ref[rows, :], part.astype(BF16))
        return new_top, total

    top, total = lax.fori_loop(
        meta_ref[base + step] - shift // TILE,
        step + 5,
        body,
        (jnp.full((1, 2 * TILE), -1e30, F32), jnp.zeros((1, 2 * TILE), F32)),
    )
    turned = heads_of(acc_ref[...] / total)
    turned_ref[...] = turned
    o_ref[...] = turned.T.astype(BF16)
    logs = top + jnp.log(total)
    log_ref[0:1, :] = logs[:, :TILE]
    log_ref[1:2, :] = logs[:, TILE:]


def attend(base, shift, meta, start, q, qcol, k, kcol, v, vcol, earlier, tokens, count):
    n = k.shape[0]
    steps = (n - DOC_MAX) // TILE
    tiles = tokens // TILE
    per = tiles // count
    alias = earlier is not None
    specs = [
        pl.BlockSpec((1, TILE), lambda i, m: (0, base + i)),
        pl.BlockSpec((TILE, PAIR), lambda i, m: (base + i, qcol)),
        pl.BlockSpec((n, PAIR), lambda i, m: (0, kcol)),
        pl.BlockSpec((n, PAIR), lambda i, m: (0, vcol)),
    ] + [ANY] * (3 if alias else 0)
    return pl.pallas_call(
        functools.partial(attend_kernel, base, shift),
        grid_spec=pltpu.PrefetchScalarGridSpec(
            num_scalar_prefetch=1,
            grid=(steps,),
            in_specs=specs,
            out_specs=[
                pl.BlockSpec((TILE, PAIR), lambda i, m: (turn(base + i, m, tiles, per, count), 0)),
                pl.BlockSpec((PAIR, TILE), lambda i, m: (0, base + i)),
                pl.BlockSpec((8, TILE), lambda i, m: (0, base + i)),
            ],
            scratch_shapes=[pltpu.VMEM((PAIR, 2 * TILE), F32)],
        ),
        out_shape=[
            jax.ShapeDtypeStruct((tokens, PAIR), BF16),
            jax.ShapeDtypeStruct((PAIR, tokens), F32),
            jax.ShapeDtypeStruct((8, tokens), F32),
        ],
        input_output_aliases={5: 0, 6: 1, 7: 2} if alias else {},
        cost_estimate=light(4 * n * PAIR),
        name="attend",
    )(meta, start, q, k, v, *(earlier if alias else ()))


def back_tile(shift, low, start_ref, q_ref, k_ref, v_ref, do_ref, turned_ref, log_ref, dk_ref, dv_ref, acc_ref):
    step = pl.program_id(0)
    query = wide(q_ref[...] * jnp.asarray(SCALE, BF16))
    out_back = wide(do_ref[...])
    start, place = mask_rows(start_ref, step, shift)
    product = do_ref[...].astype(F32).T * turned_ref[...]
    delta = jnp.concatenate(
        (
            jnp.sum(product[:HEAD], axis=0, keepdims=True),
            jnp.sum(product[HEAD:], axis=0, keepdims=True),
        ),
        axis=1,
    )
    logs = jnp.concatenate((log_ref[0:1, :], log_ref[1:2, :]), axis=1)
    acc_ref[...] = jnp.zeros_like(acc_ref)

    def body(j, carried):
        rows = pl.ds(pl.multiple_of(j * TILE, TILE), TILE)
        key_tile = k_ref[rows, :]
        scores = jnp.where(allowed(j, start, place), nt(key_tile, query), -1e30)
        prob = jnp.exp(scores - logs)
        prob_back = nt(v_ref[rows, :], out_back)
        score_back = (prob * (prob_back - delta)).astype(BF16)
        dv_ref[rows, :] += nn(prob.astype(BF16), out_back)
        dk_ref[rows, :] += nn(score_back, query)
        acc_ref[...] += tn(key_tile, score_back)
        return carried

    lax.fori_loop(low, step + 5, body, 0)
    return (heads_of(acc_ref[...]) * SCALE).T.astype(BF16)


def early_kernel(meta_ref, start_ref, q_ref, k_ref, v_ref, do_ref, turned_ref, log_ref, dq_ref, gone_ref, dk_ref, dv_ref, kept_k, kept_v, acc_ref):
    step = pl.program_id(0)

    @pl.when(step == 0)
    def _():
        kept_k[...] = jnp.zeros_like(kept_k)
        kept_v[...] = jnp.zeros_like(kept_v)

    dq_ref[...] = back_tile(
        0, meta_ref[step], start_ref, q_ref, k_ref, v_ref, do_ref, turned_ref, log_ref,
        kept_k, kept_v, acc_ref,
    )

    @pl.when(step == pl.num_programs(0) - 1)
    def _():
        gone_ref[:, :PAIR] = kept_k[:DOC_MAX, :].astype(BF16)
        gone_ref[:, PAIR:] = kept_v[:DOC_MAX, :].astype(BF16)
        dk_ref[...] = kept_k[DOC_MAX:, :]
        dv_ref[...] = kept_v[DOC_MAX:, :]


def late_kernel(base, fresh, per, count, meta_ref, start_ref, q_ref, k_ref, v_ref, do_ref, turned_ref, log_ref, dq_in, dk_in, dv_in, back_ref, packed_ref, value_ref, sums_ref, kept_k, kept_v, acc_ref):
    step = pl.program_id(0)
    held = dk_in.shape[0]
    tiles = packed_ref.shape[0] // TILE

    def rows_of(tile):
        row = turn(tile, meta_ref, tiles, per, count) * TILE
        return pl.ds(pl.multiple_of(row, TILE), TILE)

    @pl.when(step == 0)
    def _():
        kept_k[:held, :] = dk_in[...]
        kept_v[:held, :] = dv_in[...]
        kept_k[held:, :] = back_ref[:, :PAIR].astype(F32)
        kept_v[held:, :] = back_ref[:, PAIR:].astype(F32)
        for i in range(base):
            packed_ref[rows_of(i), :PAIR] = dq_in[i * TILE : (i + 1) * TILE, :]

    packed_ref[rows_of(base + step), :PAIR] = back_tile(
        DOC_MAX, meta_ref[base + step] - DOC_MAX // TILE, start_ref, q_ref, k_ref, v_ref, do_ref,
        turned_ref, log_ref, kept_k, kept_v, acc_ref,
    )

    @pl.when(step == pl.num_programs(0) - 1)
    def _():
        for i in range(tiles):
            span = slice(i * TILE, (i + 1) * TILE)
            packed_ref[rows_of(i), PAIR : 2 * PAIR] = kept_k[span, :].astype(BF16)
            if fresh:
                packed_ref[rows_of(i), 2 * PAIR :] = kept_v[span, :].astype(BF16)
        if not fresh:
            value_ref[...] = kept_v[...]
        else:
            value_ref[...] = jnp.zeros_like(value_ref)
        sums_ref[...] = jnp.broadcast_to(
            jnp.sum(packed_ref[...].astype(F32), axis=0, keepdims=True), sums_ref.shape
        )


def back_specs(base, qcol, n, kcol, vcol, tiles, per, count):
    return [
        pl.BlockSpec((1, TILE), lambda i, m: (0, base + i)),
        pl.BlockSpec((TILE, PAIR), lambda i, m: (base + i, qcol)),
        pl.BlockSpec((n, PAIR), lambda i, m: (0, kcol)),
        pl.BlockSpec((n, PAIR), lambda i, m: (0, vcol)),
        pl.BlockSpec((TILE, PAIR), lambda i, m: (turn(base + i, m, tiles, per, count), 0)),
        pl.BlockSpec((PAIR, TILE), lambda i, m: (0, base + i)),
        pl.BlockSpec((8, TILE), lambda i, m: (0, base + i)),
    ]


def whole(shape):
    return pl.BlockSpec(shape, lambda i, m: (0,) * len(shape))


def back_early(meta, start, q, qcol, k, kcol, v, vcol, do, turned, logs, tokens, count):
    n = k.shape[0]
    held = n - DOC_MAX
    tiles = tokens // TILE
    return pl.pallas_call(
        early_kernel,
        grid_spec=pltpu.PrefetchScalarGridSpec(
            num_scalar_prefetch=1,
            grid=(held // TILE,),
            in_specs=back_specs(0, qcol, n, kcol, vcol, tiles, tiles // count, count),
            out_specs=[
                pl.BlockSpec((TILE, PAIR), lambda i, m: (i, 0)),
                whole((DOC_MAX, 2 * PAIR)),
                whole((held, PAIR)),
                whole((held, PAIR)),
            ],
            scratch_shapes=[
                pltpu.VMEM((n, PAIR), F32),
                pltpu.VMEM((n, PAIR), F32),
                pltpu.VMEM((PAIR, 2 * TILE), F32),
            ],
        ),
        out_shape=[
            jax.ShapeDtypeStruct((held, PAIR), BF16),
            jax.ShapeDtypeStruct((DOC_MAX, 2 * PAIR), BF16),
            jax.ShapeDtypeStruct((held, PAIR), F32),
            jax.ShapeDtypeStruct((held, PAIR), F32),
        ],
        cost_estimate=light(12 * n * PAIR),
        name="back_early",
    )(meta, start, q, k, v, do, turned, logs)


def back_late(meta, start, q, qcol, k, kcol, v, vcol, do, turned, logs, dq, dk, dv, back, fresh, tokens, count):
    n = k.shape[0]
    held = n - DOC_MAX
    tiles = tokens // TILE
    per = tiles // count
    base = (tokens - held) // TILE
    cols = (3 if fresh else 2) * PAIR
    return pl.pallas_call(
        functools.partial(late_kernel, base, fresh, per, count),
        grid_spec=pltpu.PrefetchScalarGridSpec(
            num_scalar_prefetch=1,
            grid=(held // TILE,),
            in_specs=back_specs(base, qcol, n, kcol, vcol, tiles, per, count)
            + [whole(dq.shape), whole(dk.shape), whole(dv.shape), whole(back.shape)],
            out_specs=[
                whole((tokens, cols)),
                whole((8, PAIR) if fresh else (tokens, PAIR)),
                whole((8, cols)),
            ],
            scratch_shapes=[
                pltpu.VMEM((n, PAIR), F32),
                pltpu.VMEM((n, PAIR), F32),
                pltpu.VMEM((PAIR, 2 * TILE), F32),
            ],
        ),
        out_shape=[
            jax.ShapeDtypeStruct((tokens, cols), BF16),
            jax.ShapeDtypeStruct((8, PAIR) if fresh else (tokens, PAIR), F32),
            jax.ShapeDtypeStruct((8, cols), F32),
        ],
        cost_estimate=light(12 * n * PAIR),
        name="back_late",
    )(meta, start, q, k, v, do, turned, logs, dq, dk, dv, back)


def up_kernel(parts, places_ref, sn_ref, cot_ref, up_ref, bias_ref, down_ref, out_ref, slope_ref, sent_ref, kept_ref):
    step = pl.program_id(0)
    rows = up_ref.shape[0] * up_ref.shape[1]
    hidden = nn(sn_ref[...], up_ref[...].reshape(rows, UNIT)) + bias_ref[0]
    square = hidden * hidden
    curve = jnp.tanh(GELU_A * (hidden + GELU_B * (hidden * square)))
    half = 0.5 * (1.0 + curve)
    activated = (hidden * half).astype(BF16)
    slope_ref[...] = half + 0.5 * hidden * (1.0 - curve * curve) * (
        GELU_A * (1.0 + 3.0 * GELU_B * square)
    )
    part = nn(activated, down_ref[...].reshape(UNIT, rows))

    @pl.when(step == 0)
    def _():
        out_ref[...] = part

    @pl.when(step > 0)
    def _():
        out_ref[...] += part

    grad = nn(cot_ref[...], activated).astype(BF16)
    sent_ref[0] = grad[: rows // 2]
    kept_ref[0] = grad[rows // 2 :]


def feed_specs(gathered, seq, parts, width):
    part = width // seq
    per = width // UNIT

    def spot(i, p):
        return lax.rem(p[0] + i // per, parts)

    return (
        pl.BlockSpec((seq, part, UNIT), lambda i, p: (spot(i, p), 0, lax.rem(i, per))),
        pl.BlockSpec((UNIT // part, part, width), lambda i, p: (spot(i, p) * per + lax.rem(i, per), 1, 0)),
        pl.BlockSpec((1, width // 2, UNIT), lambda i, p: (i // per, 0, lax.rem(i, per))),
        per,
    )


def feed_up(places, sn, cot_turned, gathered, bias, seq, parts):
    rows, width = sn.shape
    up_spec, down_spec, grad_spec, per = feed_specs(gathered, seq, parts, width)
    grad = jax.ShapeDtypeStruct((parts, width // 2, width), BF16)
    return pl.pallas_call(
        functools.partial(up_kernel, parts),
        grid_spec=pltpu.PrefetchScalarGridSpec(
            num_scalar_prefetch=1,
            grid=(parts * per,),
            in_specs=[
                pl.BlockSpec((rows, width), lambda i, p: (0, 0)),
                pl.BlockSpec((width, rows), lambda i, p: (0, 0)),
                up_spec,
                pl.BlockSpec((1, 1, UNIT), lambda i, p: (lax.rem(parts - i // per, parts), 0, lax.rem(i, per))),
                down_spec,
            ],
            out_specs=[
                pl.BlockSpec((rows, width), lambda i, p: (0, 0)),
                pl.BlockSpec((rows, UNIT), lambda i, p: (0, i)),
                grad_spec,
                grad_spec,
            ],
        ),
        out_shape=[
            jax.ShapeDtypeStruct((rows, width), F32),
            jax.ShapeDtypeStruct((rows, parts * width), F32),
            grad,
            grad,
        ],
        cost_estimate=light(16 * rows * width),
        name="feed_up",
    )(places, sn, cot_turned, gathered, bias, gathered)


def down_kernel(seq, places_ref, cot_ref, sn_ref, slope_ref, up_ref, down_ref, back_ref, sent_ref, kept_ref, bias_ref, plain_ref, turned_ref):
    step = pl.program_id(0)
    rows = up_ref.shape[0] * up_ref.shape[1]
    part = rows // seq

    @pl.when(step == 0)
    def _():
        plain_ref[...] = sn_ref[...].T
        for spot, r in enumerate(halves_order(seq)):
            lines = pl.ds(pl.multiple_of(jnp.bitwise_xor(places_ref[1], r) * part, part), part)
            turned_ref[spot * part : (spot + 1) * part, :] = plain_ref[lines, :]

    hidden_back = nt(cot_ref[...], down_ref[...].reshape(UNIT, rows)) * slope_ref[...]
    rounded = hidden_back.astype(BF16)
    bias_ref[0] = jnp.sum(rounded.astype(F32), axis=0, keepdims=True)
    share = nt(rounded, up_ref[...].reshape(rows, UNIT))

    @pl.when(step == 0)
    def _():
        back_ref[...] = share

    @pl.when(step > 0)
    def _():
        back_ref[...] += share

    grad = nn(turned_ref[...], rounded).astype(BF16)
    sent_ref[0] = grad[: rows // 2]
    kept_ref[0] = grad[rows // 2 :]


def feed_down(places, cot, sn, slope, gathered, seq, parts):
    rows, width = cot.shape
    up_spec, down_spec, grad_spec, per = feed_specs(gathered, seq, parts, width)
    grad = jax.ShapeDtypeStruct((parts, width // 2, width), BF16)
    return pl.pallas_call(
        functools.partial(down_kernel, seq),
        grid_spec=pltpu.PrefetchScalarGridSpec(
            num_scalar_prefetch=1,
            grid=(parts * per,),
            in_specs=[
                pl.BlockSpec((rows, width), lambda i, p: (0, 0)),
                pl.BlockSpec((rows, width), lambda i, p: (0, 0)),
                pl.BlockSpec((rows, UNIT), lambda i, p: (0, i)),
                up_spec,
                down_spec,
            ],
            out_specs=[
                pl.BlockSpec((rows, width), lambda i, p: (0, 0)),
                grad_spec,
                grad_spec,
                pl.BlockSpec((1, 1, UNIT), lambda i, p: (i // per, 0, lax.rem(i, per))),
            ],
            scratch_shapes=[pltpu.VMEM((width, rows), BF16)] * 2,
        ),
        out_shape=[
            jax.ShapeDtypeStruct((rows, width), F32),
            grad,
            grad,
            jax.ShapeDtypeStruct((parts, 1, width), F32),
        ],
        cost_estimate=light(16 * rows * width),
        name="feed_down",
    )(places, cot, sn, slope, gathered, gathered)


def around(value, steps):
    count = lax.axis_size("tp")
    return lax.ppermute(value, "tp", [(i, (i + steps) % count) for i in range(count)])


def flipped(value, axis, bit):
    count = lax.axis_size(axis)
    return lax.ppermute(value, axis, [(i, i ^ bit) for i in range(count)])


def along(value, steps):
    count = lax.axis_size("seq")
    first, last = max(0, -steps), min(count, count - steps)
    return lax.ppermute(value, "seq", [(i, i + steps) for i in range(first, last)])


def summed(value):
    for axis in ("seq", "tp"):
        bit = 1
        while bit < lax.axis_size(axis):
            value = value + flipped(value, axis, bit)
            bit *= 2
    return value


def halves_order(seq):
    return list(range(1, seq, 2)) + list(range(0, seq, 2))


def pick(value, index, dim):
    return lax.dynamic_index_in_dim(value, index, dim, keepdims=False)


def joined(a, b):
    return (a.astype(F32) + b.astype(F32)).astype(BF16)


def seq_bits():
    bits, bit = [], 1
    while bit < lax.axis_size("seq"):
        bits.append(bit)
        bit *= 2
    return bits


class Scatter:
    def __init__(self, sent, kept, sign):
        self.sign = sign
        left = list(range(0, lax.axis_size("seq"), 2))
        got = flipped(sent, "seq", 1)
        cut = kept.shape[0] // 2
        tail = seq_bits()[1:]
        self.lanes = [
            (kept[:cut], got[:cut], left, tail),
            (kept[cut:], got[cut:], left, tail[1:] + tail[:1]),
        ]
        self.moves = None

    def merge(self):
        arrays, plans = [], []
        for kept, got, left, bits in self.lanes:
            if not bits:
                arrays.append(joined(kept, got))
                plans.append(None)
                continue
            bit = bits[0]
            goes = [i for i, r in enumerate(left) if r & bit]
            stays = [i for i, r in enumerate(left) if not r & bit]

            def some(array, spots):
                return jnp.concatenate([array[:, i : i + 1] for i in spots], axis=1)

            for spots in (goes, stays):
                arrays.append(joined(some(kept, spots), some(got, spots)))
            plans.append(([left[i] for i in stays], bits))
        self.plans = plans
        return tuple(arrays)

    def send(self, arrays):
        arrays = list(arrays)
        if self.plans[0] is None:
            blocks = [part[i, 0] for part in arrays for i in range(part.shape[0])]
            self.blocks = [blocks[0]] + [
                around(blocks[k], self.sign * k) for k in range(1, len(blocks))
            ]
            self.lanes = None
            return
        lanes = []
        for left, bits in self.plans:
            goes, stays = arrays.pop(0), arrays.pop(0)
            lanes.append((stays, flipped(goes, "seq", bits[0]), left, bits[1:]))
        self.lanes = lanes

    def result(self):
        while self.lanes is not None:
            self.send(self.merge())
        total = self.blocks[0].astype(F32)
        for block in self.blocks[1:]:
            total = total + block.astype(F32)
        return total


def tied(*groups):
    return lax.optimization_barrier(groups)


def scatter_seq(value, place):
    seq = value.shape[0]
    bits = sorted(seq_bits(), reverse=True)
    left = value.reshape((2,) * len(bits) + value.shape[1:])
    for bit in bits:
        mine = (place // bit) % 2
        left = joined(pick(left, mine, 0), flipped(pick(left, 1 - mine, 0), "seq", bit))
    return left


def center(rows):
    average = jnp.mean(rows, axis=-1, keepdims=True)
    centered = rows - average
    inverse = lax.rsqrt(jnp.mean(centered * centered, axis=-1, keepdims=True) + EPSILON)
    return centered * inverse, inverse


def norm_back(grad, gain, xhat, inverse):
    e = grad * gain
    return inverse * (
        e
        - jnp.mean(e, axis=-1, keepdims=True)
        - xhat * jnp.mean(e * xhat, axis=-1, keepdims=True)
    )


def local(
    stream, segments, skip_values, first_gain, first_shift, query_weight, query_bias, key_weight,
    value_weight, value_bias, mixing_weight, mixing_bias, second_gain, second_shift, up_weight,
    up_bias, down_weight, down_bias, cotangent,
):
    rows, width = stream.shape
    tokens = skip_values.shape[0]
    own = query_weight.shape[1]
    tp = lax.axis_size("tp")
    seq = lax.axis_size("seq")
    seq_place = lax.axis_index("seq")
    tp_place = lax.axis_index("tp")
    places = jnp.stack((tp_place, seq_place)).astype(jnp.int32)
    half = tokens - DOC_MAX
    part = width // seq
    kcol = own // PAIR

    stream_wide = stream.astype(F32)
    first_hat, first_inverse = center(stream_wide)
    piece = (first_hat * first_gain + first_shift).astype(BF16)
    piece, up_weight, down_weight, mixing_weight, segments, cotangent = lax.optimization_barrier(
        (piece, up_weight, down_weight, mixing_weight, segments, cotangent)
    )

    def own_rows(shard):
        size = shard.shape[0] // seq
        return lax.dynamic_slice_in_dim(shard, seq_place * size, size, 0)

    packet = jnp.concatenate([own_rows(w) for w in (up_weight, down_weight, mixing_weight)], axis=0)
    gathered = lax.all_gather(packet, ("tp", "seq"), axis=0, tiled=False)
    mixing_full = gathered[:, 2 * part :].reshape(tp, own, width)
    mixing_rot = jnp.concatenate([pick(mixing_full, (tp_place - k) % tp, 0) for k in range(tp)], axis=0)
    qkv_turned = jnp.concatenate(
        (
            query_weight[:, :PAIR], key_weight[:, :PAIR], value_weight,
            query_weight[:, PAIR:], key_weight[:, PAIR:],
        ),
        axis=1,
    ).T
    bias_pieces = jnp.stack([up_bias] + [around(up_bias, k) for k in range(1, tp)])[:, None]

    wqkv = jnp.concatenate((query_weight, key_weight, value_weight), axis=1)
    bias = jnp.concatenate((query_bias, jnp.zeros((own,), F32), value_bias))[None]
    made = None
    for k in range(tp):
        ahead = around(piece, 1) if k < tp - 1 else None
        made = project(k, tp, places, piece, wqkv, bias, made)
        piece = ahead
    qkv, normed = made
    qkv, packet = tied(qkv, own_rows(qkv_turned))
    qkv_full = lax.all_gather(packet, ("tp", "seq"), axis=0, tiled=False).reshape(tp, -1, width)
    shares = [
        jnp.concatenate([pick(part, (tp_place - k) % tp, 0) for k in range(tp)], axis=0)
        for part in (qkv_full[:, : 3 * PAIR], qkv_full[:, 3 * PAIR :])
    ]

    padded = jnp.concatenate((jnp.full((DOC_MAX,), -1, jnp.int32), segments))
    window = lax.dynamic_slice_in_dim(padded, seq_place * tokens, DOC_MAX + tokens, 0)
    start = jnp.sum(
        (window[:, None] < window[None, DOC_MAX:]).astype(jnp.int32), axis=0, keepdims=True
    )
    meta = jnp.concatenate((start[0, ::TILE] // TILE, places))

    halo_skip = along(skip_values[half:], 1)
    halo = along(qkv[half:, own:], 1)
    skip_early = jnp.concatenate((halo_skip, skip_values[:half]), axis=0)
    early = jnp.concatenate((halo, qkv[:half, own:]), axis=0)

    def values_of(pair):
        if pair == 0:
            return (qkv, 2 * kcol), (early, kcol)
        return (skip_values, 0), (skip_early, 0)

    steps = half // TILE
    attended = []
    for pair in range(2):
        (v, vcol), _ = values_of(pair)
        attended.append(
            attend(steps, DOC_MAX, meta, start, qkv, pair, qkv, kcol + pair, v, vcol, None, tokens, tp)
        )
    arrived = []
    for pair in range(2):
        _, (v, vcol) = values_of(pair)
        attended[pair] = attend(
            0, 0, meta, start, qkv, pair, early, pair, v, vcol, attended[pair], tokens, tp
        )
        blocks = attended[pair][0].reshape(tp, rows, PAIR)
        arrived.append([blocks[0]] + [around(blocks[k], k) for k in range(1, tp)])

    mixed_in = jnp.concatenate([arrived[pair][k] for k in range(tp) for pair in range(2)], axis=1)
    middle = stream_wide + nn(mixed_in, mixing_rot) + mixing_bias
    second_hat, second_inverse = center(middle)
    second = (second_hat * second_gain + second_shift).astype(BF16)

    def by_distance(value):
        cut = value.reshape(rows, seq, part)
        return jnp.concatenate([pick(cut, seq_place ^ r, 1) for r in halves_order(seq)], axis=1)

    lost, slope, down_sent, down_kept = feed_up(
        places, second, by_distance(cotangent).T, gathered, bias_pieces, seq, tp
    )
    output = (middle + lost + down_bias).astype(BF16)

    shape = (tp, seq // 2, part, width)
    down_sum = Scatter(down_sent.reshape(shape), down_kept.reshape(shape), 1)
    second_back, up_sent, up_kept, up_bias_grad = feed_down(
        places, cotangent, second, slope, gathered, seq, tp
    )
    up_sum = Scatter(up_sent.reshape(shape), up_kept.reshape(shape), 1)
    second_back, ready = tied(second_back, down_sum.merge())
    down_sum.send(ready)

    upstream = cotangent.astype(F32)
    middle_back = upstream + norm_back(second_back, second_gain, second_hat, second_inverse)
    mixing_back = middle_back.astype(BF16)
    attended_back = nt(mixing_back, mixing_rot).astype(BF16)
    returned = []
    for pair in range(2):
        pieces = [attended_back[:, (2 * k + pair) * PAIR :][:, :PAIR] for k in range(tp)]
        got = [pieces[0]] + [around(pieces[k], -k) for k in range(1, tp)]
        returned.append(jnp.concatenate(got, axis=0))
    mixing_grad = tn(by_distance(mixing_back), mixed_in).astype(BF16)
    mixing_grad = mixing_grad.reshape(seq, part, tp, own).transpose(2, 0, 1, 3)
    mixing_sum = Scatter(mixing_grad[:, : seq // 2], mixing_grad[:, seq // 2 :], -1)

    returned[0], ready_down, ready_up = tied(returned[0], down_sum.merge(), up_sum.merge())
    down_sum.send(ready_down)
    up_sum.send(ready_up)
    halves = []
    for pair in range(2):
        _, (v, vcol) = values_of(pair)
        _, turned, logs = attended[pair]
        dq, gone, dk, dv = back_early(
            meta, start, qkv, pair, early, pair, v, vcol, returned[pair], turned, logs, tokens, tp
        )
        halves.append((dq, dk, dv, along(gone, -1)))
    halves[0], ready_down, ready_mixing = tied(halves[0], down_sum.merge(), mixing_sum.merge())
    down_sum.send(ready_down)
    mixing_sum.send(ready_mixing)
    packets, column_sums, pieces = [], [], []
    skip_gradient = None
    for pair in range(2):
        (v, vcol), _ = values_of(pair)
        _, turned, logs = attended[pair]
        packed, values, sums = back_late(
            meta, start, qkv, pair, qkv, kcol + pair, v, vcol, returned[pair], turned, logs,
            *halves[pair], pair == 0, tokens, tp,
        )
        if pair == 0:
            halves[1], packed, ready_up, ready_mixing = tied(
                halves[1], packed, up_sum.merge(), mixing_sum.merge()
            )
            up_sum.send(ready_up)
            mixing_sum.send(ready_mixing)
        else:
            skip_gradient = values
            packed, sums, ready_up, ready_mixing = tied(
                packed, sums, up_sum.merge(), mixing_sum.merge()
            )
        packets.append(packed)
        column_sums.append(sums[0])
        blocks = packed.reshape(tp, rows, packed.shape[1])
        pieces.append([blocks[0]] + [around(blocks[k], k) for k in range(1, tp)])
    up_sum.send(ready_up)
    mixing_sum.send(ready_mixing)
    first_back = nn(jnp.concatenate(pieces[0], axis=1), shares[0])
    first_back = first_back + nn(jnp.concatenate(pieces[1], axis=1), shares[1])
    down_gradient = down_sum.result().T
    up_gradient = up_sum.result()
    mixing_gradient = mixing_sum.result().T

    stream_gradient = middle_back + norm_back(first_back, first_gain, first_hat, first_inverse)
    wide_grad = jnp.concatenate([tn(normed, packed) for packed in packets], axis=1)
    weight_grad = scatter_seq(
        wide_grad.astype(BF16).reshape(seq, part, wide_grad.shape[1]), seq_place
    ).astype(F32)
    query_gradient = jnp.concatenate(
        (weight_grad[:, :PAIR], weight_grad[:, 3 * PAIR : 4 * PAIR]), axis=1
    )
    key_gradient = jnp.concatenate(
        (weight_grad[:, PAIR : 2 * PAIR], weight_grad[:, 4 * PAIR :]), axis=1
    )
    value_gradient = weight_grad[:, 2 * PAIR : 3 * PAIR]

    column_sum = jnp.concatenate(column_sums)
    columns = qkv_turned.T.astype(F32)
    first_shift_part = jnp.sum(columns * column_sum, axis=1)
    hat_grad = (wide_grad - first_shift[:, None] * column_sum) / first_gain[:, None]
    first_gain_part = jnp.sum(columns * hat_grad, axis=1)

    def widen(value):
        size = value.shape[0]
        return lax.dynamic_update_slice_in_dim(
            jnp.zeros((size * tp,), F32), value, tp_place * size, 0
        )

    def total(parts):
        sums = summed(jnp.concatenate(parts).reshape(-1, PAIR)).reshape(-1)
        cuts, offset = [], 0
        for value in parts:
            cuts.append(sums[offset : offset + value.shape[0]])
            offset += value.shape[0]
        return cuts

    up_bias_grad = up_bias_grad.reshape(tp, width)
    up_bias_grad = jnp.concatenate([pick(up_bias_grad, (k - tp_place) % tp, 0) for k in range(tp)])
    query_part = jnp.concatenate((column_sum[:PAIR], column_sum[3 * PAIR : 4 * PAIR]))
    (
        second_gain_grad, second_shift_grad, mixing_bias_grad, down_bias_grad, up_bias_grad,
        first_gain_grad, first_shift_grad, query_bias_grad, value_bias_grad,
    ) = total(
        [
            jnp.sum(second_back * second_hat, axis=0),
            jnp.sum(second_back, axis=0),
            jnp.sum(middle_back, axis=0),
            jnp.sum(upstream, axis=0),
            up_bias_grad,
            first_gain_part,
            first_shift_part,
            widen(query_part),
            widen(column_sum[2 * PAIR : 3 * PAIR]),
        ]
    )
    return (
        output,
        stream_gradient,
        skip_gradient,
        query_gradient,
        query_bias_grad,
        key_gradient,
        value_gradient,
        value_bias_grad,
        mixing_gradient,
        mixing_bias_grad,
        first_gain_grad,
        first_shift_grad,
        second_gain_grad,
        second_shift_grad,
        up_gradient,
        up_bias_grad,
        down_gradient,
        down_bias_grad,
    )


def solution(mesh):
    split = P(("seq", "tp"), None)
    column = P(None, "tp")
    in_specs = (
        split, P(), P("seq", "tp"), P(), P(), column, P("tp"), column, column, P("tp"),
        P("tp", None), P(), P(), P(), column, P("tp"), P("tp", None), P(), split,
    )
    tile = P("seq", "tp")
    out_specs = (
        split, split, tile, tile, P(), tile, tile, P(), P("tp", "seq"), P(), P(), P(), P(), P(),
        tile, P(), P("tp", "seq"), P(),
    )
    return jax.shard_map(local, mesh=mesh, in_specs=in_specs, out_specs=out_specs, check_vma=False)
```

time: 859 us -> 647 us (0.75)
  waiting for transfers between devices: 384 us -> 188 us
  local copies, waits for them, and re-layouts: 147 us -> 106 us
  starting transfers between devices: 85.4 us -> 119 us
  Pallas kernels: 116 us -> 132 us
  matrix products: 30.5 us -> 16.8 us
    all_gather x5 -> x2, waiting for transfers between devices: 173 us -> 0.02 us  [the longest x1 0.02 us: local(): gathered = lax.all_gather(packet, ('tp', 'seq'), axis=0, tiled=False)]
    dynamic_slice x16 -> x2, local copies, waits for them, and re-layouts: 44.4 us -> 2.17 us  [pick(): return lax.dynamic_index_in_dim(value, index, dim, keepdims=False)]
    ppermute x26 -> x23, waiting for transfers between devices: 85.1 us -> 52.1 us  [flipped(): return lax.ppermute(value, axis, [(i, i ^ bit) for i in range(count)])]
    slice x15 -> x25, local copies, waits for them, and re-layouts: 15.3 us -> 33.8 us  [the longest x6 9.46 us: some(): return jnp.concatenate([array[:, i:i + 1] for i in spots], axis=1)]
    pallas_call x6 -> x10, Pallas kernels: 84.5 us -> 102 us  [the longest x1 25.7 us: feed_up(): pl.pallas_call(functools.partial(up_kernel, parts), grid_spec=pltpu.Prefe...]
    convert_element_type x23 -> x24, other arithmetic: 18.1 us -> 35.7 us  [the longest x23 35.6 us: joined(): return (a.astype(F32) + b.astype(F32)).astype(BF16)]
    ppermute x26 -> x23, starting transfers between devices: 15 us -> 32.5 us  [flipped(): return lax.ppermute(value, axis, [(i, i ^ bit) for i in range(count)])]
    ppermute x33, starting transfers between devices: 63 us -> 77.4 us  [around(): lax.ppermute(value, 'tp', [(i, (i + steps) % count) for i in range(count)])]
  transfers between devices with their start and end apart: 68 -> 62, of which waited for: 28 -> 19; matrix products, arithmetic and copies ran while one was open for 20% -> 26% of each run, Pallas kernels for 8% -> 21%
where the time goes in v2:
time: 647 us; the launch traced here: 637 us
  waiting for transfers between devices  188 us (29%)
  Pallas kernels  132 us (20%)
  starting transfers between devices  119 us (18%)
  local copies, waits for them, and re-layouts  106 us (16%)
  other arithmetic  60.4 us (9%)
  matrix products  16.8 us (3%)
  between operations  16.2 us (3%)
    ppermute x33, waiting for transfers between devices, around(): lax.ppermute(value, 'tp', [(i, (i + steps) % count) for i in range(count)])  136 us
    ppermute x33, starting transfers between devices, around(): lax.ppermute(value, 'tp', [(i, (i + steps) % count) for i in range(count)])  77.4 us
    ppermute x23, waiting for transfers between devices, flipped(): return lax.ppermute(value, axis, [(i, i ^ bit) for i in range(count)])  52.1 us
    unnamed x207, local copies, waits for them, and re-layouts  37 us
    convert_element_type x23, other arithmetic, joined(): return (a.astype(F32) + b.astype(F32)).astype(BF16)  35.6 us
    ppermute x23, starting transfers between devices, flipped(): return lax.ppermute(value, axis, [(i, i ^ bit) for i in range(count)])  32.5 us
    pallas_call x4, Pallas kernels, attend(): pl.pallas_call(functools.partial(attend_kernel, base, shift), grid_spec=p...  29.3 us
    pallas_call x1, Pallas kernels, feed_up(): pl.pallas_call(functools.partial(up_kernel, parts), grid_spec=pltpu.Prefe...  25.7 us
  transfers between devices with their start and end apart: 62, of which 19 were waited for; matrix products, arithmetic and copies ran while one was open for 26% of the time, Pallas kernels for 21%

profile of v2, /device:TPU:0, one launch (start us, length us, event | category | flops | bytes accessed | tf_op | source)
XLA Modules:
  0.0 637.0 jit_solution(18107143925786896477)
XLA Ops:
  13.4 3.1 collective-permute-start
  16.5 38.0 %collective-permute-done.piece_ref = bf16[512,1024]{1,0:T(8,128)(2,1)} collective-permute-done((bf16[512,1024]{1,0:T(8,128)(2,1)S(1)}, bf16[512,1024]{1,0:T(8,128)(2,1)}, u32[]{:S(2)}, u32[]{:S(2)}) %collective-permute-start) | collective-permute-done | bytes 1048608 | tf_op jit(solution)/shard_map/ppermute | solution.py:504
  56.4 43.3 %collective-permute-done.1.piece_ref = bf16[512,1024]{1,0:T(8,128)(2,1)} collective-permute-done((bf16[512,1024]{1,0:T(8,128)(2,1)}, bf16[512,1024]{1,0:T(8,128)(2,1)}, u32[]{:S(2)}, u32[]{:S(2)}) %collective-permute-start.1) | collective-permute-done | bytes 1048608 | tf_op jit(solution)/shard_map/ppermute | solution.py:504
  99.7 3.2 collective-permute-start.2
  106.8 4.6 project.4
  114.1 4.1 project.5
  118.2 4.1 project.6
  122.4 23.0 %collective-permute-done.2.piece_ref = bf16[512,1024]{1,0:T(8,128)(2,1)S(1)} collective-permute-done((bf16[512,1024]{1,0:T(8,128)(2,1)}, bf16[512,1024]{1,0:T(8,128)(2,1)S(1)}, u32[]{:S(2)}, u32[]{:S(2)}) %collective-permute-start.2) | collective-permute-done | bytes 1048608 | tf_op jit(solution)/shard_map/ppermute | solution.py:504
  146.3 4.3 project.7
  151.5 20.4 %collective-permute-start.11 = (f32[1024]{0:T(1024)S(1)}, f32[1024]{0:T(1024)S(1)}, u32[]{:S(2)}, u32[]{:S(2)}) collective-permute-start(f32[1024]{0:T(1024)S(1)} %copy-done.77), channel_id=1, source_target_pairs={{0,1},{1,2},{2,3},{3,0},{4,5},{5,6},{6,7},{7,4},{8,9},{9,10},{10,1... | collective-permute-start | bytes 12296 | tf_op jit(solution)/shard_map/ppermute | solution.py:504
  174.1 2.8 collective-permute-start.13
  179.3 2.5 convert_reduce_fusion
  181.9 2.3 copy.141
  194.9 4.1 collective-permute-start.3
  203.6 7.8 %attend.4 = (bf16[2048,128]{1,0:T(8,128)(2,1)}, f32[128,2048]{1,0:T(8,128)}, f32[8,2048]{1,0:T(8,128)}) custom-call(s32[10]{0:T(128)} %pad_add_fusion.meta_ref, s32[1,2048]{1,0:T(1,128)} %bitcast.224, bf16[2048,640]{1,0:T(8,128)(2,1)} %get-tuple-element.119.q_ref.k_ref.v_ref, bf16[2048,640]{1,0:T(8,128)(2,1)} %get-tuple-element.119.q_ref.k_ref.v_ref, ...), custom_call_target="tpu_custom_call" | custom-call | flops 1 | bytes 1048576 | tf_op jit(solution)/shard_map/attend/pallas_call | solution.py:162
  211.4 7.9 %attend.6 = (bf16[2048,128]{1,0:T(8,128)(2,1)}, f32[128,2048]{1,0:T(8,128)}, f32[8,2048]{1,0:T(8,128)}) custom-call(s32[10]{0:T(128)} %pad_add_fusion.meta_ref, s32[1,2048]{1,0:T(1,128)} %bitcast.225, bf16[2048,640]{1,0:T(8,128)(2,1)} %get-tuple-element.119.q_ref.k_ref.v_ref, bf16[2048,640]{1,0:T(8,128)(2,1)} %get-tuple-element.119.q_ref.k_ref.v_ref, ...), custom_call_target="tpu_custom_call" | custom-call | flops 1 | bytes 1048576 | tf_op jit(solution)/shard_map/attend/pallas_call | solution.py:162
  220.6 6.8 %attend.5 = (bf16[2048,128]{1,0:T(8,128)(2,1)}, f32[128,2048]{1,0:T(8,128)}, f32[8,2048]{1,0:T(8,128)}) custom-call(s32[10]{0:T(128)} %pad_add_fusion.meta_ref, s32[1,2048]{1,0:T(1,128)} %bitcast.226, bf16[2048,640]{1,0:T(8,128)(2,1)} %get-tuple-element.119.q_ref.k_ref.v_ref, ...), custom_call_target="tpu_custom_call", output_to_operand_aliasing={{0}: (5, {}), {1}: (6, {}), {2}: (7, {})} | custom-call | flops 1 | bytes 1048576 | tf_op jit(solution)/shard_map/attend/pallas_call | solution.py:162
  228.8 6.8 %attend.7 = (bf16[2048,128]{1,0:T(8,128)(2,1)}, f32[128,2048]{1,0:T(8,128)}, f32[8,2048]{1,0:T(8,128)}) custom-call(s32[10]{0:T(128)} %pad_add_fusion.meta_ref, s32[1,2048]{1,0:T(1,128)} %bitcast.227, bf16[2048,640]{1,0:T(8,128)(2,1)} %get-tuple-element.119.q_ref.k_ref.v_ref, ...), custom_call_target="tpu_custom_call", output_to_operand_aliasing={{0}: (5, {}), {1}: (6, {}), {2}: (7, {})} | custom-call | flops 1 | bytes 1048576 | tf_op jit(solution)/shard_map/attend/pallas_call | solution.py:162
  237.6 4.3 collective-permute-start.7
  241.9 2.4 collective-permute-start.9
  244.3 2.5 collective-permute-start.10
  246.9 11.8 %collective-permute-done.7 = bf16[512,128]{1,0:T(8,128)(2,1)S(1)} collective-permute-done((bf16[512,128]{1,0:T(8,128)(2,1)S(1)}, bf16[512,128]{1,0:T(8,128)(2,1)S(1)}, u32[]{:S(2)}, u32[]{:S(2)}) %collective-permute-start.7) | collective-permute-done | bytes 131104 | tf_op jit(solution)/shard_map/ppermute | solution.py:504
  258.8 2.8 collective-permute-done.8
  269.9 25.7 %feed_up.1 = (f32[512,1024]{1,0:T(8,128)}, f32[512,4096]{1,0:T(8,128)}, bf16[4,512,1024]{2,1,0:T(8,128)(2,1)}, bf16[4,512,1024]{2,1,0:T(8,128)(2,1)}) custom-call(s32[2]{0:T(128)} %pad_add_fusion.1.place_ref.places_ref, bf16[512,1024]{1,0:T(8,128)(2,1)} %add_convert_fusion.9.sn_ref, bf16[1024,512]{1,0:T(8,128)(2,1)} %bitcast.19.cot_ref, ...), custom_call_target="tpu_custom_call" | custom-call | flops 1 | bytes 8388608 | tf_op jit(solution)/shard_map/feed_up/pallas_call | solution.py:407
  295.6 6.2 copy.126
  309.5 22.7 %feed_down.1 = (f32[512,1024]{1,0:T(8,128)}, bf16[4,512,1024]{2,1,0:T(8,128)(2,1)}, bf16[4,512,1024]{2,1,0:T(8,128)(2,1)}, f32[4,1,1024]{2,1,0:T(1,128)}) custom-call(s32[2]{0:T(128)} %pad_add_fusion.1.place_ref.places_ref, bf16[512,1024]{1,0:T(8,128)(2,1)} %cot_ref, bf16[512,1024]{1,0:T(8,128)(2,1)} %add_convert_fusion.9.sn_ref, ...), custom_call_target="tpu_custom_call" | custom-call | flops 1 | bytes 8388608 | tf_op jit(solution)/shard_map/feed_down/pallas_call | solution.py:471
  332.2 4.0 fusion.83
  339.9 2.4 copy.147
  342.3 2.8 fusion.89
  350.8 4.0 fusion.81
  361.1 3.6 add_convert_fusion.4
  374.7 2.8 reshape.196
  377.5 4.5 copy.139
  382.0 2.3 collective-permute-start.23
  385.2 2.5 convolution_convert_fusion.1
  387.8 5.7 collective-permute-start.19
  400.8 3.9 add_convert_fusion
  412.5 8.3 %back_early.2 = (bf16[1024,128]{1,0:T(8,128)(2,1)}, bf16[1024,256]{1,0:T(8,128)(2,1)}, f32[1024,128]{1,0:T(8,128)}, f32[1024,128]{1,0:T(8,128)}) custom-call(s32[10]{0:T(128)} %pad_add_fusion.meta_ref, s32[1,2048]{1,0:T(1,128)} %bitcast.228, bf16[2048,640]{1,0:T(8,128)(2,1)} %get-tuple-element.119.q_ref.k_ref.v_ref, ...), custom_call_target="tpu_custom_call" | custom-call | flops 1 | bytes 3145728 | tf_op jit(solution)/shard_map/back_early/pallas_call | solution.py:298
  423.5 2.5 add_convert_fusion.20
  426.0 3.7 collective-permute-start.27
  430.5 8.2 %back_early.3 = (bf16[1024,128]{1,0:T(8,128)(2,1)}, bf16[1024,256]{1,0:T(8,128)(2,1)}, f32[1024,128]{1,0:T(8,128)}, f32[1024,128]{1,0:T(8,128)}) custom-call(s32[10]{0:T(128)} %pad_add_fusion.meta_ref, s32[1,2048]{1,0:T(1,128)} %bitcast.229, bf16[2048,640]{1,0:T(8,128)(2,1)} %get-tuple-element.119.q_ref.k_ref.v_ref, ...), custom_call_target="tpu_custom_call" | custom-call | flops 1 | bytes 3145728 | tf_op jit(solution)/shard_map/back_early/pallas_call | solution.py:298
  439.9 4.4 collective-permute-start.30
  457.9 10.0 %back_late.2 = (bf16[2048,384]{1,0:T(8,128)(2,1)}, f32[8,128]{1,0:T(8,128)}, f32[8,384]{1,0:T(8,128)}) custom-call(s32[10]{0:T(128)} %pad_add_fusion.meta_ref, s32[1,2048]{1,0:T(1,128)} %bitcast.230, bf16[2048,640]{1,0:T(8,128)(2,1)} %get-tuple-element.119.q_ref.k_ref.v_ref, bf16[2048,640]{1,0:T(8,128)(2,1)} %get-tuple-element.119.q_ref.k_ref.v_ref, ...), custom_call_target="tpu_custom_call" | custom-call | flops 1 | bytes 3145728 | tf_op jit(solution)/shard_map/back_late/pallas_call | solution.py:334
  474.1 3.7 collective-permute-start.59
  483.9 2.9 collective-permute-done.58
  488.5 4.2 collective-permute-done.57
  493.7 2.7 add_convert_fusion.12
  496.4 2.8 add_convert_fusion.14
  499.2 6.5 %collective-permute-start.39 = (bf16[2,1,128,256]{2,3,1,0:T(8,128)(2,1)}, bf16[2,1,128,256]{2,3,1,0:T(8,128)(2,1)S(1)}, u32[]{:S(2)}, u32[]{:S(2)}) collective-permute-start(bf16[2,1,128,256]{2,3,1,0:T(8,128)(2,1)} %get-tuple-element.189), channel_id=1, source_target_pairs={{0,8},{4,12},{8,0},{12,4},{16,24},{20,28},{24,16},{28,20},{1,9},{5... | collective-permute-start | bytes 393224 | tf_op jit(solution)/shard_map/ppermute | solution.py:509
  507.8 3.5 fusion.99
  514.1 10.2 %back_late.3 = (bf16[2048,256]{1,0:T(8,128)(2,1)}, f32[2048,128]{1,0:T(8,128)}, f32[8,256]{1,0:T(8,128)}) custom-call(s32[10]{0:T(128)} %pad_add_fusion.meta_ref, s32[1,2048]{1,0:T(1,128)} %bitcast.231, bf16[2048,640]{1,0:T(8,128)(2,1)} %get-tuple-element.119.q_ref.k_ref.v_ref, bf16[2048,640]{1,0:T(8,128)(2,1)} %get-tuple-element.119.q_ref.k_ref.v_ref, ...), custom_call_target="tpu_custom_call" | custom-call | flops 1 | bytes 3145728 | tf_op jit(solution)/shard_map/back_late/pallas_call | solution.py:334
  528.6 3.5 fusion.100
  536.9 3.4 collective-permute-start.47
  540.4 2.4 collective-permute-start.52
  544.3 2.4 collective-permute-start.51
  548.6 4.0 collective-permute-done.49
  555.7 2.9 collective-permute-start.50
  559.2 29.9 %collective-permute-done.50 = f32[92,128]{1,0:T(8,128)S(1)} collective-permute-done((f32[92,128]{1,0:T(8,128)S(1)}, f32[92,128]{1,0:T(8,128)S(1)}, u32[]{:S(2)}, u32[]{:S(2)}) %collective-permute-start.50) | collective-permute-done | bytes 47136 | tf_op jit(solution)/shard_map/ppermute | solution.py:509
  594.4 3.9 collective-permute-done.42
  598.3 4.1 collective-permute-start.56
  604.7 3.7 collective-permute-done.35
  608.5 3.2 fusion.79
  611.7 7.0 %collective-permute-done.43 = bf16[2,2,128,640]{3,2,1,0:T(8,128)(2,1)S(1)} collective-permute-done((bf16[2,2,128,640]{3,2,1,0:T(8,128)(2,1)S(1)}, bf16[2,2,128,640]{3,2,1,0:T(8,128)(2,1)S(1)}, u32[]{:S(2)}, u32[]{:S(2)}) %collective-permute-start.43) | collective-permute-done | bytes 655392 | tf_op jit(solution)/shard_map/ppermute | solution.py:509
  621.6 4.4 collective-permute-done.44
  (419 shorter events, 166.5 us)
Async XLA Ops:
  7.2 254.5 %all-gather.5.cloned.1.call-start = ((), (), s32[]{:S(2)}) async-start(), calls=%async_computation | async-start | bytes 19464192 | tf_op jit(solution)/shard_map/all_gather | solution.py:663
  12.5 91.0 %copy-start.25 = (bf16[1024,256]{1,0:T(8,128)(2,1)S(1)}, bf16[1024,256]{1,0:T(8,128)(2,1)}, u32[]{:S(2)}) copy-start(bf16[1024,256]{1,0:T(8,128)(2,1)} %param.26) | copy-start | bytes 1572868
  13.4 289.0 %all-gather.7.cloned.1.call-start = ((), (), s32[]{:S(2)}) async-start(), calls=%async_computation.1 | async-start | bytes 5406720 | tf_op jit(solution)/shard_map/all_gather | solution.py:684
  13.4 41.1 %collective-permute-start = (bf16[512,1024]{1,0:T(8,128)(2,1)S(1)}, bf16[512,1024]{1,0:T(8,128)(2,1)}, u32[]{:S(2)}, u32[]{:S(2)}) collective-permute-start(bf16[512,1024]{1,0:T(8,128)(2,1)S(1)} %fusion.17.piece_ref), channel_id=1, source_target_pairs={{0,1},{1,2},{2,3},{3,0},{4,5},{5,6},{6,7},{7,4},{8,9},{9,10},{10,1... | collective-permute-start | bytes 3145736 | tf_op jit(solution)/shard_map/ppermute | solution.py:504
  54.6 45.1 %collective-permute-start.1 = (bf16[512,1024]{1,0:T(8,128)(2,1)}, bf16[512,1024]{1,0:T(8,128)(2,1)}, u32[]{:S(2)}, u32[]{:S(2)}) collective-permute-start(bf16[512,1024]{1,0:T(8,128)(2,1)} %collective-permute-done.piece_ref), channel_id=1, source_target_pairs={{0,1},{1,2},{2,3},{3,0},{4,5},{5,6},{6,7},{7,4},{8,9},{9,10},{10,1... | collective-permute-start | bytes 3145736 | tf_op jit(solution)/shard_map/ppermute | solution.py:504
  99.7 45.6 %collective-permute-start.2 = (bf16[512,1024]{1,0:T(8,128)(2,1)}, bf16[512,1024]{1,0:T(8,128)(2,1)S(1)}, u32[]{:S(2)}, u32[]{:S(2)}) collective-permute-start(bf16[512,1024]{1,0:T(8,128)(2,1)} %collective-permute-done.1.piece_ref), channel_id=1, source_target_pairs={{0,1},{1,2},{2,3},{3,0},{4,5},{5,6},{6,7},{7,4},{8,9},{9,10},{10,1... | collective-permute-start | bytes 3145736 | tf_op jit(solution)/shard_map/ppermute | solution.py:504
  151.5 85.4 %collective-permute-start.11 = (f32[1024]{0:T(1024)S(1)}, f32[1024]{0:T(1024)S(1)}, u32[]{:S(2)}, u32[]{:S(2)}) collective-permute-start(f32[1024]{0:T(1024)S(1)} %copy-done.77), channel_id=1, source_target_pairs={{0,1},{1,2},{2,3},{3,0},{4,5},{5,6},{6,7},{7,4},{8,9},{9,10},{10,1... | collective-permute-start | bytes 12296 | tf_op jit(solution)/shard_map/ppermute | solution.py:504
  171.9 65.0 %collective-permute-start.12 = (f32[1024]{0:T(1024)S(1)}, f32[1024]{0:T(1024)S(1)}, u32[]{:S(2)}, u32[]{:S(2)}) collective-permute-start(f32[1024]{0:T(1024)S(1)} %copy-done.77), channel_id=1, source_target_pairs={{0,2},{1,3},{2,0},{3,1},{4,6},{5,7},{6,4},{7,5},{8,10},{9,11},{10,... | collective-permute-start | bytes 12296 | tf_op jit(solution)/shard_map/ppermute | solution.py:504
  174.1 62.8 %collective-permute-start.13 = (f32[1024]{0:T(1024)S(1)}, f32[1024]{0:T(1024)S(1)}, u32[]{:S(2)}, u32[]{:S(2)}) collective-permute-start(f32[1024]{0:T(1024)S(1)} %copy-done.77), channel_id=1, source_target_pairs={{0,3},{1,0},{2,1},{3,2},{4,7},{5,4},{6,5},{7,6},{8,11},{9,8},{10,9... | collective-permute-start | bytes 12296 | tf_op jit(solution)/shard_map/ppermute | solution.py:504
  177.7 25.1 %collective-permute-start.4 = (bf16[1024,128]{1,0:T(8,128)(2,1)}, bf16[1024,128]{1,0:T(8,128)(2,1)S(1)}, u32[]{:S(2)}, u32[]{:S(2)}) collective-permute-start(bf16[1024,128]{1,0:T(8,128)(2,1)} %get-tuple-element.312), channel_id=1, source_target_pairs={{0,4},{4,8},{8,12},{12,16},{16,20},{20,24},{24,28},{1,5},{5,9},{9,... | collective-permute-start | bytes 786440 | tf_op jit(solution)/shard_map/ppermute | solution.py:515
  194.9 24.4 %collective-permute-start.3 = (bf16[1024,384]{1,0:T(8,128)(2,1)}, bf16[1024,384]{1,0:T(8,128)(2,1)S(1)}, u32[]{:S(2)}, u32[]{:S(2)}) collective-permute-start(bf16[1024,384]{1,0:T(8,128)(2,1)} %get-tuple-element.234), channel_id=1, source_target_pairs={{0,4},{4,8},{8,12},{12,16},{16,20},{20,24},{24,28},{1,5},{5,9},{9,... | collective-permute-start | bytes 2359304 | tf_op jit(solution)/shard_map/ppermute | solution.py:515
  228.8 15.5 %collective-permute-start.5 = (bf16[512,128]{1,0:T(8,128)(2,1)S(1)}, bf16[512,128]{1,0:T(8,128)(2,1)S(1)}, u32[]{:S(2)}, u32[]{:S(2)}) collective-permute-start(bf16[512,128]{1,0:T(8,128)(2,1)S(1)} %get-tuple-element.310), channel_id=1, source_target_pairs={{0,1},{1,2},{2,3},{3,0},{4,5},{5,6},{6,7},{7,4},{8,9},{9,10},{10,1... | collective-permute-start | bytes 393224 | tf_op jit(solution)/shard_map/ppermute | solution.py:504
  236.8 10.0 %collective-permute-start.6 = (bf16[512,128]{1,0:T(8,128)(2,1)S(1)}, bf16[512,128]{1,0:T(8,128)(2,1)S(1)}, u32[]{:S(2)}, u32[]{:S(2)}) collective-permute-start(bf16[512,128]{1,0:T(8,128)(2,1)S(1)} %get-tuple-element.306), channel_id=1, source_target_pairs={{0,1},{1,2},{2,3},{3,0},{4,5},{5,6},{6,7},{7,4},{8,9},{9,10},{10,1... | collective-permute-start | bytes 393224 | tf_op jit(solution)/shard_map/ppermute | solution.py:504
  237.6 21.2 %collective-permute-start.7 = (bf16[512,128]{1,0:T(8,128)(2,1)S(1)}, bf16[512,128]{1,0:T(8,128)(2,1)S(1)}, u32[]{:S(2)}, u32[]{:S(2)}) collective-permute-start(bf16[512,128]{1,0:T(8,128)(2,1)S(1)} %get-tuple-element.309), channel_id=1, source_target_pairs={{0,2},{1,3},{2,0},{3,1},{4,6},{5,7},{6,4},{7,5},{8,10},{9,11},{10,... | collective-permute-start | bytes 393224 | tf_op jit(solution)/shard_map/ppermute | solution.py:504
  241.9 19.7 %collective-permute-start.8 = (bf16[512,128]{1,0:T(8,128)(2,1)S(1)}, bf16[512,128]{1,0:T(8,128)(2,1)S(1)}, u32[]{:S(2)}, u32[]{:S(2)}) collective-permute-start(bf16[512,128]{1,0:T(8,128)(2,1)S(1)} %get-tuple-element.305), channel_id=1, source_target_pairs={{0,2},{1,3},{2,0},{3,1},{4,6},{5,7},{6,4},{7,5},{8,10},{9,11},{10,... | collective-permute-start | bytes 393224 | tf_op jit(solution)/shard_map/ppermute | solution.py:504
  241.9 19.7 %collective-permute-start.9 = (bf16[512,128]{1,0:T(8,128)(2,1)S(1)}, bf16[512,128]{1,0:T(8,128)(2,1)S(1)}, u32[]{:S(2)}, u32[]{:S(2)}) collective-permute-start(bf16[512,128]{1,0:T(8,128)(2,1)S(1)} %get-tuple-element.308), channel_id=1, source_target_pairs={{0,3},{1,0},{2,1},{3,2},{4,7},{5,4},{6,5},{7,6},{8,11},{9,8},{10,9... | collective-permute-start | bytes 393224 | tf_op jit(solution)/shard_map/ppermute | solution.py:504
  244.3 17.4 %collective-permute-start.10 = (bf16[512,128]{1,0:T(8,128)(2,1)S(1)}, bf16[512,128]{1,0:T(8,128)(2,1)S(1)}, u32[]{:S(2)}, u32[]{:S(2)}) collective-permute-start(bf16[512,128]{1,0:T(8,128)(2,1)S(1)} %get-tuple-element.304), channel_id=1, source_target_pairs={{0,3},{1,0},{2,1},{3,2},{4,7},{5,4},{6,5},{7,6},{8,11},{9,8},{10,9... | collective-permute-start | bytes 393224 | tf_op jit(solution)/shard_map/ppermute | solution.py:504
  301.8 54.3 %collective-permute-start.14 = (bf16[4,4,128,1024]{2,3,1,0:T(8,128)(2,1)}, bf16[4,4,128,1024]{2,3,1,0:T(8,128)(2,1)}, u32[]{:S(2)}, u32[]{:S(2)}) collective-permute-start(bf16[4,4,128,1024]{2,3,1,0:T(8,128)(2,1)} %copy.126), channel_id=1, source_target_pairs={{0,4},{4,0},{8,12},{12,8},{16,20},{20,16},{24,28},{28,24},{1,5},{5... | collective-permute-start | bytes 12582920 | tf_op jit(solution)/shard_map/ppermute | solution.py:509
  350.8 43.7 %collective-permute-start.24 = (bf16[4,4,128,1024]{3,2,1,0:T(8,128)(2,1)}, bf16[4,4,128,1024]{3,2,1,0:T(8,128)(2,1)}, u32[]{:S(2)}, u32[]{:S(2)}) collective-permute-start(bf16[4,4,128,1024]{3,2,1,0:T(8,128)(2,1)} %bitcast.242), channel_id=1, source_target_pairs={{0,4},{4,0},{8,12},{12,8},{16,20},{20,16},{24,28},{28,24},{1,5},{5... | collective-permute-start | bytes 12582920 | tf_op jit(solution)/shard_map/ppermute | solution.py:509
  382.0 39.7 %collective-permute-start.23 = (bf16[2,2,128,1024]{2,3,1,0:T(8,128)(2,1)}, bf16[2,2,128,1024]{2,3,1,0:T(8,128)(2,1)}, u32[]{:S(2)}, u32[]{:S(2)}) collective-permute-start(bf16[2,2,128,1024]{2,3,1,0:T(8,128)(2,1)} %get-tuple-element.147), channel_id=1, source_target_pairs={{0,16},{4,20},{8,24},{12,28},{16,0},{20,4},{24,8},{28,12},{1,17},{... | collective-permute-start | bytes 3145736 | tf_op jit(solution)/shard_map/ppermute | solution.py:509
  384.3 39.2 %collective-permute-start.22 = (bf16[2,2,128,1024]{2,3,1,0:T(8,128)(2,1)}, bf16[2,2,128,1024]{2,3,1,0:T(8,128)(2,1)}, u32[]{:S(2)}, u32[]{:S(2)}) collective-permute-start(bf16[2,2,128,1024]{2,3,1,0:T(8,128)(2,1)} %add_convert_fusion.7), channel_id=1, source_target_pairs={{0,8},{4,12},{8,0},{12,4},{16,24},{20,28},{24,16},{28,20},{1,9},{5... | collective-permute-start | bytes 3145736 | tf_op jit(solution)/shard_map/ppermute | solution.py:509
  387.8 16.9 %collective-permute-start.19 = (bf16[512,128]{1,0:T(8,128)(2,1)S(1)}, bf16[512,128]{1,0:T(8,128)(2,1)S(1)}, u32[]{:S(2)}, u32[]{:S(2)}) collective-permute-start(bf16[512,128]{1,0:T(8,128)(2,1)S(1)} %get-tuple-element.291), channel_id=1, source_target_pairs={{0,3},{1,0},{2,1},{3,2},{4,7},{5,4},{6,5},{7,6},{8,11},{9,8},{10,9... | collective-permute-start | bytes 393224 | tf_op jit(solution)/shard_map/ppermute | solution.py:504
  393.5 14.3 %collective-permute-start.15 = (bf16[512,128]{1,0:T(8,128)(2,1)S(1)}, bf16[512,128]{1,0:T(8,128)(2,1)S(1)}, u32[]{:S(2)}, u32[]{:S(2)}) collective-permute-start(bf16[512,128]{1,0:T(8,128)(2,1)S(1)} %get-tuple-element.294), channel_id=1, source_target_pairs={{0,3},{1,0},{2,1},{3,2},{4,7},{5,4},{6,5},{7,6},{8,11},{9,8},{10,9... | collective-permute-start | bytes 393224 | tf_op jit(solution)/shard_map/ppermute | solution.py:504
  394.6 13.2 %collective-permute-start.16 = (bf16[512,128]{1,0:T(8,128)(2,1)S(1)}, bf16[512,128]{1,0:T(8,128)(2,1)S(1)}, u32[]{:S(2)}, u32[]{:S(2)}) collective-permute-start(bf16[512,128]{1,0:T(8,128)(2,1)S(1)} %get-tuple-element.293), channel_id=1, source_target_pairs={{0,2},{1,3},{2,0},{3,1},{4,6},{5,7},{6,4},{7,5},{8,10},{9,11},{10,... | collective-permute-start | bytes 393224 | tf_op jit(solution)/shard_map/ppermute | solution.py:504
  404.7 6.8 %collective-permute-start.17 = (bf16[512,128]{1,0:T(8,128)(2,1)S(1)}, bf16[512,128]{1,0:T(8,128)(2,1)S(1)}, u32[]{:S(2)}, u32[]{:S(2)}) collective-permute-start(bf16[512,128]{1,0:T(8,128)(2,1)S(1)} %get-tuple-element.292), channel_id=1, source_target_pairs={{0,1},{1,2},{2,3},{3,0},{4,5},{5,6},{6,7},{7,4},{8,9},{9,10},{10,1... | collective-permute-start | bytes 393224 | tf_op jit(solution)/shard_map/ppermute | solution.py:504
  407.8 36.5 %collective-permute-start.28 = (bf16[4,4,128,256]{2,3,1,0:T(8,128)(2,1)}, bf16[4,4,128,256]{2,3,1,0:T(8,128)(2,1)}, u32[]{:S(2)}, u32[]{:S(2)}) collective-permute-start(bf16[4,4,128,256]{2,3,1,0:T(8,128)(2,1)} %slice.689), channel_id=1, source_target_pairs={{0,4},{4,0},{8,12},{12,8},{16,20},{20,16},{24,28},{28,24},{1,5},{5... | collective-permute-start | bytes 3145736 | tf_op jit(solution)/shard_map/ppermute | solution.py:509
  407.8 13.0 %collective-permute-start.20 = (bf16[512,128]{1,0:T(8,128)(2,1)S(1)}, bf16[512,128]{1,0:T(8,128)(2,1)S(1)}, u32[]{:S(2)}, u32[]{:S(2)}) collective-permute-start(bf16[512,128]{1,0:T(8,128)(2,1)S(1)} %get-tuple-element.290), channel_id=1, source_target_pairs={{0,2},{1,3},{2,0},{3,1},{4,6},{5,7},{6,4},{7,5},{8,10},{9,11},{10,... | collective-permute-start | bytes 393224 | tf_op jit(solution)/shard_map/ppermute | solution.py:504
  411.5 9.3 %collective-permute-start.21 = (bf16[512,128]{1,0:T(8,128)(2,1)S(1)}, bf16[512,128]{1,0:T(8,128)(2,1)S(1)}, u32[]{:S(2)}, u32[]{:S(2)}) collective-permute-start(bf16[512,128]{1,0:T(8,128)(2,1)S(1)} %get-tuple-element.289), channel_id=1, source_target_pairs={{0,1},{1,2},{2,3},{3,0},{4,5},{5,6},{6,7},{7,4},{8,9},{9,10},{10,1... | collective-permute-start | bytes 393224 | tf_op jit(solution)/shard_map/ppermute | solution.py:504
  426.0 24.8 %collective-permute-start.27 = (bf16[2,1,128,1024]{2,3,1,0:T(8,128)(2,1)S(1)}, bf16[2,1,128,1024]{2,3,1,0:T(8,128)(2,1)}, u32[]{:S(2)}, u32[]{:S(2)}) collective-permute-start(bf16[2,1,128,1024]{2,3,1,0:T(8,128)(2,1)S(1)} %get-tuple-element.160), channel_id=1, source_target_pairs={{0,8},{4,12},{8,0},{12,4},{16,24},{20,28},{24,16},{28,20},{1,9},{5... | collective-permute-start | bytes 1572872 | tf_op jit(solution)/shard_map/ppermute | solution.py:509
  429.6 22.3 %collective-permute-start.26 = (bf16[2,1,128,1024]{2,3,1,0:T(8,128)(2,1)}, bf16[2,1,128,1024]{2,3,1,0:T(8,128)(2,1)}, u32[]{:S(2)}, u32[]{:S(2)}) collective-permute-start(bf16[2,1,128,1024]{2,3,1,0:T(8,128)(2,1)} %get-tuple-element.158), channel_id=1, source_target_pairs={{0,16},{4,20},{8,24},{12,28},{16,0},{20,4},{24,8},{28,12},{1,17},{... | collective-permute-start | bytes 1572872 | tf_op jit(solution)/shard_map/ppermute | solution.py:509
  438.6 14.5 %collective-permute-start.25 = (bf16[1024,256]{1,0:T(8,128)(2,1)}, bf16[1024,256]{1,0:T(8,128)(2,1)S(1)}, u32[]{:S(2)}, u32[]{:S(2)}) collective-permute-start(bf16[1024,256]{1,0:T(8,128)(2,1)} %get-tuple-element.156), channel_id=1, source_target_pairs={{4,0},{8,4},{12,8},{16,12},{20,16},{24,20},{28,24},{5,1},{9,5},{13... | collective-permute-start | bytes 1572872 | tf_op jit(solution)/shard_map/ppermute | solution.py:515
  439.9 53.7 %collective-permute-start.30 = (bf16[2,2,128,1024]{3,2,1,0:T(8,128)(2,1)}, bf16[2,2,128,1024]{3,2,1,0:T(8,128)(2,1)}, u32[]{:S(2)}, u32[]{:S(2)}) collective-permute-start(bf16[2,2,128,1024]{3,2,1,0:T(8,128)(2,1)} %get-tuple-element.169), channel_id=1, source_target_pairs={{0,16},{4,20},{8,24},{12,28},{16,0},{20,4},{24,8},{28,12},{1,17},{... | collective-permute-start | bytes 3145736 | tf_op jit(solution)/shard_map/ppermute | solution.py:509
  444.3 52.1 %collective-permute-start.29 = (bf16[2,2,128,1024]{3,2,1,0:T(8,128)(2,1)}, bf16[2,2,128,1024]{3,2,1,0:T(8,128)(2,1)}, u32[]{:S(2)}, u32[]{:S(2)}) collective-permute-start(bf16[2,2,128,1024]{3,2,1,0:T(8,128)(2,1)} %add_convert_fusion.3), channel_id=1, source_target_pairs={{0,8},{4,12},{8,0},{12,4},{16,24},{20,28},{24,16},{28,20},{1,9},{5... | collective-permute-start | bytes 3145736 | tf_op jit(solution)/shard_map/ppermute | solution.py:509
  454.9 19.2 %collective-permute-start.32 = (bf16[2,2,128,256]{2,3,1,0:T(8,128)(2,1)}, bf16[2,2,128,256]{2,3,1,0:T(8,128)(2,1)}, u32[]{:S(2)}, u32[]{:S(2)}) collective-permute-start(bf16[2,2,128,256]{2,3,1,0:T(8,128)(2,1)} %get-tuple-element.173), channel_id=1, source_target_pairs={{0,16},{4,20},{8,24},{12,28},{16,0},{20,4},{24,8},{28,12},{1,17},{... | collective-permute-start | bytes 786440 | tf_op jit(solution)/shard_map/ppermute | solution.py:509
  456.9 23.1 %collective-permute-start.31 = (bf16[2,2,128,256]{2,3,1,0:T(8,128)(2,1)}, bf16[2,2,128,256]{2,3,1,0:T(8,128)(2,1)S(1)}, u32[]{:S(2)}, u32[]{:S(2)}) collective-permute-start(bf16[2,2,128,256]{2,3,1,0:T(8,128)(2,1)} %add_convert_fusion.25), channel_id=1, source_target_pairs={{0,8},{4,12},{8,0},{12,4},{16,24},{20,28},{24,16},{28,20},{1,9},{5... | collective-permute-start | bytes 786440 | tf_op jit(solution)/shard_map/ppermute | solution.py:509
  470.7 16.2 %collective-permute-start.58 = (bf16[128,1024]{0,1:T(8,128)(2,1)}, bf16[128,1024]{0,1:T(8,128)(2,1)S(1)}, u32[]{:S(2)}, u32[]{:S(2)}) collective-permute-start(bf16[128,1024]{0,1:T(8,128)(2,1)} %get-tuple-element.296), channel_id=1, source_target_pairs={{0,2},{1,3},{2,0},{3,1},{4,6},{5,7},{6,4},{7,5},{8,10},{9,11},{10,... | collective-permute-start | bytes 786440 | tf_op jit(solution)/shard_map/ppermute | solution.py:504
  474.1 14.4 %collective-permute-start.59 = (bf16[128,1024]{0,1:T(8,128)(2,1)}, bf16[128,1024]{0,1:T(8,128)(2,1)S(1)}, u32[]{:S(2)}, u32[]{:S(2)}) collective-permute-start(bf16[128,1024]{0,1:T(8,128)(2,1)} %get-tuple-element.297), channel_id=1, source_target_pairs={{0,3},{1,0},{2,1},{3,2},{4,7},{5,4},{6,5},{7,6},{8,11},{9,8},{10,9... | collective-permute-start | bytes 786440 | tf_op jit(solution)/shard_map/ppermute | solution.py:504
  480.7 12.0 %collective-permute-start.57 = (bf16[128,1024]{0,1:T(8,128)(2,1)}, bf16[128,1024]{0,1:T(8,128)(2,1)S(1)}, u32[]{:S(2)}, u32[]{:S(2)}) collective-permute-start(bf16[128,1024]{0,1:T(8,128)(2,1)} %slice_bitcast_fusion.2), channel_id=1, source_target_pairs={{0,1},{1,2},{2,3},{3,0},{4,5},{5,6},{6,7},{7,4},{8,9},{9,10},{10,1... | collective-permute-start | bytes 786440 | tf_op jit(solution)/shard_map/ppermute | solution.py:504
  486.8 12.3 %collective-permute-start.18 = (bf16[1024,256]{1,0:T(8,128)(2,1)}, bf16[1024,256]{1,0:T(8,128)(2,1)S(1)}, u32[]{:S(2)}, u32[]{:S(2)}) collective-permute-start(bf16[1024,256]{1,0:T(8,128)(2,1)} %get-tuple-element.143), channel_id=1, source_target_pairs={{4,0},{8,4},{12,8},{16,12},{20,16},{24,20},{28,24},{5,1},{9,5},{13... | collective-permute-start | bytes 1572872 | tf_op jit(solution)/shard_map/ppermute | solution.py:515
  499.2 25.2 %collective-permute-start.39 = (bf16[2,1,128,256]{2,3,1,0:T(8,128)(2,1)}, bf16[2,1,128,256]{2,3,1,0:T(8,128)(2,1)S(1)}, u32[]{:S(2)}, u32[]{:S(2)}) collective-permute-start(bf16[2,1,128,256]{2,3,1,0:T(8,128)(2,1)} %get-tuple-element.189), channel_id=1, source_target_pairs={{0,8},{4,12},{8,0},{12,4},{16,24},{20,28},{24,16},{28,20},{1,9},{5... | collective-permute-start | bytes 393224 | tf_op jit(solution)/shard_map/ppermute | solution.py:509
  505.7 18.7 %collective-permute-start.38 = (bf16[2,1,128,256]{2,3,1,0:T(8,128)(2,1)S(1)}, bf16[2,1,128,256]{2,3,1,0:T(8,128)(2,1)S(1)}, u32[]{:S(2)}, u32[]{:S(2)}) collective-permute-start(bf16[2,1,128,256]{2,3,1,0:T(8,128)(2,1)S(1)} %get-tuple-element.187), channel_id=1, source_target_pairs={{0,16},{4,20},{8,24},{12,28},{16,0},{20,4},{24,8},{28,12},{1,17},{... | collective-permute-start | bytes 393224 | tf_op jit(solution)/shard_map/ppermute | solution.py:509
  506.1 18.4 %collective-permute-start.37 = (bf16[2,1,128,1024]{3,2,1,0:T(8,128)(2,1)}, bf16[2,1,128,1024]{3,2,1,0:T(8,128)(2,1)}, u32[]{:S(2)}, u32[]{:S(2)}) collective-permute-start(bf16[2,1,128,1024]{3,2,1,0:T(8,128)(2,1)} %get-tuple-element.185), channel_id=1, source_target_pairs={{0,8},{4,12},{8,0},{12,4},{16,24},{20,28},{24,16},{28,20},{1,9},{5... | collective-permute-start | bytes 1572872 | tf_op jit(solution)/shard_map/ppermute | solution.py:509
  506.2 19.8 %collective-permute-start.36 = (bf16[2,1,128,1024]{3,2,1,0:T(8,128)(2,1)}, bf16[2,1,128,1024]{3,2,1,0:T(8,128)(2,1)}, u32[]{:S(2)}, u32[]{:S(2)}) collective-permute-start(bf16[2,1,128,1024]{3,2,1,0:T(8,128)(2,1)} %get-tuple-element.183), channel_id=1, source_target_pairs={{0,16},{4,20},{8,24},{12,28},{16,0},{20,4},{24,8},{28,12},{1,17},{... | collective-permute-start | bytes 1572872 | tf_op jit(solution)/shard_map/ppermute | solution.py:509
  512.5 91.2 %collective-permute-start.33 = (bf16[512,384]{1,0:T(8,128)(2,1)}, bf16[512,384]{1,0:T(8,128)(2,1)}, u32[]{:S(2)}, u32[]{:S(2)}) collective-permute-start(bf16[512,384]{1,0:T(8,128)(2,1)} %get-tuple-element.270), channel_id=1, source_target_pairs={{0,1},{1,2},{2,3},{3,0},{4,5},{5,6},{6,7},{7,4},{8,9},{9,10},{10,1... | collective-permute-start | bytes 1179656 | tf_op jit(solution)/shard_map/ppermute | solution.py:504
  535.6 66.8 %copy-start.46 = (bf16[256,1024]{1,0:T(8,128)(2,1)S(1)}, bf16[256,1024]{1,0:T(8,128)(2,1)}, u32[]{:S(2)}) copy-start(bf16[256,1024]{1,0:T(8,128)(2,1)} %get-tuple-element.253) | copy-start | bytes 1572868
  535.6 1.3 collective-permute-start.46
  536.9 7.3 %collective-permute-start.47 = (f32[92,128]{1,0:T(8,128)S(1)}, f32[92,128]{1,0:T(8,128)S(1)}, u32[]{:S(2)}, u32[]{:S(2)}) collective-permute-start(f32[92,128]{1,0:T(8,128)S(1)} %bitcast_add_fusion), channel_id=1, source_target_pairs={{0,8},{4,12},{8,0},{12,4},{16,24},{20,28},{24,16},{28,20},{1,9},{5... | collective-permute-start | bytes 141320 | tf_op jit(solution)/shard_map/ppermute | solution.py:509
  540.4 13.1 %collective-permute-start.52 = (bf16[128,256]{0,1:T(8,128)(2,1)S(1)}, bf16[128,256]{0,1:T(8,128)(2,1)S(1)}, u32[]{:S(2)}, u32[]{:S(2)}) collective-permute-start(bf16[128,256]{0,1:T(8,128)(2,1)S(1)} %get-tuple-element.321), channel_id=1, source_target_pairs={{0,2},{1,3},{2,0},{3,1},{4,6},{5,7},{6,4},{7,5},{8,10},{9,11},{10,... | collective-permute-start | bytes 196616 | tf_op jit(solution)/shard_map/ppermute | solution.py:504
  542.8 12.8 %collective-permute-start.53 = (bf16[128,256]{0,1:T(8,128)(2,1)S(1)}, bf16[128,256]{0,1:T(8,128)(2,1)S(1)}, u32[]{:S(2)}, u32[]{:S(2)}) collective-permute-start(bf16[128,256]{0,1:T(8,128)(2,1)S(1)} %get-tuple-element.322), channel_id=1, source_target_pairs={{0,1},{1,2},{2,3},{3,0},{4,5},{5,6},{6,7},{7,4},{8,9},{9,10},{10,1... | collective-permute-start | bytes 196616 | tf_op jit(solution)/shard_map/ppermute | solution.py:504
  544.3 4.2 collective-permute-start.48
  544.3 11.3 %collective-permute-start.51 = (bf16[128,256]{0,1:T(8,128)(2,1)S(1)}, bf16[128,256]{0,1:T(8,128)(2,1)S(1)}, u32[]{:S(2)}, u32[]{:S(2)}) collective-permute-start(bf16[128,256]{0,1:T(8,128)(2,1)S(1)} %slice_bitcast_fusion.8), channel_id=1, source_target_pairs={{0,3},{1,0},{2,1},{3,2},{4,7},{5,4},{6,5},{7,6},{8,11},{9,8},{10,9... | collective-permute-start | bytes 196616 | tf_op jit(solution)/shard_map/ppermute | solution.py:504
  548.4 4.2 collective-permute-start.49
  552.6 51.5 %collective-permute-start.34 = (bf16[512,384]{1,0:T(8,128)(2,1)S(1)}, bf16[512,384]{1,0:T(8,128)(2,1)S(1)}, u32[]{:S(2)}, u32[]{:S(2)}) collective-permute-start(bf16[512,384]{1,0:T(8,128)(2,1)S(1)} %copy-done.59), channel_id=1, source_target_pairs={{0,2},{1,3},{2,0},{3,1},{4,6},{5,7},{6,4},{7,5},{8,10},{9,11},{10,... | collective-permute-start | bytes 1179656 | tf_op jit(solution)/shard_map/ppermute | solution.py:504
  553.5 39.1 %collective-permute-start.40 = (bf16[512,256]{1,0:T(8,128)(2,1)S(1)}, bf16[512,256]{1,0:T(8,128)(2,1)S(1)}, u32[]{:S(2)}, u32[]{:S(2)}) collective-permute-start(bf16[512,256]{1,0:T(8,128)(2,1)S(1)} %get-tuple-element.275), channel_id=1, source_target_pairs={{0,1},{1,2},{2,3},{3,0},{4,5},{5,6},{6,7},{7,4},{8,9},{9,10},{10,1... | collective-permute-start | bytes 786440 | tf_op jit(solution)/shard_map/ppermute | solution.py:504
  555.6 37.6 %collective-permute-start.41 = (bf16[512,256]{1,0:T(8,128)(2,1)S(1)}, bf16[512,256]{1,0:T(8,128)(2,1)S(1)}, u32[]{:S(2)}, u32[]{:S(2)}) collective-permute-start(bf16[512,256]{1,0:T(8,128)(2,1)S(1)} %get-tuple-element.274), channel_id=1, source_target_pairs={{0,2},{1,3},{2,0},{3,1},{4,6},{5,7},{6,4},{7,5},{8,10},{9,11},{10,... | collective-permute-start | bytes 786440 | tf_op jit(solution)/shard_map/ppermute | solution.py:504
  555.7 33.5 %collective-permute-start.50 = (f32[92,128]{1,0:T(8,128)S(1)}, f32[92,128]{1,0:T(8,128)S(1)}, u32[]{:S(2)}, u32[]{:S(2)}) collective-permute-start(f32[92,128]{1,0:T(8,128)S(1)} %add.456), channel_id=1, source_target_pairs={{0,2},{1,3},{2,0},{3,1},{4,6},{5,7},{6,4},{7,5},{8,10},{9,11},{10,... | collective-permute-start | bytes 141320 | tf_op jit(solution)/shard_map/ppermute | solution.py:509
  589.1 9.2 %collective-permute-start.42 = (bf16[512,256]{1,0:T(8,128)(2,1)S(1)}, bf16[512,256]{1,0:T(8,128)(2,1)S(1)}, u32[]{:S(2)}, u32[]{:S(2)}) collective-permute-start(bf16[512,256]{1,0:T(8,128)(2,1)S(1)} %get-tuple-element.273), channel_id=1, source_target_pairs={{0,3},{1,0},{2,1},{3,2},{4,7},{5,4},{6,5},{7,6},{8,11},{9,8},{10,9... | collective-permute-start | bytes 786440 | tf_op jit(solution)/shard_map/ppermute | solution.py:504
  592.6 15.9 %collective-permute-start.35 = (bf16[512,384]{1,0:T(8,128)(2,1)S(1)}, bf16[512,384]{1,0:T(8,128)(2,1)S(1)}, u32[]{:S(2)}, u32[]{:S(2)}) collective-permute-start(bf16[512,384]{1,0:T(8,128)(2,1)S(1)} %copy-done.58), channel_id=1, source_target_pairs={{0,3},{1,0},{2,1},{3,2},{4,7},{5,4},{6,5},{7,6},{8,11},{9,8},{10,9... | collective-permute-start | bytes 1179656 | tf_op jit(solution)/shard_map/ppermute | solution.py:504
  593.2 33.1 %collective-permute-start.55 = (bf16[128,1024]{1,0:T(8,128)(2,1)S(1)}, bf16[128,1024]{1,0:T(8,128)(2,1)S(1)}, u32[]{:S(2)}, u32[]{:S(2)}) collective-permute-start(bf16[128,1024]{1,0:T(8,128)(2,1)S(1)} %get-tuple-element.298), channel_id=1, source_target_pairs={{0,2},{1,3},{2,0},{3,1},{4,6},{5,7},{6,4},{7,5},{8,10},{9,11},{10,... | collective-permute-start | bytes 786440 | tf_op jit(solution)/shard_map/ppermute | solution.py:504
  598.3 28.0 %collective-permute-start.56 = (bf16[128,1024]{1,0:T(8,128)(2,1)S(1)}, bf16[128,1024]{1,0:T(8,128)(2,1)S(1)}, u32[]{:S(2)}, u32[]{:S(2)}) collective-permute-start(bf16[128,1024]{1,0:T(8,128)(2,1)S(1)} %get-tuple-element.299), channel_id=1, source_target_pairs={{0,3},{1,0},{2,1},{3,2},{4,7},{5,4},{6,5},{7,6},{8,11},{9,8},{10,9... | collective-permute-start | bytes 786440 | tf_op jit(solution)/shard_map/ppermute | solution.py:504
  603.7 22.6 %collective-permute-start.54 = (bf16[128,1024]{1,0:T(8,128)(2,1)S(1)}, bf16[128,1024]{1,0:T(8,128)(2,1)S(1)}, u32[]{:S(2)}, u32[]{:S(2)}) collective-permute-start(bf16[128,1024]{1,0:T(8,128)(2,1)S(1)} %slice_bitcast_fusion.5), channel_id=1, source_target_pairs={{0,1},{1,2},{2,3},{3,0},{4,5},{5,6},{6,7},{7,4},{8,9},{9,10},{10,1... | collective-permute-start | bytes 786440 | tf_op jit(solution)/shard_map/ppermute | solution.py:504
  604.1 14.6 %collective-permute-start.43 = (bf16[2,2,128,640]{3,2,1,0:T(8,128)(2,1)S(1)}, bf16[2,2,128,640]{3,2,1,0:T(8,128)(2,1)S(1)}, u32[]{:S(2)}, u32[]{:S(2)}) collective-permute-start(bf16[2,2,128,640]{3,2,1,0:T(8,128)(2,1)S(1)} %fusion.52), channel_id=1, source_target_pairs={{0,16},{4,20},{8,24},{12,28},{16,0},{20,4},{24,8},{28,12},{1,17},{... | collective-permute-start | bytes 1966088 | tf_op jit(solution)/shard_map/ppermute | solution.py:509
  618.9 7.1 %collective-permute-start.44 = (bf16[2,128,640]{2,1,0:T(8,128)(2,1)S(1)}, bf16[2,128,640]{2,1,0:T(8,128)(2,1)S(1)}, u32[]{:S(2)}, u32[]{:S(2)}) collective-permute-start(bf16[2,128,640]{2,1,0:T(8,128)(2,1)S(1)} %dynamic-slice_bitcast_fusion.12), channel_id=1, source_target_pairs={{0,8},{4,12},{8,0},{12,4},{16,24},{20,28},{24,16},{28,20},{1,9},{5... | collective-permute-start | bytes 983048 | tf_op jit(solution)/shard_map/ppermute | solution.py:509
  626.2 1.5 collective-permute-start.45
  (80 other events, 855.3 us)
Sparse Core Ops, SparseCore 0:
  13.5 168.2 all-gather.4
  184.7 75.3 all-gather.6

commit v3 on v2

--- a/solution.py
+++ b/solution.py
@@ -18,6 +18,7 @@
 SCALE = HEAD ** -0.5
 GELU_A = 0.7978845608028654
 GELU_B = 0.044715
+SEQ = ("run", "core")
 
 
 def dot(a, b, dims, out=F32):
@@ -359,144 +360,161 @@
     )(meta, start, q, k, v, do, turned, logs, dq, dk, dv, back)
 
 
-def up_kernel(parts, places_ref, sn_ref, cot_ref, up_ref, bias_ref, down_ref, out_ref, slope_ref, sent_ref, kept_ref):
-    step = pl.program_id(0)
-    rows = up_ref.shape[0] * up_ref.shape[1]
-    hidden = nn(sn_ref[...], up_ref[...].reshape(rows, UNIT)) + bias_ref[0]
-    square = hidden * hidden
-    curve = jnp.tanh(GELU_A * (hidden + GELU_B * (hidden * square)))
-    half = 0.5 * (1.0 + curve)
-    activated = (hidden * half).astype(BF16)
-    slope_ref[...] = half + 0.5 * hidden * (1.0 - curve * curve) * (
-        GELU_A * (1.0 + 3.0 * GELU_B * square)
-    )
-    part = nn(activated, down_ref[...].reshape(UNIT, rows))
-
-    @pl.when(step == 0)
+def store_grad(grad_ref, grad):
+    runs, _, lanes, rows, cols = grad_ref.shape
+    for j in range(lanes):
+        grad_ref[:, 0, j] = grad[:, j * cols : (j + 1) * cols].reshape(runs, rows, cols)
+
+
+def accumulate(ref, value):
+    @pl.when(pl.program_id(0) == 0)
     def _():
-        out_ref[...] = part
-
-    @pl.when(step > 0)
+        ref[...] = value
+
+    @pl.when(pl.program_id(0) > 0)
     def _():
-        out_ref[...] += part
-
-    grad = nn(cot_ref[...], activated).astype(BF16)
-    sent_ref[0] = grad[: rows // 2]
-    kept_ref[0] = grad[rows // 2 :]
+        ref[...] += value
+
+
+def up_kernel(places_ref, sn_ref, got_ref, cot_ref, up_ref, bias_ref, down_ref, out_ref, other_ref, slope_ref, grad_ref, act_ref):
+    width = up_ref.shape[0] * up_ref.shape[1]
+    rows = sn_ref.shape[0]
+    up = up_ref[...].reshape(width, UNIT)
+    down = down_ref[...].reshape(UNIT, width)
+    for i, (piece_ref, sum_ref) in enumerate(((sn_ref, out_ref), (got_ref, other_ref))):
+        span = slice(i * rows, (i + 1) * rows)
+        hidden = nn(piece_ref[...], up) + bias_ref[0]
+        square = hidden * hidden
+        curve = jnp.tanh(GELU_A * (hidden + GELU_B * (hidden * square)))
+        half = 0.5 * (1.0 + curve)
+        activated = (hidden * half).astype(BF16)
+        slope_ref[span, :] = half + 0.5 * hidden * (1.0 - curve * curve) * (
+            GELU_A * (1.0 + 3.0 * GELU_B * square)
+        )
+        act_ref[span, :] = activated
+        accumulate(sum_ref, nn(activated, down))
+    store_grad(grad_ref, nn(cot_ref[...], act_ref[...]).astype(BF16))
 
 
 def feed_specs(gathered, seq, parts, width):
     part = width // seq
     per = width // UNIT
+    run = seq // 2
 
     def spot(i, p):
-        return lax.rem(p[0] + i // per, parts)
-
+        return lax.rem(p[0] + i, parts)
+
+    def grad_spec(kind):
+        return pl.BlockSpec(
+            (run, 1, UNIT // PAIR, width // run, PAIR), lambda i, p: (0, spot(i, p), kind, 0, 0)
+        )
+
+    grad = jax.ShapeDtypeStruct((run, parts, 2 * UNIT // PAIR, width // run, PAIR), BF16)
     return (
-        pl.BlockSpec((seq, part, UNIT), lambda i, p: (spot(i, p), 0, lax.rem(i, per))),
-        pl.BlockSpec((UNIT // part, part, width), lambda i, p: (spot(i, p) * per + lax.rem(i, per), 1, 0)),
-        pl.BlockSpec((1, width // 2, UNIT), lambda i, p: (i // per, 0, lax.rem(i, per))),
-        per,
-    )
-
-
-def feed_up(places, sn, cot_turned, gathered, bias, seq, parts):
+        pl.BlockSpec((seq, part, UNIT), lambda i, p: (spot(i, p), 0, p[1])),
+        pl.BlockSpec((UNIT // part, part, width), lambda i, p: (spot(i, p) * per + p[1], 1, 0)),
+        grad_spec,
+        grad,
+    )
+
+
+def fixed(shape):
+    return pl.BlockSpec(shape, lambda i, p: (0,) * len(shape))
+
+
+def feed_up(places, sn, got, cot_turned, gathered, bias, seq, parts):
     rows, width = sn.shape
-    up_spec, down_spec, grad_spec, per = feed_specs(gathered, seq, parts, width)
-    grad = jax.ShapeDtypeStruct((parts, width // 2, width), BF16)
+    up_spec, down_spec, grad_spec, grad = feed_specs(gathered, seq, parts, width)
     return pl.pallas_call(
-        functools.partial(up_kernel, parts),
+        up_kernel,
         grid_spec=pltpu.PrefetchScalarGridSpec(
             num_scalar_prefetch=1,
-            grid=(parts * per,),
+            grid=(parts,),
             in_specs=[
-                pl.BlockSpec((rows, width), lambda i, p: (0, 0)),
-                pl.BlockSpec((width, rows), lambda i, p: (0, 0)),
+                fixed((rows, width)),
+                fixed((rows, width)),
+                fixed((width, 2 * rows)),
                 up_spec,
-                pl.BlockSpec((1, 1, UNIT), lambda i, p: (lax.rem(parts - i // per, parts), 0, lax.rem(i, per))),
+                pl.BlockSpec((1, 1, UNIT), lambda i, p: (lax.rem(parts - i, parts), 0, p[1])),
                 down_spec,
             ],
             out_specs=[
-                pl.BlockSpec((rows, width), lambda i, p: (0, 0)),
-                pl.BlockSpec((rows, UNIT), lambda i, p: (0, i)),
-                grad_spec,
-                grad_spec,
-            ],
+                fixed((rows, width)),
+                fixed((rows, width)),
+                pl.BlockSpec((2 * rows, UNIT), lambda i, p: (0, i)),
+                grad_spec(0),
+            ],
+            scratch_shapes=[pltpu.VMEM((2 * rows, UNIT), BF16)],
         ),
         out_shape=[
             jax.ShapeDtypeStruct((rows, width), F32),
-            jax.ShapeDtypeStruct((rows, parts * width), F32),
-            grad,
+            jax.ShapeDtypeStruct((rows, width), F32),
+            jax.ShapeDtypeStruct((2 * rows, parts * UNIT), F32),
             grad,
         ],
         cost_estimate=light(16 * rows * width),
         name="feed_up",
-    )(places, sn, cot_turned, gathered, bias, gathered)
-
-
-def down_kernel(seq, places_ref, cot_ref, sn_ref, slope_ref, up_ref, down_ref, back_ref, sent_ref, kept_ref, bias_ref, plain_ref, turned_ref):
-    step = pl.program_id(0)
-    rows = up_ref.shape[0] * up_ref.shape[1]
-    part = rows // seq
-
-    @pl.when(step == 0)
+    )(places, sn, got, cot_turned, gathered, bias, gathered)
+
+
+def down_kernel(places_ref, cot_ref, cot_got_ref, sn_ref, got_ref, slope_ref, up_ref, down_ref, grads_ref, back_ref, other_ref, grad_ref, bias_ref, turned_ref, hidden_ref):
+    width = up_ref.shape[0] * up_ref.shape[1]
+    rows = sn_ref.shape[0]
+
+    @pl.when(pl.program_id(0) == 0)
     def _():
-        plain_ref[...] = sn_ref[...].T
-        for spot, r in enumerate(halves_order(seq)):
-            lines = pl.ds(pl.multiple_of(jnp.bitwise_xor(places_ref[1], r) * part, part), part)
-            turned_ref[spot * part : (spot + 1) * part, :] = plain_ref[lines, :]
-
-    hidden_back = nt(cot_ref[...], down_ref[...].reshape(UNIT, rows)) * slope_ref[...]
-    rounded = hidden_back.astype(BF16)
-    bias_ref[0] = jnp.sum(rounded.astype(F32), axis=0, keepdims=True)
-    share = nt(rounded, up_ref[...].reshape(rows, UNIT))
-
-    @pl.when(step == 0)
-    def _():
-        back_ref[...] = share
-
-    @pl.when(step > 0)
-    def _():
-        back_ref[...] += share
-
-    grad = nn(turned_ref[...], rounded).astype(BF16)
-    sent_ref[0] = grad[: rows // 2]
-    kept_ref[0] = grad[rows // 2 :]
-
-
-def feed_down(places, cot, sn, slope, gathered, seq, parts):
+        turned_ref[:, :rows] = sn_ref[...].T
+        turned_ref[:, rows:] = got_ref[...].T
+
+    up = up_ref[...].reshape(width, UNIT)
+    down = down_ref[...].reshape(UNIT, width)
+    total = jnp.zeros((1, UNIT), F32)
+    for i, (piece_ref, sum_ref) in enumerate(((cot_ref, back_ref), (cot_got_ref, other_ref))):
+        span = slice(i * rows, (i + 1) * rows)
+        rounded = (nt(piece_ref[...], down) * slope_ref[span, :]).astype(BF16)
+        total = total + jnp.sum(rounded.astype(F32), axis=0, keepdims=True)
+        hidden_ref[span, :] = rounded
+        accumulate(sum_ref, nt(rounded, up))
+    bias_ref[0] = total
+    store_grad(grad_ref, nn(turned_ref[...], hidden_ref[...]).astype(BF16))
+
+
+def feed_down(places, cot, cot_got, sn, got, slope, gathered, grads, seq, parts):
     rows, width = cot.shape
-    up_spec, down_spec, grad_spec, per = feed_specs(gathered, seq, parts, width)
-    grad = jax.ShapeDtypeStruct((parts, width // 2, width), BF16)
+    up_spec, down_spec, grad_spec, grad = feed_specs(gathered, seq, parts, width)
     return pl.pallas_call(
-        functools.partial(down_kernel, seq),
+        down_kernel,
         grid_spec=pltpu.PrefetchScalarGridSpec(
             num_scalar_prefetch=1,
-            grid=(parts * per,),
-            in_specs=[
-                pl.BlockSpec((rows, width), lambda i, p: (0, 0)),
-                pl.BlockSpec((rows, width), lambda i, p: (0, 0)),
-                pl.BlockSpec((rows, UNIT), lambda i, p: (0, i)),
+            grid=(parts,),
+            in_specs=[fixed((rows, width))] * 4
+            + [
+                pl.BlockSpec((2 * rows, UNIT), lambda i, p: (0, i)),
                 up_spec,
                 down_spec,
+                ANY,
             ],
             out_specs=[
-                pl.BlockSpec((rows, width), lambda i, p: (0, 0)),
-                grad_spec,
-                grad_spec,
-                pl.BlockSpec((1, 1, UNIT), lambda i, p: (i // per, 0, lax.rem(i, per))),
-            ],
-            scratch_shapes=[pltpu.VMEM((width, rows), BF16)] * 2,
+                fixed((rows, width)),
+                fixed((rows, width)),
+                grad_spec(1),
+                pl.BlockSpec((1, 1, UNIT), lambda i, p: (i, 0, 0)),
+            ],
+            scratch_shapes=[
+                pltpu.VMEM((width, 2 * rows), BF16),
+                pltpu.VMEM((2 * rows, UNIT), BF16),
+            ],
         ),
         out_shape=[
             jax.ShapeDtypeStruct((rows, width), F32),
+            jax.ShapeDtypeStruct((rows, width), F32),
             grad,
-            grad,
-            jax.ShapeDtypeStruct((parts, 1, width), F32),
+            jax.ShapeDtypeStruct((parts, 1, UNIT), F32),
         ],
+        input_output_aliases={8: 2},
         cost_estimate=light(16 * rows * width),
         name="feed_down",
-    )(places, cot, sn, slope, gathered, gathered)
+    )(places, cot, cot_got, sn, got, slope, gathered, gathered, grads)
 
 
 def around(value, steps):
@@ -510,13 +528,13 @@
 
 
 def along(value, steps):
-    count = lax.axis_size("seq")
+    count = lax.axis_size(SEQ)
     first, last = max(0, -steps), min(count, count - steps)
-    return lax.ppermute(value, "seq", [(i, i + steps) for i in range(first, last)])
+    return lax.ppermute(value, SEQ, [(i, i + steps) for i in range(first, last)])
 
 
 def summed(value):
-    for axis in ("seq", "tp"):
+    for axis in (SEQ, "tp"):
         bit = 1
         while bit < lax.axis_size(axis):
             value = value + flipped(value, axis, bit)
@@ -538,7 +556,7 @@
 
 def seq_bits():
     bits, bit = [], 1
-    while bit < lax.axis_size("seq"):
+    while bit < lax.axis_size(SEQ):
         bits.append(bit)
         bit *= 2
     return bits
@@ -547,8 +565,8 @@
 class Scatter:
     def __init__(self, sent, kept, sign):
         self.sign = sign
-        left = list(range(0, lax.axis_size("seq"), 2))
-        got = flipped(sent, "seq", 1)
+        left = list(range(0, lax.axis_size(SEQ), 2))
+        got = flipped(sent, SEQ, 1)
         cut = kept.shape[0] // 2
         tail = seq_bits()[1:]
         self.lanes = [
@@ -589,7 +607,7 @@
         lanes = []
         for left, bits in self.plans:
             goes, stays = arrays.pop(0), arrays.pop(0)
-            lanes.append((stays, flipped(goes, "seq", bits[0]), left, bits[1:]))
+            lanes.append((stays, flipped(goes, SEQ, bits[0]), left, bits[1:]))
         self.lanes = lanes
 
     def result(self):
@@ -606,13 +624,31 @@
 
 
 def scatter_seq(value, place):
-    seq = value.shape[0]
-    bits = sorted(seq_bits(), reverse=True)
+    bits = seq_bits()
     left = value.reshape((2,) * len(bits) + value.shape[1:])
-    for bit in bits:
+    for spot, bit in enumerate(bits):
+        dim = len(bits) - 1 - spot
         mine = (place // bit) % 2
-        left = joined(pick(left, mine, 0), flipped(pick(left, 1 - mine, 0), "seq", bit))
+        left = joined(pick(left, mine, dim), flipped(pick(left, 1 - mine, dim), SEQ, bit))
     return left
+
+
+def swapped(value, bit, place, dim):
+    other = flipped(value, SEQ, bit)
+    low = (place // bit) % 2 == 0
+    return jnp.stack((jnp.where(low, value, other), jnp.where(low, other, value)), axis=dim)
+
+
+def quarter(shard, place):
+    size = shard.shape[0] // 4
+    spot = 2 * ((place // 2) % 2) + place % 2
+    return lax.dynamic_slice_in_dim(shard, spot * size, size, 0)
+
+
+def shards(own, piece, place):
+    got = jnp.stack([around(piece, k) for k in range(1, lax.axis_size("tp"))])
+    got = swapped(swapped(got, 2, place, 1), 1, place, 2)
+    return jnp.concatenate((own[None], got.reshape((-1,) + own.shape)), axis=0)
 
 
 def center(rows):
@@ -640,10 +676,11 @@
     tokens = skip_values.shape[0]
     own = query_weight.shape[1]
     tp = lax.axis_size("tp")
-    seq = lax.axis_size("seq")
-    seq_place = lax.axis_index("seq")
+    seq = lax.axis_size(SEQ)
+    seq_place = lax.axis_index(SEQ)
     tp_place = lax.axis_index("tp")
-    places = jnp.stack((tp_place, seq_place)).astype(jnp.int32)
+    core = lax.axis_index("core")
+    places = jnp.stack((tp_place, core)).astype(jnp.int32)
     half = tokens - DOC_MAX
     part = width // seq
     kcol = own // PAIR
@@ -659,10 +696,7 @@
         size = shard.shape[0] // seq
         return lax.dynamic_slice_in_dim(shard, seq_place * size, size, 0)
 
-    packet = jnp.concatenate([own_rows(w) for w in (up_weight, down_weight, mixing_weight)], axis=0)
-    gathered = lax.all_gather(packet, ("tp", "seq"), axis=0, tiled=False)
-    mixing_full = gathered[:, 2 * part :].reshape(tp, own, width)
-    mixing_rot = jnp.concatenate([pick(mixing_full, (tp_place - k) % tp, 0) for k in range(tp)], axis=0)
+    packet = jnp.concatenate([own_rows(w) for w in (up_weight, down_weight)], axis=0)
     qkv_turned = jnp.concatenate(
         (
             query_weight[:, :PAIR], key_weight[:, :PAIR], value_weight,
@@ -670,33 +704,42 @@
         ),
         axis=1,
     ).T
+    qkv_piece = quarter(qkv_turned, seq_place)
     bias_pieces = jnp.stack([up_bias] + [around(up_bias, k) for k in range(1, tp)])[:, None]
+    cot_got = flipped(cotangent, "core", 1)
+    cot_turned = jnp.concatenate((cotangent, cot_got), axis=0).T
+
+    padded = jnp.concatenate((jnp.full((DOC_MAX,), -1, jnp.int32), segments))
+    window = lax.dynamic_slice_in_dim(padded, seq_place * tokens, DOC_MAX + tokens, 0)
+    start = jnp.sum(
+        (window[:, None] < window[None, DOC_MAX:]).astype(jnp.int32), axis=0, keepdims=True
+    )
+    meta = jnp.concatenate((start[0, ::TILE] // TILE, places))
+    halo_skip = along(skip_values[half:], 1)
+    skip_early = jnp.concatenate((halo_skip, skip_values[:half]), axis=0)
 
     wqkv = jnp.concatenate((query_weight, key_weight, value_weight), axis=1)
     bias = jnp.concatenate((query_bias, jnp.zeros((own,), F32), value_bias))[None]
     made = None
     for k in range(tp):
+        if k == tp - 1:
+            (
+                piece, meta, start, skip_early, bias_pieces, cot_got, cot_turned, qkv_piece,
+                mixing_piece,
+            ) = tied(
+                piece, meta, start, skip_early, bias_pieces, cot_got, cot_turned, qkv_piece,
+                quarter(mixing_weight, seq_place),
+            )
         ahead = around(piece, 1) if k < tp - 1 else None
         made = project(k, tp, places, piece, wqkv, bias, made)
         piece = ahead
+        if k == 0:
+            piece, packet = tied(piece, packet)
+            gathered = lax.all_gather(packet, ("tp",) + SEQ, axis=0, tiled=False)
     qkv, normed = made
-    qkv, packet = tied(qkv, own_rows(qkv_turned))
-    qkv_full = lax.all_gather(packet, ("tp", "seq"), axis=0, tiled=False).reshape(tp, -1, width)
-    shares = [
-        jnp.concatenate([pick(part, (tp_place - k) % tp, 0) for k in range(tp)], axis=0)
-        for part in (qkv_full[:, : 3 * PAIR], qkv_full[:, 3 * PAIR :])
-    ]
-
-    padded = jnp.concatenate((jnp.full((DOC_MAX,), -1, jnp.int32), segments))
-    window = lax.dynamic_slice_in_dim(padded, seq_place * tokens, DOC_MAX + tokens, 0)
-    start = jnp.sum(
-        (window[:, None] < window[None, DOC_MAX:]).astype(jnp.int32), axis=0, keepdims=True
-    )
-    meta = jnp.concatenate((start[0, ::TILE] // TILE, places))
-
-    halo_skip = along(skip_values[half:], 1)
+    mixing_rot = shards(mixing_weight, mixing_piece, seq_place).reshape(tp * own, width)
+
     halo = along(qkv[half:, own:], 1)
-    skip_early = jnp.concatenate((halo_skip, skip_values[:half]), axis=0)
     early = jnp.concatenate((halo, qkv[:half, own:]), axis=0)
 
     def values_of(pair):
@@ -729,19 +772,24 @@
         cut = value.reshape(rows, seq, part)
         return jnp.concatenate([pick(cut, seq_place ^ r, 1) for r in halves_order(seq)], axis=1)
 
-    lost, slope, down_sent, down_kept = feed_up(
-        places, second, by_distance(cotangent).T, gathered, bias_pieces, seq, tp
-    )
-    output = (middle + lost + down_bias).astype(BF16)
-
-    shape = (tp, seq // 2, part, width)
-    down_sum = Scatter(down_sent.reshape(shape), down_kept.reshape(shape), 1)
-    second_back, up_sent, up_kept, up_bias_grad = feed_down(
-        places, cotangent, second, slope, gathered, seq, tp
-    )
-    up_sum = Scatter(up_sent.reshape(shape), up_kept.reshape(shape), 1)
-    second_back, ready = tied(second_back, down_sum.merge())
-    down_sum.send(ready)
+    got = flipped(second, "core", 1)
+    lost, lost_other, slope, grads = feed_up(
+        places, second, got, cot_turned, gathered, bias_pieces, seq, tp
+    )
+    qkv_piece, lost_other = tied(qkv_piece, lost_other)
+    output = (middle + (lost + flipped(lost_other, "core", 1)) + down_bias).astype(BF16)
+    second_back, back_other, grads, up_bias_grad = feed_down(
+        places, cotangent, cot_got, second, got, slope, gathered, grads, seq, tp
+    )
+    qkv_full = shards(qkv_turned, qkv_piece, seq_place)
+    shares = [
+        qkv_full[:, cut].reshape(-1, width) for cut in (slice(0, 3 * PAIR), slice(3 * PAIR, None))
+    ]
+    back_other, grads = tied(back_other, grads)
+    second_back = second_back + flipped(back_other, "core", 1)
+    grads = lax.psum_scatter(
+        grads.reshape((-1,) + grads.shape[2:]), ("run", "tp"), scatter_dimension=0, tiled=True
+    )[0]
 
     upstream = cotangent.astype(F32)
     middle_back = upstream + norm_back(second_back, second_gain, second_hat, second_inverse)
@@ -756,9 +804,6 @@
     mixing_grad = mixing_grad.reshape(seq, part, tp, own).transpose(2, 0, 1, 3)
     mixing_sum = Scatter(mixing_grad[:, : seq // 2], mixing_grad[:, seq // 2 :], -1)
 
-    returned[0], ready_down, ready_up = tied(returned[0], down_sum.merge(), up_sum.merge())
-    down_sum.send(ready_down)
-    up_sum.send(ready_up)
     halves = []
     for pair in range(2):
         _, (v, vcol) = values_of(pair)
@@ -767,10 +812,10 @@
             meta, start, qkv, pair, early, pair, v, vcol, returned[pair], turned, logs, tokens, tp
         )
         halves.append((dq, dk, dv, along(gone, -1)))
-    halves[0], ready_down, ready_mixing = tied(halves[0], down_sum.merge(), mixing_sum.merge())
-    down_sum.send(ready_down)
+    halves[0], ready_mixing = tied(halves[0], mixing_sum.merge())
     mixing_sum.send(ready_mixing)
     packets, column_sums, pieces = [], [], []
+    weight_grads, wide_grads = [], []
     skip_gradient = None
     for pair in range(2):
         (v, vcol), _ = values_of(pair)
@@ -780,33 +825,34 @@
             *halves[pair], pair == 0, tokens, tp,
         )
         if pair == 0:
-            halves[1], packed, ready_up, ready_mixing = tied(
-                halves[1], packed, up_sum.merge(), mixing_sum.merge()
-            )
-            up_sum.send(ready_up)
+            halves[1], packed, ready_mixing = tied(halves[1], packed, mixing_sum.merge())
             mixing_sum.send(ready_mixing)
         else:
             skip_gradient = values
-            packed, sums, ready_up, ready_mixing = tied(
-                packed, sums, up_sum.merge(), mixing_sum.merge()
-            )
-        packets.append(packed)
+            packed, sums, ready_mixing = tied(packed, sums, mixing_sum.merge())
+            mixing_sum.send(ready_mixing)
         column_sums.append(sums[0])
         blocks = packed.reshape(tp, rows, packed.shape[1])
         pieces.append([blocks[0]] + [around(blocks[k], k) for k in range(1, tp)])
-    up_sum.send(ready_up)
-    mixing_sum.send(ready_mixing)
+        wide_grads.append(tn(normed, packed))
+        weight_grads.append(
+            scatter_seq(wide_grads[pair].astype(BF16).reshape(seq, part, -1), seq_place)
+        )
     first_back = nn(jnp.concatenate(pieces[0], axis=1), shares[0])
     first_back = first_back + nn(jnp.concatenate(pieces[1], axis=1), shares[1])
-    down_gradient = down_sum.result().T
-    up_gradient = up_sum.result()
     mixing_gradient = mixing_sum.result().T
 
+    cut = grads.reshape(grads.shape[0], 2, part, PAIR)
+    kept = pick(cut, core, 1)
+    came = flipped(pick(cut, 1 - core, 1), "core", 1)
+    ordered = jnp.stack((jnp.where(core == 0, kept, came), jnp.where(core == 0, came, kept)))
+    ordered = ordered.astype(F32).reshape(2, 2, -1, part, PAIR)
+    down_gradient = ordered[:, 0].transpose(0, 1, 3, 2).reshape(-1, part)
+    up_gradient = ordered[:, 1].transpose(2, 0, 1, 3).reshape(part, -1)
+
     stream_gradient = middle_back + norm_back(first_back, first_gain, first_hat, first_inverse)
-    wide_grad = jnp.concatenate([tn(normed, packed) for packed in packets], axis=1)
-    weight_grad = scatter_seq(
-        wide_grad.astype(BF16).reshape(seq, part, wide_grad.shape[1]), seq_place
-    ).astype(F32)
+    wide_grad = jnp.concatenate(wide_grads, axis=1)
+    weight_grad = jnp.concatenate(weight_grads, axis=1).astype(F32)
     query_gradient = jnp.concatenate(
         (weight_grad[:, :PAIR], weight_grad[:, 3 * PAIR : 4 * PAIR]), axis=1
     )
@@ -835,23 +881,29 @@
             offset += value.shape[0]
         return cuts
 
-    up_bias_grad = up_bias_grad.reshape(tp, width)
-    up_bias_grad = jnp.concatenate([pick(up_bias_grad, (k - tp_place) % tp, 0) for k in range(tp)])
+    up_bias_grad = up_bias_grad.reshape(tp, UNIT)
+    zero = jnp.zeros((UNIT,), F32)
+    up_parts = []
+    for k in range(tp):
+        made_here = pick(up_bias_grad, (k - tp_place) % tp, 0)
+        up_parts += [jnp.where(core == 0, made_here, zero), jnp.where(core == 0, zero, made_here)]
+    up_bias_grad = jnp.concatenate(up_parts)
     query_part = jnp.concatenate((column_sum[:PAIR], column_sum[3 * PAIR : 4 * PAIR]))
-    (
-        second_gain_grad, second_shift_grad, mixing_bias_grad, down_bias_grad, up_bias_grad,
-        first_gain_grad, first_shift_grad, query_bias_grad, value_bias_grad,
-    ) = total(
+    first_gain_grad, first_shift_grad, query_bias_grad, value_bias_grad = total(
+        [
+            first_gain_part,
+            first_shift_part,
+            widen(query_part),
+            widen(column_sum[2 * PAIR : 3 * PAIR]),
+        ]
+    )
+    second_gain_grad, second_shift_grad, mixing_bias_grad, down_bias_grad, up_bias_grad = total(
         [
             jnp.sum(second_back * second_hat, axis=0),
             jnp.sum(second_back, axis=0),
             jnp.sum(middle_back, axis=0),
             jnp.sum(upstream, axis=0),
             up_bias_grad,
-            first_gain_part,
-            first_shift_part,
-            widen(query_part),
-            widen(column_sum[2 * PAIR : 3 * PAIR]),
         ]
     )
     return (
@@ -877,15 +929,18 @@
 
 
 def solution(mesh):
-    split = P(("seq", "tp"), None)
+    seq, tp = mesh.shape["seq"], mesh.shape["tp"]
+    mesh = jax.sharding.Mesh(mesh.devices.reshape(seq // 2, 2, tp), SEQ + ("tp",))
+    split = P(SEQ + ("tp",), None)
     column = P(None, "tp")
+    tile = P(SEQ, "tp")
+    turned = P("tp", SEQ)
     in_specs = (
-        split, P(), P("seq", "tp"), P(), P(), column, P("tp"), column, column, P("tp"),
+        split, P(), tile, P(), P(), column, P("tp"), column, column, P("tp"),
         P("tp", None), P(), P(), P(), column, P("tp"), P("tp", None), P(), split,
     )
-    tile = P("seq", "tp")
     out_specs = (
-        split, split, tile, tile, P(), tile, tile, P(), P("tp", "seq"), P(), P(), P(), P(), P(),
-        tile, P(), P("tp", "seq"), P(),
+        split, split, tile, tile, P(), tile, tile, P(), turned, P(), P(), P(), P(), P(),
+        tile, P(), turned, P(),
     )
     return jax.shard_map(local, mesh=mesh, in_specs=in_specs, out_specs=out_specs, check_vma=False)

time: 647 us -> 685 us (1.059)
  waiting for transfers between devices: 188 us -> 211 us
  local copies, waits for them, and re-layouts: 106 us -> 89.8 us
  Pallas kernels: 132 us -> 147 us
  starting transfers between devices: 119 us -> 129 us
    convert_element_type x23 -> x13, other arithmetic: 35.6 us -> 7.75 us  [joined(): return (a.astype(F32) + b.astype(F32)).astype(BF16)]
    unnamed x207 -> x117, local copies, waits for them, and re-layouts: 37 us -> 19.3 us
    ppermute x33, waiting for transfers between devices: 136 us -> 153 us  [around(): lax.ppermute(value, 'tp', [(i, (i + steps) % count) for i in range(count)])]
    ppermute x33, starting transfers between devices: 77.4 us -> 92.3 us  [around(): lax.ppermute(value, 'tp', [(i, (i + steps) % count) for i in range(count)])]
    another operation x0 -> x4, local copies, waits for them, and re-layouts: none -> 14.9 us  [the longest x2 12.4 us: swapped(): jnp.stack((jnp.where(low, value, other), jnp.where(low, other, value)), a...]
    another operation x1 -> x11, other arithmetic: 0.58 us -> 14.8 us  [the longest x8 12.7 us: swapped(): jnp.stack((jnp.where(low, value, other), jnp.where(low, other, value)), a...]
    slice x5 -> x0, local copies, waits for them, and re-layouts: 14 us -> none  [the longest x2 7.92 us: __init__(): kept[cut:]]
    pallas_call x4, Pallas kernels: 29.3 us -> 37.1 us  [attend(): pl.pallas_call(functools.partial(attend_kernel, base, shift), grid_spec=p...]
  transfers between devices with their start and end apart: 62 -> 69, of which waited for: 19 -> 22; matrix products, arithmetic and copies ran while one was open for 26% -> 23% of each run, Pallas kernels for 21% -> 15%
where the time goes in v3:
time: 685 us; the launch traced here: 673 us
  waiting for transfers between devices  211 us (31%)
  Pallas kernels  147 us (21%)
  starting transfers between devices  129 us (19%)
  local copies, waits for them, and re-layouts  89.8 us (13%)
  other arithmetic  65.6 us (10%)
  between operations  15.7 us (2%)
  matrix products  14.6 us (2%)
    ppermute x33, waiting for transfers between devices, around(): lax.ppermute(value, 'tp', [(i, (i + steps) % count) for i in range(count)])  153 us
    ppermute x33, starting transfers between devices, around(): lax.ppermute(value, 'tp', [(i, (i + steps) % count) for i in range(count)])  92.3 us
    ppermute x30, waiting for transfers between devices, flipped(): return lax.ppermute(value, axis, [(i, i ^ bit) for i in range(count)])  57.6 us
    pallas_call x4, Pallas kernels, attend(): pl.pallas_call(functools.partial(attend_kernel, base, shift), grid_spec=p...  37.1 us
    ppermute x30, starting transfers between devices, flipped(): return lax.ppermute(value, axis, [(i, i ^ bit) for i in range(count)])  28.5 us
    pallas_call x1, Pallas kernels, feed_up(): pl.pallas_call(up_kernel, grid_spec=pltpu.PrefetchScalarGridSpec(num_scal...  25.7 us
    pallas_call x2, Pallas kernels, back_late(): pl.pallas_call(functools.partial(late_kernel, base, fresh, per, count), g...  25.2 us
    pallas_call x1, Pallas kernels, feed_down(): pl.pallas_call(down_kernel, grid_spec=pltpu.PrefetchScalarGridSpec(num_sc...  22.9 us
  transfers between devices with their start and end apart: 69, of which 22 were waited for; matrix products, arithmetic and copies ran while one was open for 23% of the time, Pallas kernels for 15%

profile of v3, /device:TPU:0, one launch (start us, length us, event | category | flops | bytes accessed | tf_op | source)
XLA Modules:
  0.0 672.5 jit_solution(11118312901790066527)
XLA Ops:
  11.9 3.1 collective-permute-start
  16.9 23.6 %collective-permute-done.piece_ref = bf16[512,1024]{1,0:T(8,128)(2,1)} collective-permute-done((bf16[512,1024]{1,0:T(8,128)(2,1)}, bf16[512,1024]{1,0:T(8,128)(2,1)}, u32[]{:S(2)}, u32[]{:S(2)}) %collective-permute-start) | collective-permute-done | bytes 1048608 | tf_op jit(solution)/shard_map/ppermute | solution.py:522
  43.7 3.1 collective-permute-start.3
  60.0 2.5 convert_reduce_fusion
  66.2 30.8 %collective-permute-done.1.piece_ref = bf16[512,1024]{1,0:T(8,128)(2,1)} collective-permute-done((bf16[512,1024]{1,0:T(8,128)(2,1)}, bf16[512,1024]{1,0:T(8,128)(2,1)}, u32[]{:S(2)}, u32[]{:S(2)}) %collective-permute-start.1) | collective-permute-done | bytes 1048608 | tf_op jit(solution)/shard_map/ppermute | solution.py:522
  97.1 10.0 %collective-permute-start.2 = (bf16[512,1024]{1,0:T(8,128)(2,1)}, bf16[512,1024]{1,0:T(8,128)(2,1)}, u32[]{:S(2)}, u32[]{:S(2)}) collective-permute-start(bf16[512,1024]{1,0:T(8,128)(2,1)} %collective-permute-done.1.piece_ref), channel_id=1, source_target_pairs={{0,1},{1,2},{2,3},{3,0},{4,5},{5,6},{6,7},{7,4},{8,9},{9,10},{10,1... | collective-permute-start | bytes 3145736 | tf_op jit(solution)/shard_map/ppermute | solution.py:522
  111.5 4.1 project.4
  115.7 14.0 %collective-permute-done.6 = f32[1024]{0:T(1024)} collective-permute-done((f32[1024]{0:T(1024)}, f32[1024]{0:T(1024)}, u32[]{:S(2)}, u32[]{:S(2)}) %collective-permute-start.6) | collective-permute-done | bytes 4128 | tf_op jit(solution)/shard_map/ppermute | solution.py:522
  132.9 4.1 project.5
  137.1 3.0 maximum_bitcast_fusion
  140.1 4.1 project.6
  144.2 3.1 collective-permute-start.15
  150.4 4.1 project.7
  159.2 6.0 collective-permute-done.16
  166.9 10.3 %attend.4 = (bf16[2048,128]{1,0:T(8,128)(2,1)}, f32[128,2048]{1,0:T(8,128)}, f32[8,2048]{1,0:T(8,128)}) custom-call(s32[10]{0:T(128)} %pad_add_fusion.meta_ref, s32[1,2048]{1,0:T(1,128)} %bitcast.249, bf16[2048,640]{1,0:T(8,128)(2,1)} %get-tuple-element.117.q_ref.k_ref.v_ref, bf16[2048,640]{1,0:T(8,128)(2,1)} %get-tuple-element.117.q_ref.k_ref.v_ref, ...), custom_call_target="tpu_custom_call" | custom-call | flops 1 | bytes 1048576 | tf_op jit(solution)/shard_map/attend/pallas_call | solution.py:163
  177.1 10.3 %attend.6 = (bf16[2048,128]{1,0:T(8,128)(2,1)}, f32[128,2048]{1,0:T(8,128)}, f32[8,2048]{1,0:T(8,128)}) custom-call(s32[10]{0:T(128)} %pad_add_fusion.meta_ref, s32[1,2048]{1,0:T(1,128)} %bitcast.250, bf16[2048,640]{1,0:T(8,128)(2,1)} %get-tuple-element.117.q_ref.k_ref.v_ref, bf16[2048,640]{1,0:T(8,128)(2,1)} %get-tuple-element.117.q_ref.k_ref.v_ref, ...), custom_call_target="tpu_custom_call" | custom-call | flops 1 | bytes 1048576 | tf_op jit(solution)/shard_map/attend/pallas_call | solution.py:163
  190.1 8.3 %attend.5 = (bf16[2048,128]{1,0:T(8,128)(2,1)}, f32[128,2048]{1,0:T(8,128)}, f32[8,2048]{1,0:T(8,128)}) custom-call(s32[10]{0:T(128)} %pad_add_fusion.meta_ref, s32[1,2048]{1,0:T(1,128)} %bitcast.251, bf16[2048,640]{1,0:T(8,128)(2,1)} %get-tuple-element.117.q_ref.k_ref.v_ref, ...), custom_call_target="tpu_custom_call", output_to_operand_aliasing={{0}: (5, {}), {1}: (6, {}), {2}: (7, {})} | custom-call | flops 1 | bytes 1048576 | tf_op jit(solution)/shard_map/attend/pallas_call | solution.py:163
  200.2 10.0 %collective-permute-start.9 = (bf16[512,128]{1,0:T(8,128)(2,1)S(1)}, bf16[512,128]{1,0:T(8,128)(2,1)S(1)}, u32[]{:S(2)}, u32[]{:S(2)}) collective-permute-start(bf16[512,128]{1,0:T(8,128)(2,1)S(1)} %get-tuple-element.259), channel_id=1, source_target_pairs={{0,1},{1,2},{2,3},{3,0},{4,5},{5,6},{6,7},{7,4},{8,9},{9,10},{10,1... | collective-permute-start | bytes 393224 | tf_op jit(solution)/shard_map/ppermute | solution.py:522
  210.2 8.3 %attend.7 = (bf16[2048,128]{1,0:T(8,128)(2,1)}, f32[128,2048]{1,0:T(8,128)}, f32[8,2048]{1,0:T(8,128)}) custom-call(s32[10]{0:T(128)} %pad_add_fusion.meta_ref, s32[1,2048]{1,0:T(1,128)} %bitcast.252, bf16[2048,640]{1,0:T(8,128)(2,1)} %get-tuple-element.117.q_ref.k_ref.v_ref, ...), custom_call_target="tpu_custom_call", output_to_operand_aliasing={{0}: (5, {}), {1}: (6, {}), {2}: (7, {})} | custom-call | flops 1 | bytes 1048576 | tf_op jit(solution)/shard_map/attend/pallas_call | solution.py:163
  220.4 3.2 collective-permute-start.11
  223.7 3.5 collective-permute-start.13
  230.2 5.9 collective-permute-done.11
  240.2 3.8 collective-permute-done.14
  252.0 3.9 copy.126.cot_ref
  255.9 25.7 %feed_up.1 = (f32[512,1024]{1,0:T(8,128)}, f32[512,1024]{1,0:T(8,128)}, f32[1024,2048]{1,0:T(8,128)}, bf16[4,4,8,256,128]{4,3,2,1,0:T(8,128)(2,1)}) custom-call(s32[2]{0:T(128)} %pad_add_fusion.1.place_ref.places_ref, bf16[512,1024]{1,0:T(8,128)(2,1)} %add_convert_fusion.1.sn_ref, bf16[512,1024]{1,0:T(8,128)(2,1)} %collective-permute-done.20.got_ref, ...), custom_call_target="tpu_custom_call" | custom-call | flops 1 | bytes 8388608 | tf_op jit(solution)/shard_map/feed_up/pallas_call | solution.py:428
  281.7 22.9 %feed_down.1 = (f32[512,1024]{1,0:T(8,128)}, f32[512,1024]{1,0:T(8,128)}, bf16[4,4,8,256,128]{4,3,2,1,0:T(8,128)(2,1)}, f32[4,1,512]{2,1,0:T(1,128)}) custom-call(s32[2]{0:T(128)} %pad_add_fusion.1.place_ref.places_ref, bf16[512,1024]{1,0:T(8,128)(2,1)} %cot_ref, ...), custom_call_target="tpu_custom_call", output_to_operand_aliasing={{2}: (8, {})} | custom-call | flops 1 | bytes 8388608 | tf_op jit(solution)/shard_map/feed_down/pallas_call | solution.py:485
  307.4 3.2 collective-permute-start.38
  311.4 11.8 %collective-permute-done.37 = bf16[160,1024]{0,1:T(8,128)(2,1)S(1)} collective-permute-done((bf16[160,1024]{0,1:T(8,128)(2,1)}, bf16[160,1024]{0,1:T(8,128)(2,1)S(1)}, u32[]{:S(2)}, u32[]{:S(2)}) %collective-permute-start.37) | collective-permute-done | bytes 327712 | tf_op jit(solution)/shard_map/ppermute | solution.py:522
  323.2 21.9 %collective-permute-done.38 = bf16[160,1024]{0,1:T(8,128)(2,1)S(1)} collective-permute-done((bf16[160,1024]{0,1:T(8,128)(2,1)}, bf16[160,1024]{0,1:T(8,128)(2,1)S(1)}, u32[]{:S(2)}, u32[]{:S(2)}) %collective-permute-start.38) | collective-permute-done | bytes 327712 | tf_op jit(solution)/shard_map/ppermute | solution.py:522
  350.0 2.5 copy.143
  353.2 22.1 %collective-permute-done.40 = bf16[3,160,1024]{2,1,0:T(8,128)(2,1)} collective-permute-done((bf16[3,160,1024]{2,1,0:T(8,128)(2,1)}, bf16[3,160,1024]{2,1,0:T(8,128)(2,1)}, u32[]{:S(2)}, u32[]{:S(2)}) %collective-permute-start.40) | collective-permute-done | bytes 983072 | tf_op jit(solution)/shard_map/ppermute | solution.py:527
  375.3 2.5 copy.137
  384.1 4.5 copy.139
  388.5 3.3 multiply_reduce_fusion
  392.0 3.4 fusion.57
  403.8 2.8 reshape.228
  406.5 3.2 copy.135
  412.6 21.0 %collective-permute-start.27 = (bf16[512,128]{1,0:T(8,128)(2,1)S(1)}, bf16[512,128]{1,0:T(8,128)(2,1)S(1)}, u32[]{:S(2)}, u32[]{:S(2)}) collective-permute-start(bf16[512,128]{1,0:T(8,128)(2,1)S(1)} %get-tuple-element.236), channel_id=1, source_target_pairs={{0,3},{1,0},{2,1},{3,2},{4,7},{5,4},{6,5},{7,6},{8,11},{9,8},{10,9... | collective-permute-start | bytes 393224 | tf_op jit(solution)/shard_map/ppermute | solution.py:522
  435.0 3.3 collective-permute-done.63
  438.3 3.1 collective-permute-start.23
  442.6 10.7 %collective-permute-done.28 = bf16[512,128]{1,0:T(8,128)(2,1)S(1)} collective-permute-done((bf16[512,128]{1,0:T(8,128)(2,1)S(1)}, bf16[512,128]{1,0:T(8,128)(2,1)S(1)}, u32[]{:S(2)}, u32[]{:S(2)}) %collective-permute-start.28) | collective-permute-done | bytes 131104 | tf_op jit(solution)/shard_map/ppermute | solution.py:522
  453.5 10.9 %collective-permute-start.64 = (f32[64,128]{1,0:T(8,128)S(1)}, f32[64,128]{1,0:T(8,128)S(1)}, u32[]{:S(2)}, u32[]{:S(2)}) collective-permute-start(f32[64,128]{1,0:T(8,128)S(1)} %add.378), channel_id=1, source_target_pairs={{0,1},{1,0},{2,3},{3,2},{4,5},{5,4},{6,7},{7,6},{8,9},{9,8},{10,11... | collective-permute-start | bytes 98312 | tf_op jit(solution)/shard_map/ppermute | solution.py:527
  465.3 9.7 %back_early.3 = (bf16[1024,128]{1,0:T(8,128)(2,1)}, bf16[1024,256]{1,0:T(8,128)(2,1)}, f32[1024,128]{1,0:T(8,128)}, f32[1024,128]{1,0:T(8,128)}) custom-call(s32[10]{0:T(128)} %pad_add_fusion.meta_ref, s32[1,2048]{1,0:T(1,128)} %bitcast.253, bf16[2048,640]{1,0:T(8,128)(2,1)} %get-tuple-element.117.q_ref.k_ref.v_ref, ...), custom_call_target="tpu_custom_call" | custom-call | flops 1 | bytes 3145728 | tf_op jit(solution)/shard_map/back_early/pallas_call | solution.py:299
  481.0 9.7 %back_early.2 = (bf16[1024,128]{1,0:T(8,128)(2,1)}, bf16[1024,256]{1,0:T(8,128)(2,1)}, f32[1024,128]{1,0:T(8,128)}, f32[1024,128]{1,0:T(8,128)}) custom-call(s32[10]{0:T(128)} %pad_add_fusion.meta_ref, s32[1,2048]{1,0:T(1,128)} %bitcast.254, bf16[2048,640]{1,0:T(8,128)(2,1)} %get-tuple-element.117.q_ref.k_ref.v_ref, ...), custom_call_target="tpu_custom_call" | custom-call | flops 1 | bytes 3145728 | tf_op jit(solution)/shard_map/back_early/pallas_call | solution.py:299
  498.3 3.4 collective-permute-start.33
  501.9 12.6 %back_late.2 = (bf16[2048,384]{1,0:T(8,128)(2,1)}, f32[8,128]{1,0:T(8,128)}, f32[8,384]{1,0:T(8,128)}) custom-call(s32[10]{0:T(128)} %pad_add_fusion.meta_ref, s32[1,2048]{1,0:T(1,128)} %bitcast.255, bf16[2048,640]{1,0:T(8,128)(2,1)} %get-tuple-element.117.q_ref.k_ref.v_ref, bf16[2048,640]{1,0:T(8,128)(2,1)} %get-tuple-element.117.q_ref.k_ref.v_ref, ...), custom_call_target="tpu_custom_call" | custom-call | flops 1 | bytes 3145728 | tf_op jit(solution)/shard_map/back_late/pallas_call | solution.py:335
  517.2 4.6 copy.140
  521.8 2.8 select_bitcast_fusion.1
  524.6 3.8 pad_maximum_fusion
  528.4 8.0 %copy.142 = bf16[3,2,2,160,1024]{4,3,2,1,0:T(8,128)(2,1)} copy(bf16[3,2,2,160,1024]{3,4,0,1,2:T(8,128)(2,1)} %pad_maximum_fusion) | data formatting | bytes 7864320 | tf_op jit(solution)/shard_map/stack | solution.py:639
  536.3 3.3 fusion
  550.0 12.7 %back_late.3 = (bf16[2048,256]{1,0:T(8,128)(2,1)}, f32[2048,128]{1,0:T(8,128)}, f32[8,256]{1,0:T(8,128)}) custom-call(s32[10]{0:T(128)} %pad_add_fusion.meta_ref, s32[1,2048]{1,0:T(1,128)} %bitcast.256, bf16[2048,640]{1,0:T(8,128)(2,1)} %get-tuple-element.117.q_ref.k_ref.v_ref, bf16[2048,640]{1,0:T(8,128)(2,1)} %get-tuple-element.117.q_ref.k_ref.v_ref, ...), custom_call_target="tpu_custom_call" | custom-call | flops 1 | bytes 3145728 | tf_op jit(solution)/shard_map/back_late/pallas_call | solution.py:335
  565.2 3.8 fusion.69
  569.0 2.7 fusion.1
  572.9 7.2 %collective-permute-start.59 = (bf16[128,256]{0,1:T(8,128)(2,1)S(1)}, bf16[128,256]{0,1:T(8,128)(2,1)S(1)}, u32[]{:S(2)}, u32[]{:S(2)}) collective-permute-start(bf16[128,256]{0,1:T(8,128)(2,1)S(1)} %get-tuple-element.270), channel_id=1, source_target_pairs={{0,2},{1,3},{2,0},{3,1},{4,6},{5,7},{6,4},{7,5},{8,10},{9,11},{10,... | collective-permute-start | bytes 196616 | tf_op jit(solution)/shard_map/ppermute | solution.py:522
  580.2 2.9 collective-permute-start.55
  583.1 3.8 collective-permute-start.58
  587.1 3.6 collective-permute-done.56
  595.1 23.6 %collective-permute-done.57 = f32[28,128]{1,0:T(8,128)S(1)} collective-permute-done((f32[28,128]{1,0:T(8,128)S(1)}, f32[28,128]{1,0:T(8,128)S(1)}, u32[]{:S(2)}, u32[]{:S(2)}) %collective-permute-start.57) | collective-permute-done | bytes 14368 | tf_op jit(solution)/shard_map/ppermute | solution.py:527
  621.8 3.1 collective-permute-start.46
  625.0 4.8 collective-permute-done.44
  629.8 10.1 %collective-permute-done.45 = bf16[512,256]{1,0:T(8,128)(2,1)S(1)} collective-permute-done((bf16[512,256]{1,0:T(8,128)(2,1)S(1)}, bf16[512,256]{1,0:T(8,128)(2,1)S(1)}, u32[]{:S(2)}, u32[]{:S(2)}) %collective-permute-start.45) | collective-permute-done | bytes 262176 | tf_op jit(solution)/shard_map/ppermute | solution.py:522
  643.2 4.9 collective-permute-done.36
  654.7 2.8 collective-permute-done.52
  (351 shorter events, 151.4 us)
Async XLA Ops:
  7.2 248.7 %all-gather.3.cloned.1.call-start = ((), (), s32[]{:S(2)}) async-start(), calls=%async_computation.2 | async-start | bytes 17301504 | tf_op jit(solution)/shard_map/all_gather | solution.py:738
  11.9 28.5 %collective-permute-start = (bf16[512,1024]{1,0:T(8,128)(2,1)}, bf16[512,1024]{1,0:T(8,128)(2,1)}, u32[]{:S(2)}, u32[]{:S(2)}) collective-permute-start(bf16[512,1024]{1,0:T(8,128)(2,1)} %fusion.10.piece_ref), channel_id=1, source_target_pairs={{0,1},{1,2},{2,3},{3,0},{4,5},{5,6},{6,7},{7,4},{8,9},{9,10},{10,1... | collective-permute-start | bytes 3145736 | tf_op jit(solution)/shard_map/ppermute | solution.py:522
  40.5 618.2 %reduce-scatter.2.cloned.1.call-start = ((), (), s32[]{:S(2)}) async-start(), calls=%async_computation.1 | async-start | bytes 8912896 | tf_op jit(solution)/shard_map/reduce_scatter | solution.py:790
  40.5 68.4 %collective-permute-start.4 = (f32[1024]{0:T(1024)}, f32[1024]{0:T(1024)}, u32[]{:S(2)}, u32[]{:S(2)}) collective-permute-start(f32[1024]{0:T(1024)} %param.34), channel_id=1, source_target_pairs={{0,1},{1,2},{2,3},{3,0},{4,5},{5,6},{6,7},{7,4},{8,9},{9,10},{10,1... | collective-permute-start | bytes 12296 | tf_op jit(solution)/shard_map/ppermute | solution.py:522
  40.6 75.1 %collective-permute-start.5 = (f32[1024]{0:T(1024)}, f32[1024]{0:T(1024)}, u32[]{:S(2)}, u32[]{:S(2)}) collective-permute-start(f32[1024]{0:T(1024)} %param.34), channel_id=1, source_target_pairs={{0,2},{1,3},{2,0},{3,1},{4,6},{5,7},{6,4},{7,5},{8,10},{9,11},{10,... | collective-permute-start | bytes 12296 | tf_op jit(solution)/shard_map/ppermute | solution.py:522
  42.9 94.2 %collective-permute-start.7 = (bf16[512,1024]{1,0:T(8,128)(2,1)S(1)}, bf16[512,1024]{1,0:T(8,128)(2,1)}, u32[]{:S(2)}, u32[]{:S(2)}) collective-permute-start(bf16[512,1024]{1,0:T(8,128)(2,1)S(1)} %copy-done.10), channel_id=1, source_target_pairs={{0,4},{4,0},{1,5},{5,1},{2,6},{6,2},{3,7},{7,3},{8,12},{12,8},{9,1... | collective-permute-start | bytes 3145736 | tf_op jit(solution)/shard_map/ppermute | solution.py:527
  43.7 87.3 %collective-permute-start.3 = (bf16[1024,128]{1,0:T(8,128)(2,1)}, bf16[1024,128]{1,0:T(8,128)(2,1)}, u32[]{:S(2)}, u32[]{:S(2)}) collective-permute-start(bf16[1024,128]{1,0:T(8,128)(2,1)} %get-tuple-element.261), channel_id=1, source_target_pairs={{0,4},{4,8},{8,12},{12,16},{16,20},{20,24},{24,28},{1,5},{5,9},{9,... | collective-permute-start | bytes 786440 | tf_op jit(solution)/shard_map/ppermute | solution.py:533
  56.2 40.8 %collective-permute-start.1 = (bf16[512,1024]{1,0:T(8,128)(2,1)}, bf16[512,1024]{1,0:T(8,128)(2,1)}, u32[]{:S(2)}, u32[]{:S(2)}) collective-permute-start(bf16[512,1024]{1,0:T(8,128)(2,1)} %collective-permute-done.piece_ref), channel_id=1, source_target_pairs={{0,1},{1,2},{2,3},{3,0},{4,5},{5,6},{6,7},{7,4},{8,9},{9,10},{10,1... | collective-permute-start | bytes 3145736 | tf_op jit(solution)/shard_map/ppermute | solution.py:522
  97.1 47.2 %collective-permute-start.2 = (bf16[512,1024]{1,0:T(8,128)(2,1)}, bf16[512,1024]{1,0:T(8,128)(2,1)}, u32[]{:S(2)}, u32[]{:S(2)}) collective-permute-start(bf16[512,1024]{1,0:T(8,128)(2,1)} %collective-permute-done.1.piece_ref), channel_id=1, source_target_pairs={{0,1},{1,2},{2,3},{3,0},{4,5},{5,6},{6,7},{7,4},{8,9},{9,10},{10,1... | collective-permute-start | bytes 3145736 | tf_op jit(solution)/shard_map/ppermute | solution.py:522
  109.0 20.7 %collective-permute-start.6 = (f32[1024]{0:T(1024)}, f32[1024]{0:T(1024)}, u32[]{:S(2)}, u32[]{:S(2)}) collective-permute-start(f32[1024]{0:T(1024)} %param.34), channel_id=1, source_target_pairs={{0,3},{1,0},{2,1},{3,2},{4,7},{5,4},{6,5},{7,6},{8,11},{9,8},{10,9... | collective-permute-start | bytes 12296 | tf_op jit(solution)/shard_map/ppermute | solution.py:522
  144.2 14.9 %collective-permute-start.15 = (bf16[64,1024]{1,0:T(8,128)(2,1)S(1)}, bf16[64,1024]{1,0:T(8,128)(2,1)S(1)}, u32[]{:S(2)}, u32[]{:S(2)}) collective-permute-start(bf16[64,1024]{1,0:T(8,128)(2,1)S(1)} %constant_dynamic-slice_fusion.16), channel_id=1, source_target_pairs={{0,1},{1,2},{2,3},{3,0},{4,5},{5,6},{6,7},{7,4},{8,9},{9,10},{10,1... | collective-permute-start | bytes 393224 | tf_op jit(solution)/shard_map/ppermute | solution.py:522
  147.4 17.8 %collective-permute-start.16 = (bf16[64,1024]{1,0:T(8,128)(2,1)S(1)}, bf16[64,1024]{1,0:T(8,128)(2,1)S(1)}, u32[]{:S(2)}, u32[]{:S(2)}) collective-permute-start(bf16[64,1024]{1,0:T(8,128)(2,1)S(1)} %constant_dynamic-slice_fusion.16), channel_id=1, source_target_pairs={{0,2},{1,3},{2,0},{3,1},{4,6},{5,7},{6,4},{7,5},{8,10},{9,11},{10,... | collective-permute-start | bytes 393224 | tf_op jit(solution)/shard_map/ppermute | solution.py:522
  149.3 15.8 %collective-permute-start.17 = (bf16[64,1024]{1,0:T(8,128)(2,1)S(1)}, bf16[64,1024]{1,0:T(8,128)(2,1)S(1)}, u32[]{:S(2)}, u32[]{:S(2)}) collective-permute-start(bf16[64,1024]{1,0:T(8,128)(2,1)S(1)} %constant_dynamic-slice_fusion.16), channel_id=1, source_target_pairs={{0,3},{1,0},{2,1},{3,2},{4,7},{5,4},{6,5},{7,6},{8,11},{9,8},{10,9... | collective-permute-start | bytes 393224 | tf_op jit(solution)/shard_map/ppermute | solution.py:522
  157.0 30.7 %collective-permute-start.8 = (bf16[1024,384]{1,0:T(8,128)(2,1)}, bf16[1024,384]{1,0:T(8,128)(2,1)}, u32[]{:S(2)}, u32[]{:S(2)}) collective-permute-start(bf16[1024,384]{1,0:T(8,128)(2,1)} %get-tuple-element.201), channel_id=1, source_target_pairs={{0,4},{4,8},{8,12},{12,16},{16,20},{20,24},{24,28},{1,5},{5,9},{9,... | collective-permute-start | bytes 2359304 | tf_op jit(solution)/shard_map/ppermute | solution.py:533
  165.2 22.2 %collective-permute-start.18 = (bf16[3,64,1024]{2,1,0:T(8,128)(2,1)S(1)}, bf16[3,64,1024]{2,1,0:T(8,128)(2,1)S(1)}, u32[]{:S(2)}, u32[]{:S(2)}) collective-permute-start(bf16[3,64,1024]{2,1,0:T(8,128)(2,1)S(1)} %pad_maximum_fusion.12), channel_id=1, source_target_pairs={{0,8},{4,12},{8,0},{12,4},{16,24},{20,28},{24,16},{28,20},{1,9},{5... | collective-permute-start | bytes 1179656 | tf_op jit(solution)/shard_map/ppermute | solution.py:527
  187.6 57.2 %collective-permute-start.19 = (bf16[3,2,64,1024]{3,2,1,0:T(8,128)(2,1)S(1)}, bf16[3,2,64,1024]{3,2,1,0:T(8,128)(2,1)}, u32[]{:S(2)}, u32[]{:S(2)}) collective-permute-start(bf16[3,2,64,1024]{3,2,1,0:T(8,128)(2,1)S(1)} %pad_maximum_fusion.7), channel_id=1, source_target_pairs={{0,4},{4,0},{8,12},{12,8},{16,20},{20,16},{24,28},{28,24},{1,5},{5... | collective-permute-start | bytes 2359304 | tf_op jit(solution)/shard_map/ppermute | solution.py:527
  200.2 23.4 %collective-permute-start.9 = (bf16[512,128]{1,0:T(8,128)(2,1)S(1)}, bf16[512,128]{1,0:T(8,128)(2,1)S(1)}, u32[]{:S(2)}, u32[]{:S(2)}) collective-permute-start(bf16[512,128]{1,0:T(8,128)(2,1)S(1)} %get-tuple-element.259), channel_id=1, source_target_pairs={{0,1},{1,2},{2,3},{3,0},{4,5},{5,6},{6,7},{7,4},{8,9},{9,10},{10,1... | collective-permute-start | bytes 393224 | tf_op jit(solution)/shard_map/ppermute | solution.py:522
  220.4 8.3 %collective-permute-start.10 = (bf16[512,128]{1,0:T(8,128)(2,1)}, bf16[512,128]{1,0:T(8,128)(2,1)S(1)}, u32[]{:S(2)}, u32[]{:S(2)}) collective-permute-start(bf16[512,128]{1,0:T(8,128)(2,1)} %get-tuple-element.255), channel_id=1, source_target_pairs={{0,1},{1,2},{2,3},{3,0},{4,5},{5,6},{6,7},{7,4},{8,9},{9,10},{10,1... | collective-permute-start | bytes 393224 | tf_op jit(solution)/shard_map/ppermute | solution.py:522
  220.4 15.7 %collective-permute-start.11 = (bf16[512,128]{1,0:T(8,128)(2,1)}, bf16[512,128]{1,0:T(8,128)(2,1)S(1)}, u32[]{:S(2)}, u32[]{:S(2)}) collective-permute-start(bf16[512,128]{1,0:T(8,128)(2,1)} %get-tuple-element.258), channel_id=1, source_target_pairs={{0,2},{1,3},{2,0},{3,1},{4,6},{5,7},{6,4},{7,5},{8,10},{9,11},{10,... | collective-permute-start | bytes 393224 | tf_op jit(solution)/shard_map/ppermute | solution.py:522
  223.6 15.3 %collective-permute-start.12 = (bf16[512,128]{1,0:T(8,128)(2,1)}, bf16[512,128]{1,0:T(8,128)(2,1)S(1)}, u32[]{:S(2)}, u32[]{:S(2)}) collective-permute-start(bf16[512,128]{1,0:T(8,128)(2,1)} %get-tuple-element.254), channel_id=1, source_target_pairs={{0,2},{1,3},{2,0},{3,1},{4,6},{5,7},{6,4},{7,5},{8,10},{9,11},{10,... | collective-permute-start | bytes 393224 | tf_op jit(solution)/shard_map/ppermute | solution.py:522
  223.7 15.9 %collective-permute-start.13 = (bf16[512,128]{1,0:T(8,128)(2,1)S(1)}, bf16[512,128]{1,0:T(8,128)(2,1)S(1)}, u32[]{:S(2)}, u32[]{:S(2)}) collective-permute-start(bf16[512,128]{1,0:T(8,128)(2,1)S(1)} %get-tuple-element.257), channel_id=1, source_target_pairs={{0,3},{1,0},{2,1},{3,2},{4,7},{5,4},{6,5},{7,6},{8,11},{9,8},{10,9... | collective-permute-start | bytes 393224 | tf_op jit(solution)/shard_map/ppermute | solution.py:522
  228.7 15.4 %collective-permute-start.14 = (bf16[512,128]{1,0:T(8,128)(2,1)S(1)}, bf16[512,128]{1,0:T(8,128)(2,1)S(1)}, u32[]{:S(2)}, u32[]{:S(2)}) collective-permute-start(bf16[512,128]{1,0:T(8,128)(2,1)S(1)} %get-tuple-element.253), channel_id=1, source_target_pairs={{0,3},{1,0},{2,1},{3,2},{4,7},{5,4},{6,5},{7,6},{8,11},{9,8},{10,9... | collective-permute-start | bytes 393224 | tf_op jit(solution)/shard_map/ppermute | solution.py:522
  304.5 84.0 %collective-permute-start.22 = (f32[512,1024]{1,0:T(8,128)}, f32[512,1024]{1,0:T(8,128)}, u32[]{:S(2)}, u32[]{:S(2)}) collective-permute-start(f32[512,1024]{1,0:T(8,128)} %get-tuple-element.141), channel_id=1, source_target_pairs={{0,4},{4,0},{1,5},{5,1},{2,6},{6,2},{3,7},{7,3},{8,12},{12,8},{9,1... | collective-permute-start | bytes 6291464 | tf_op jit(solution)/shard_map/ppermute | solution.py:527
  305.1 18.1 %collective-permute-start.37 = (bf16[160,1024]{0,1:T(8,128)(2,1)}, bf16[160,1024]{0,1:T(8,128)(2,1)S(1)}, u32[]{:S(2)}, u32[]{:S(2)}) collective-permute-start(bf16[160,1024]{0,1:T(8,128)(2,1)} %dynamic-slice_bitcast_fusion), channel_id=1, source_target_pairs={{0,1},{1,2},{2,3},{3,0},{4,5},{5,6},{6,7},{7,4},{8,9},{9,10},{10,1... | collective-permute-start | bytes 983048 | tf_op jit(solution)/shard_map/ppermute | solution.py:522
  307.4 37.7 %collective-permute-start.38 = (bf16[160,1024]{0,1:T(8,128)(2,1)}, bf16[160,1024]{0,1:T(8,128)(2,1)S(1)}, u32[]{:S(2)}, u32[]{:S(2)}) collective-permute-start(bf16[160,1024]{0,1:T(8,128)(2,1)} %dynamic-slice_bitcast_fusion), channel_id=1, source_target_pairs={{0,2},{1,3},{2,0},{3,1},{4,6},{5,7},{6,4},{7,5},{8,10},{9,11},{10,... | collective-permute-start | bytes 983048 | tf_op jit(solution)/shard_map/ppermute | solution.py:522
  310.6 34.4 %collective-permute-start.39 = (bf16[160,1024]{0,1:T(8,128)(2,1)}, bf16[160,1024]{0,1:T(8,128)(2,1)S(1)}, u32[]{:S(2)}, u32[]{:S(2)}) collective-permute-start(bf16[160,1024]{0,1:T(8,128)(2,1)} %dynamic-slice_bitcast_fusion), channel_id=1, source_target_pairs={{0,3},{1,0},{2,1},{3,2},{4,7},{5,4},{6,5},{7,6},{8,11},{9,8},{10,9... | collective-permute-start | bytes 983048 | tf_op jit(solution)/shard_map/ppermute | solution.py:522
  349.9 25.4 %collective-permute-start.40 = (bf16[3,160,1024]{2,1,0:T(8,128)(2,1)}, bf16[3,160,1024]{2,1,0:T(8,128)(2,1)}, u32[]{:S(2)}, u32[]{:S(2)}) collective-permute-start(bf16[3,160,1024]{2,1,0:T(8,128)(2,1)} %copy.136), channel_id=1, source_target_pairs={{0,8},{4,12},{8,0},{12,4},{16,24},{20,28},{24,16},{28,20},{1,9},{5... | collective-permute-start | bytes 2949128 | tf_op jit(solution)/shard_map/ppermute | solution.py:527
  349.9 42.0 %collective-permute-start.21 = (f32[512,1024]{1,0:T(8,128)}, f32[512,1024]{1,0:T(8,128)}, u32[]{:S(2)}, u32[]{:S(2)}) collective-permute-start(f32[512,1024]{1,0:T(8,128)} %get-tuple-element.134), channel_id=1, source_target_pairs={{0,4},{4,0},{1,5},{5,1},{2,6},{6,2},{3,7},{7,3},{8,12},{12,8},{9,1... | collective-permute-start | bytes 6291464 | tf_op jit(solution)/shard_map/ppermute | solution.py:527
  395.4 15.8 %collective-permute-start.61 = (f32[64,128]{1,0:T(8,128)S(1)}, f32[64,128]{1,0:T(8,128)S(1)}, u32[]{:S(2)}, u32[]{:S(2)}) collective-permute-start(f32[64,128]{1,0:T(8,128)S(1)} %bitcast.258), channel_id=1, source_target_pairs={{0,4},{4,0},{8,12},{12,8},{16,20},{20,16},{24,28},{28,24},{1,5},{5... | collective-permute-start | bytes 98312 | tf_op jit(solution)/shard_map/ppermute | solution.py:527
  410.8 82.6 %collective-permute-start.31 = (bf16[4,4,128,256]{2,3,1,0:T(8,128)(2,1)}, bf16[4,4,128,256]{2,3,1,0:T(8,128)(2,1)}, u32[]{:S(2)}, u32[]{:S(2)}) collective-permute-start(bf16[4,4,128,256]{2,3,1,0:T(8,128)(2,1)} %slice.436), channel_id=1, source_target_pairs={{0,4},{4,0},{8,12},{12,8},{16,20},{20,16},{24,28},{28,24},{1,5},{5... | collective-permute-start | bytes 3145736 | tf_op jit(solution)/shard_map/ppermute | solution.py:527
  411.2 22.9 %collective-permute-start.62 = (f32[64,128]{1,0:T(8,128)S(1)}, f32[64,128]{1,0:T(8,128)S(1)}, u32[]{:S(2)}, u32[]{:S(2)}) collective-permute-start(f32[64,128]{1,0:T(8,128)S(1)} %bitcast_add_fusion), channel_id=1, source_target_pairs={{0,8},{4,12},{8,0},{12,4},{16,24},{20,28},{24,16},{28,20},{1,9},{5... | collective-permute-start | bytes 98312 | tf_op jit(solution)/shard_map/ppermute | solution.py:527
  412.6 28.8 %collective-permute-start.27 = (bf16[512,128]{1,0:T(8,128)(2,1)S(1)}, bf16[512,128]{1,0:T(8,128)(2,1)S(1)}, u32[]{:S(2)}, u32[]{:S(2)}) collective-permute-start(bf16[512,128]{1,0:T(8,128)(2,1)S(1)} %get-tuple-element.236), channel_id=1, source_target_pairs={{0,3},{1,0},{2,1},{3,2},{4,7},{5,4},{6,5},{7,6},{8,11},{9,8},{10,9... | collective-permute-start | bytes 393224 | tf_op jit(solution)/shard_map/ppermute | solution.py:522
  433.6 19.7 %collective-permute-start.28 = (bf16[512,128]{1,0:T(8,128)(2,1)S(1)}, bf16[512,128]{1,0:T(8,128)(2,1)S(1)}, u32[]{:S(2)}, u32[]{:S(2)}) collective-permute-start(bf16[512,128]{1,0:T(8,128)(2,1)S(1)} %get-tuple-element.235), channel_id=1, source_target_pairs={{0,2},{1,3},{2,0},{3,1},{4,6},{5,7},{6,4},{7,5},{8,10},{9,11},{10,... | collective-permute-start | bytes 393224 | tf_op jit(solution)/shard_map/ppermute | solution.py:522
  433.6 19.9 %collective-permute-start.29 = (bf16[512,128]{1,0:T(8,128)(2,1)S(1)}, bf16[512,128]{1,0:T(8,128)(2,1)S(1)}, u32[]{:S(2)}, u32[]{:S(2)}) collective-permute-start(bf16[512,128]{1,0:T(8,128)(2,1)S(1)} %get-tuple-element.234), channel_id=1, source_target_pairs={{0,1},{1,2},{2,3},{3,0},{4,5},{5,6},{6,7},{7,4},{8,9},{9,10},{10,1... | collective-permute-start | bytes 393224 | tf_op jit(solution)/shard_map/ppermute | solution.py:522
  438.3 36.8 %collective-permute-start.23 = (bf16[512,128]{1,0:T(8,128)(2,1)}, bf16[512,128]{1,0:T(8,128)(2,1)}, u32[]{:S(2)}, u32[]{:S(2)}) collective-permute-start(bf16[512,128]{1,0:T(8,128)(2,1)} %get-tuple-element.239), channel_id=1, source_target_pairs={{0,3},{1,0},{2,1},{3,2},{4,7},{5,4},{6,5},{7,6},{8,11},{9,8},{10,9... | collective-permute-start | bytes 393224 | tf_op jit(solution)/shard_map/ppermute | solution.py:522
  441.4 37.0 %collective-permute-start.24 = (bf16[512,128]{1,0:T(8,128)(2,1)}, bf16[512,128]{1,0:T(8,128)(2,1)}, u32[]{:S(2)}, u32[]{:S(2)}) collective-permute-start(bf16[512,128]{1,0:T(8,128)(2,1)} %get-tuple-element.238), channel_id=1, source_target_pairs={{0,2},{1,3},{2,0},{3,1},{4,6},{5,7},{6,4},{7,5},{8,10},{9,11},{10,... | collective-permute-start | bytes 393224 | tf_op jit(solution)/shard_map/ppermute | solution.py:522
  453.3 25.8 %collective-permute-start.25 = (bf16[512,128]{1,0:T(8,128)(2,1)}, bf16[512,128]{1,0:T(8,128)(2,1)}, u32[]{:S(2)}, u32[]{:S(2)}) collective-permute-start(bf16[512,128]{1,0:T(8,128)(2,1)} %get-tuple-element.237), channel_id=1, source_target_pairs={{0,1},{1,2},{2,3},{3,0},{4,5},{5,6},{6,7},{7,4},{8,9},{9,10},{10,1... | collective-permute-start | bytes 393224 | tf_op jit(solution)/shard_map/ppermute | solution.py:522
  453.5 21.5 %collective-permute-start.64 = (f32[64,128]{1,0:T(8,128)S(1)}, f32[64,128]{1,0:T(8,128)S(1)}, u32[]{:S(2)}, u32[]{:S(2)}) collective-permute-start(f32[64,128]{1,0:T(8,128)S(1)} %add.378), channel_id=1, source_target_pairs={{0,1},{1,0},{2,3},{3,2},{4,5},{5,4},{6,7},{7,6},{8,9},{9,8},{10,11... | collective-permute-start | bytes 98312 | tf_op jit(solution)/shard_map/ppermute | solution.py:527
  475.0 42.2 %collective-permute-start.41 = (bf16[3,2,160,1024]{3,2,1,0:T(8,128)(2,1)}, bf16[3,2,160,1024]{3,2,1,0:T(8,128)(2,1)}, u32[]{:S(2)}, u32[]{:S(2)}) collective-permute-start(bf16[3,2,160,1024]{3,2,1,0:T(8,128)(2,1)} %copy.139), channel_id=1, source_target_pairs={{0,4},{4,0},{8,12},{12,8},{16,20},{20,16},{24,28},{28,24},{1,5},{5... | collective-permute-start | bytes 5898248 | tf_op jit(solution)/shard_map/ppermute | solution.py:527
  475.1 23.2 %collective-permute-start.30 = (bf16[1024,256]{1,0:T(8,128)(2,1)}, bf16[1024,256]{1,0:T(8,128)(2,1)}, u32[]{:S(2)}, u32[]{:S(2)}) collective-permute-start(bf16[1024,256]{1,0:T(8,128)(2,1)} %get-tuple-element.153), channel_id=1, source_target_pairs={{4,0},{8,4},{12,8},{16,12},{20,16},{24,20},{28,24},{5,1},{9,5},{13... | collective-permute-start | bytes 1572872 | tf_op jit(solution)/shard_map/ppermute | solution.py:533
  478.4 13.7 %collective-permute-start.65 = (f32[64,128]{1,0:T(8,128)S(1)}, f32[64,128]{1,0:T(8,128)S(1)}, u32[]{:S(2)}, u32[]{:S(2)}) collective-permute-start(f32[64,128]{1,0:T(8,128)S(1)} %add.379), channel_id=1, source_target_pairs={{0,2},{1,3},{2,0},{3,1},{4,6},{5,7},{6,4},{7,5},{8,10},{9,11},{10,... | collective-permute-start | bytes 98312 | tf_op jit(solution)/shard_map/ppermute | solution.py:527
  490.7 53.6 %collective-permute-start.26 = (bf16[1024,256]{1,0:T(8,128)(2,1)}, bf16[1024,256]{1,0:T(8,128)(2,1)}, u32[]{:S(2)}, u32[]{:S(2)}) collective-permute-start(bf16[1024,256]{1,0:T(8,128)(2,1)} %get-tuple-element.147), channel_id=1, source_target_pairs={{4,0},{8,4},{12,8},{16,12},{20,16},{24,20},{28,24},{5,1},{9,5},{13... | collective-permute-start | bytes 1572872 | tf_op jit(solution)/shard_map/ppermute | solution.py:533
  498.3 43.4 %collective-permute-start.33 = (bf16[2,2,128,256]{2,3,1,0:T(8,128)(2,1)}, bf16[2,2,128,256]{2,3,1,0:T(8,128)(2,1)}, u32[]{:S(2)}, u32[]{:S(2)}) collective-permute-start(bf16[2,2,128,256]{2,3,1,0:T(8,128)(2,1)} %get-tuple-element.162), channel_id=1, source_target_pairs={{0,16},{4,20},{8,24},{12,28},{16,0},{20,4},{24,8},{28,12},{1,17},{... | collective-permute-start | bytes 786440 | tf_op jit(solution)/shard_map/ppermute | solution.py:527
  501.7 41.9 %collective-permute-start.32 = (bf16[2,2,128,256]{2,3,1,0:T(8,128)(2,1)}, bf16[2,2,128,256]{2,3,1,0:T(8,128)(2,1)S(1)}, u32[]{:S(2)}, u32[]{:S(2)}) collective-permute-start(bf16[2,2,128,256]{2,3,1,0:T(8,128)(2,1)} %add_convert_fusion.5), channel_id=1, source_target_pairs={{0,8},{4,12},{8,0},{12,4},{16,24},{20,28},{24,16},{28,20},{1,9},{5... | collective-permute-start | bytes 786440 | tf_op jit(solution)/shard_map/ppermute | solution.py:527
  544.3 18.4 %collective-permute-start.43 = (bf16[2,1,128,256]{2,3,1,0:T(8,128)(2,1)}, bf16[2,1,128,256]{2,3,1,0:T(8,128)(2,1)S(1)}, u32[]{:S(2)}, u32[]{:S(2)}) collective-permute-start(bf16[2,1,128,256]{2,3,1,0:T(8,128)(2,1)} %get-tuple-element.174), channel_id=1, source_target_pairs={{0,8},{4,12},{8,0},{12,4},{16,24},{20,28},{24,16},{28,20},{1,9},{5... | collective-permute-start | bytes 393224 | tf_op jit(solution)/shard_map/ppermute | solution.py:527
  544.3 18.4 %collective-permute-start.42 = (bf16[2,1,128,256]{2,3,1,0:T(8,128)(2,1)}, bf16[2,1,128,256]{2,3,1,0:T(8,128)(2,1)S(1)}, u32[]{:S(2)}, u32[]{:S(2)}) collective-permute-start(bf16[2,1,128,256]{2,3,1,0:T(8,128)(2,1)} %get-tuple-element.172), channel_id=1, source_target_pairs={{0,16},{4,20},{8,24},{12,28},{16,0},{20,4},{24,8},{28,12},{1,17},{... | collective-permute-start | bytes 393224 | tf_op jit(solution)/shard_map/ppermute | solution.py:527
  548.8 71.1 %collective-permute-start.47 = (bf16[2,2,128,384]{3,2,0,1:T(8,128)(2,1)}, bf16[2,2,128,384]{3,2,0,1:T(8,128)(2,1)}, u32[]{:S(2)}, u32[]{:S(2)}) collective-permute-start(bf16[2,2,128,384]{3,2,0,1:T(8,128)(2,1)} %bitcast.210), channel_id=1, source_target_pairs={{0,4},{4,0},{8,12},{12,8},{16,20},{20,16},{24,28},{28,24},{1,5},{5... | collective-permute-start | bytes 1179656 | tf_op jit(solution)/shard_map/ppermute | solution.py:527
  572.9 7.3 %collective-permute-start.54 = (f32[28,128]{1,0:T(8,128)S(1)}, f32[28,128]{1,0:T(8,128)S(1)}, u32[]{:S(2)}, u32[]{:S(2)}) collective-permute-start(f32[28,128]{1,0:T(8,128)S(1)} %fusion.55), channel_id=1, source_target_pairs={{0,8},{4,12},{8,0},{12,4},{16,24},{20,28},{24,16},{28,20},{1,9},{5... | collective-permute-start | bytes 43016 | tf_op jit(solution)/shard_map/ppermute | solution.py:527
  572.9 18.4 %collective-permute-start.59 = (bf16[128,256]{0,1:T(8,128)(2,1)S(1)}, bf16[128,256]{0,1:T(8,128)(2,1)S(1)}, u32[]{:S(2)}, u32[]{:S(2)}) collective-permute-start(bf16[128,256]{0,1:T(8,128)(2,1)S(1)} %get-tuple-element.270), channel_id=1, source_target_pairs={{0,2},{1,3},{2,0},{3,1},{4,6},{5,7},{6,4},{7,5},{8,10},{9,11},{10,... | collective-permute-start | bytes 196616 | tf_op jit(solution)/shard_map/ppermute | solution.py:522
  580.2 12.8 %collective-permute-start.60 = (bf16[128,256]{0,1:T(8,128)(2,1)S(1)}, bf16[128,256]{0,1:T(8,128)(2,1)S(1)}, u32[]{:S(2)}, u32[]{:S(2)}) collective-permute-start(bf16[128,256]{0,1:T(8,128)(2,1)S(1)} %get-tuple-element.271), channel_id=1, source_target_pairs={{0,1},{1,2},{2,3},{3,0},{4,5},{5,6},{6,7},{7,4},{8,9},{9,10},{10,1... | collective-permute-start | bytes 196616 | tf_op jit(solution)/shard_map/ppermute | solution.py:522
  580.2 6.7 collective-permute-start.55
  583.1 9.9 %collective-permute-start.58 = (bf16[128,256]{0,1:T(8,128)(2,1)S(1)}, bf16[128,256]{0,1:T(8,128)(2,1)S(1)}, u32[]{:S(2)}, u32[]{:S(2)}) collective-permute-start(bf16[128,256]{0,1:T(8,128)(2,1)S(1)} %slice_bitcast_fusion.4), channel_id=1, source_target_pairs={{0,3},{1,0},{2,1},{3,2},{4,7},{5,4},{6,5},{7,6},{8,11},{9,8},{10,9... | collective-permute-start | bytes 196616 | tf_op jit(solution)/shard_map/ppermute | solution.py:522
  590.7 52.5 %collective-permute-start.34 = (bf16[512,384]{1,0:T(8,128)(2,1)S(1)}, bf16[512,384]{1,0:T(8,128)(2,1)S(1)}, u32[]{:S(2)}, u32[]{:S(2)}) collective-permute-start(bf16[512,384]{1,0:T(8,128)(2,1)S(1)} %copy-done.31), channel_id=1, source_target_pairs={{0,1},{1,2},{2,3},{3,0},{4,5},{5,6},{6,7},{7,4},{8,9},{9,10},{10,1... | collective-permute-start | bytes 1179656 | tf_op jit(solution)/shard_map/ppermute | solution.py:522
  591.3 51.9 %collective-permute-start.35 = (bf16[512,384]{1,0:T(8,128)(2,1)S(1)}, bf16[512,384]{1,0:T(8,128)(2,1)S(1)}, u32[]{:S(2)}, u32[]{:S(2)}) collective-permute-start(bf16[512,384]{1,0:T(8,128)(2,1)S(1)} %copy-done.30), channel_id=1, source_target_pairs={{0,2},{1,3},{2,0},{3,1},{4,6},{5,7},{6,4},{7,5},{8,10},{9,11},{10,... | collective-permute-start | bytes 1179656 | tf_op jit(solution)/shard_map/ppermute | solution.py:522
  593.0 28.8 %collective-permute-start.50 = (bf16[2,2,128,256]{3,2,0,1:T(8,128)(2,1)S(1)}, bf16[2,2,128,256]{3,2,0,1:T(8,128)(2,1)S(1)}, u32[]{:S(2)}, u32[]{:S(2)}) collective-permute-start(bf16[2,2,128,256]{3,2,0,1:T(8,128)(2,1)S(1)} %bitcast.257), channel_id=1, source_target_pairs={{0,4},{4,0},{8,12},{12,8},{16,20},{20,16},{24,28},{28,24},{1,5},{5... | collective-permute-start | bytes 786440 | tf_op jit(solution)/shard_map/ppermute | solution.py:527
  593.0 25.7 %collective-permute-start.57 = (f32[28,128]{1,0:T(8,128)S(1)}, f32[28,128]{1,0:T(8,128)S(1)}, u32[]{:S(2)}, u32[]{:S(2)}) collective-permute-start(f32[28,128]{1,0:T(8,128)S(1)} %add.363), channel_id=1, source_target_pairs={{0,2},{1,3},{2,0},{3,1},{4,6},{5,7},{6,4},{7,5},{8,10},{9,11},{10,... | collective-permute-start | bytes 43016 | tf_op jit(solution)/shard_map/ppermute | solution.py:527
  618.7 11.1 %collective-permute-start.44 = (bf16[512,256]{1,0:T(8,128)(2,1)S(1)}, bf16[512,256]{1,0:T(8,128)(2,1)S(1)}, u32[]{:S(2)}, u32[]{:S(2)}) collective-permute-start(bf16[512,256]{1,0:T(8,128)(2,1)S(1)} %get-tuple-element.220), channel_id=1, source_target_pairs={{0,1},{1,2},{2,3},{3,0},{4,5},{5,6},{6,7},{7,4},{8,9},{9,10},{10,1... | collective-permute-start | bytes 786440 | tf_op jit(solution)/shard_map/ppermute | solution.py:522
  619.9 20.1 %collective-permute-start.45 = (bf16[512,256]{1,0:T(8,128)(2,1)S(1)}, bf16[512,256]{1,0:T(8,128)(2,1)S(1)}, u32[]{:S(2)}, u32[]{:S(2)}) collective-permute-start(bf16[512,256]{1,0:T(8,128)(2,1)S(1)} %get-tuple-element.219), channel_id=1, source_target_pairs={{0,2},{1,3},{2,0},{3,1},{4,6},{5,7},{6,4},{7,5},{8,10},{9,11},{10,... | collective-permute-start | bytes 786440 | tf_op jit(solution)/shard_map/ppermute | solution.py:522
  621.8 18.7 %collective-permute-start.46 = (bf16[512,256]{1,0:T(8,128)(2,1)S(1)}, bf16[512,256]{1,0:T(8,128)(2,1)S(1)}, u32[]{:S(2)}, u32[]{:S(2)}) collective-permute-start(bf16[512,256]{1,0:T(8,128)(2,1)S(1)} %get-tuple-element.218), channel_id=1, source_target_pairs={{0,3},{1,0},{2,1},{3,2},{4,7},{5,4},{6,5},{7,6},{8,11},{9,8},{10,9... | collective-permute-start | bytes 786440 | tf_op jit(solution)/shard_map/ppermute | solution.py:522
  629.8 18.4 %collective-permute-start.36 = (bf16[512,384]{1,0:T(8,128)(2,1)S(1)}, bf16[512,384]{1,0:T(8,128)(2,1)S(1)}, u32[]{:S(2)}, u32[]{:S(2)}) collective-permute-start(bf16[512,384]{1,0:T(8,128)(2,1)S(1)} %copy-done.29), channel_id=1, source_target_pairs={{0,3},{1,0},{2,1},{3,2},{4,7},{5,4},{6,5},{7,6},{8,11},{9,8},{10,9... | collective-permute-start | bytes 1179656 | tf_op jit(solution)/shard_map/ppermute | solution.py:522
  639.9 12.6 %collective-permute-start.48 = (bf16[2,128,384]{2,1,0:T(8,128)(2,1)S(1)}, bf16[2,128,384]{2,1,0:T(8,128)(2,1)S(1)}, u32[]{:S(2)}, u32[]{:S(2)}) collective-permute-start(bf16[2,128,384]{2,1,0:T(8,128)(2,1)S(1)} %dynamic-slice_bitcast_fusion.2), channel_id=1, source_target_pairs={{0,8},{4,12},{8,0},{12,4},{16,24},{20,28},{24,16},{28,20},{1,9},{5... | collective-permute-start | bytes 589832 | tf_op jit(solution)/shard_map/ppermute | solution.py:527
  640.5 11.9 %collective-permute-start.51 = (bf16[2,128,256]{2,1,0:T(8,128)(2,1)S(1)}, bf16[2,128,256]{2,1,0:T(8,128)(2,1)S(1)}, u32[]{:S(2)}, u32[]{:S(2)}) collective-permute-start(bf16[2,128,256]{2,1,0:T(8,128)(2,1)S(1)} %dynamic-slice_bitcast_fusion.3), channel_id=1, source_target_pairs={{0,8},{4,12},{8,0},{12,4},{16,24},{20,28},{24,16},{28,20},{1,9},{5... | collective-permute-start | bytes 393224 | tf_op jit(solution)/shard_map/ppermute | solution.py:527
  652.4 5.0 collective-permute-start.52
  652.6 6.0 collective-permute-start.49
  (49 other events, 476.1 us)
Sparse Core Ops, SparseCore 0:
  40.6 157.6 all-gather.2
  352.6 209.5 reduce-scatter.1
